TPU v7x, 32 devices: a whole 2x2x4 slice. The times are simulated.
32 devices in a mesh: section: 2 (over x), dp: 8 (over z, core), tensor: 2 (over y).
Axes of the slice: x: 2, y: 2, z: 4, core: 2. Of those that a mesh axis runs over, the one named last changes fastest.
Arguments:
- x_in: bfloat16 [4, 2048, 768], P(None, ('dp', 'tensor')), may hold values from -6 to 6
- d_out: bfloat16 [4, 2048, 768], P(None, ('dp', 'tensor')), may hold values from -6 to 6
- lengths: int32 [4, 8, 4], P(None, 'dp'), may hold values from 1 to 192, 256 in all within a row
- routes: int32 [2, 4, 2048, 1], P('section', None, 'dp'), may hold values from 0 to 7; in each aligned block of 256 rows (0 to 255, 256 to 511, ..., all dimensions but the last counted through in order) at most 64 rows name the same one
- gain_attn: bfloat16 [2, 768], P('section'), may hold values from 0.5 to 1.5
- w_qkv: bfloat16 [2, 3, 768, 768], P('section', None, 'dp', 'tensor'), may hold values from -0.21875 to 0.21875
- w_attn_out: bfloat16 [2, 768, 768], P('section', 'tensor', 'dp'), may hold values from -0.875 to 0.875
- gain_ffn: bfloat16 [2, 768], P('section'), may hold values from 0.5 to 1.5
- w_router: bfloat16 [2, 768, 8], P('section'), may hold values from -0.15625 to 0.15625
- w_in: bfloat16 [2, 8, 768, 3072], P('section', 'dp', None, 'tensor'), may hold values from -0.21875 to 0.21875
- w_exp_out: bfloat16 [2, 8, 3072, 768], P('section', 'dp', 'tensor'), may hold values from -0.875 to 0.875
Outputs:
- section_out: bfloat16 [2, 4, 2048, 768], P('section', None, ('dp', 'tensor'))
- section_in_grad: bfloat16 [2, 4, 2048, 768], P('section', None, ('dp', 'tensor'))
- g_gain_attn: float32 [2, 768], P('section')
- g_w_qkv: float32 [2, 3, 768, 768], P('section', None, 'dp', 'tensor')
- g_w_attn_out: float32 [2, 768, 768], P('section', 'tensor', 'dp')
- g_gain_ffn: float32 [2, 768], P('section')
- g_w_router: float32 [2, 768, 8], P('section')
- g_w_in: float32 [2, 8, 768, 3072], P('section', 'dp', None, 'tensor')
- g_w_exp_out: float32 [2, 8, 3072, 768], P('section', 'dp', 'tensor')
Inputs may be any that keep to these rules, and one draw needn't show every extreme that they name: The 4 lengths of each group sum to 256, and the longest of each group is exactly 192. `routes`: within the 256 tokens of one group, one micro-batch and one layer, no expert is named by more than 64 tokens; in some of these blocks one expert is named by exactly 64.
All inputs are finite; a program needn't handle non-finite values.
Results may differ from a plain program's by a relative error of at most 0.025.
Values may be sent and summed in bfloat16 or wider, within the bound.
No kernel may reach another device: no remote copies, remote signals or barrier semaphores. Data moves between devices by JAX's collectives and lax.ppermute only.
A program may use at most 256 MiB of HBM per device.

v0:
```python
import math

import jax
import jax.numpy as jnp
from jax import lax
from jax.sharding import PartitionSpec as P

HD = 64


EPSILON = 1e-06
NEGATIVE = -1e30


def from_behind(block, axis, distance):
    devices = range(lax.axis_size(axis))
    route = [(i - distance, i) for i in devices if i - distance in devices]
    return lax.ppermute(block, axis, route)


def in_blocks(shard, dim, length):
    before, after = (shard.shape[:dim], shard.shape[dim + 1 :])
    return jnp.moveaxis(shard.reshape(*before, length, -1, *after), dim, 0)


def sent_and_summed(shard, axis, dim):
    parts = in_blocks(shard, dim, lax.axis_size(axis))
    arrived = lax.all_to_all(parts, axis, split_axis=0, concat_axis=0, tiled=True)
    return arrived.astype(jnp.float32).sum(axis=0)


def rows_gather(values):
    return lax.all_gather(values, "tensor", axis=0, tiled=True)


def rows_sum(values):
    return lax.psum_scatter(
        values.astype(jnp.bfloat16), "tensor", scatter_dimension=0, tiled=True
    ).astype(jnp.float32)


def to_experts(values):
    return lax.all_to_all(values, "dp", split_axis=0, concat_axis=0, tiled=True)


def from_experts(values):
    return lax.all_to_all(
        values.astype(jnp.bfloat16), "dp", split_axis=0, concat_axis=0, tiled=True
    ).astype(values.dtype)


def smooth_gate(values):
    return jax.nn.gelu(values, approximate=True)


def norm_forward(inputs, gain):
    scaling = lax.rsqrt(jnp.mean(inputs * inputs, axis=-1, keepdims=True) + EPSILON)
    return (inputs * scaling * gain, scaling)


def norm_backward(upstream, inputs, scaling, gain):
    weighted = upstream * gain
    gain_grad = jnp.sum(upstream * inputs * scaling, axis=0)
    inner = jnp.mean(weighted * inputs, axis=-1, keepdims=True)
    return (scaling * weighted - inputs * scaling * scaling * scaling * inner, gain_grad)


def sequence_mask(lengths_row, count):
    bounds = jnp.cumsum(lengths_row)
    places = jnp.arange(count, dtype=jnp.int32)
    segment = jnp.sum((places[:, None] >= bounds[None, :]).astype(jnp.int32), axis=1)
    return (segment[:, None] == segment[None, :]) & (places[:, None] >= places[None, :])


def split_heads(values):
    return values.reshape(values.shape[0], -1, HD)


def masked_scores(qkv, lengths_row):
    count = qkv.shape[1]
    scaled = jnp.einsum(
        "qhd,khd->hqk", split_heads(qkv[0]), split_heads(qkv[1]), preferred_element_type=jnp.float32
    ) * (1.0 / math.sqrt(HD))
    return jnp.where(sequence_mask(lengths_row, count)[None], scaled, NEGATIVE)


def slot_table(route_row, experts, capacity):
    onehot = (route_row[:, None] == jnp.arange(experts, dtype=jnp.int32)[None, :]).astype(jnp.int32)
    ranking = jnp.sum((jnp.cumsum(onehot, axis=0) - 1) * onehot, axis=1)
    slots = route_row * capacity + ranking
    placing = (slots[None, :] == jnp.arange(experts * capacity, dtype=jnp.int32)[:, None]).astype(
        jnp.bfloat16
    )
    return (slots, placing)


def own_routing(route_row, tensor_index, own_count, experts):
    own_route = lax.dynamic_slice_in_dim(route_row, tensor_index * own_count, own_count)
    return (own_route[:, None] == jnp.arange(experts, dtype=jnp.int32)[None, :]).astype(jnp.float32)


def forward_tick(inputs, params, lengths_row, route_row, tensor_index):
    gain_a, gain_f, qkv_w, out_w, router_w, in_w, expert_w = params
    own_count = inputs.shape[0]
    group_count = route_row.shape[0]
    experts = router_w.shape[1]
    capacity = 2 * group_count // experts
    normed, scale_attn = norm_forward(inputs, gain_a)
    normed_full = rows_gather(normed.astype(jnp.bfloat16))
    qkv = jnp.einsum("rd,cdk->crk", normed_full, qkv_w, preferred_element_type=jnp.float32).astype(
        jnp.bfloat16
    )
    scores = masked_scores(qkv, lengths_row)
    log_total = jax.nn.logsumexp(scores, axis=-1)
    probs_low = jnp.exp(scores - log_total[..., None]).astype(jnp.bfloat16)
    mixed = jnp.einsum(
        "hqk,khd->qhd", probs_low, split_heads(qkv[2]), preferred_element_type=jnp.float32
    )
    mixed = mixed.reshape(group_count, -1).astype(jnp.bfloat16)
    attended = rows_sum(jnp.dot(mixed, out_w, preferred_element_type=jnp.float32))
    hidden = inputs + attended
    normed_ffn, scale_ffn = norm_forward(hidden, gain_f)
    normed_own = normed_ffn.astype(jnp.bfloat16)
    own_hot = own_routing(route_row, tensor_index, own_count, experts)
    chances = jax.nn.softmax(
        jnp.dot(normed_own, router_w, preferred_element_type=jnp.float32), axis=-1
    )
    gating = jnp.sum(chances * own_hot, axis=1)
    slots, placing = slot_table(route_row, experts, capacity)
    normed_group = rows_gather(normed_own)
    outgoing = jnp.dot(placing, normed_group, preferred_element_type=jnp.float32).astype(
        jnp.bfloat16
    )
    received = to_experts(outgoing)
    before = jnp.dot(received, in_w, preferred_element_type=jnp.float32)
    active = smooth_gate(before).astype(jnp.bfloat16)
    returned = from_experts(jnp.dot(active, expert_w, preferred_element_type=jnp.float32))
    expert_own = rows_sum(jnp.take(returned, slots, axis=0))
    result = (hidden + gating[:, None] * expert_own).astype(jnp.bfloat16)
    state = (
        inputs,
        scale_attn,
        normed_full,
        qkv,
        log_total,
        mixed,
        hidden,
        scale_ffn,
        normed_own,
        received,
        before,
        chances,
        gating,
        expert_own,
    )
    return (state, result)


def backward_tick(upstream, state, params, lengths_row, route_row, tensor_index):
    (
        inputs,
        scale_attn,
        normed_full,
        qkv,
        log_total,
        mixed,
        hidden,
        scale_ffn,
        normed_own,
        received,
        before,
        chances,
        gating,
        expert_own,
    ) = state
    gain_a, gain_f, qkv_w, out_w, router_w, in_w, expert_w = params
    own_count = inputs.shape[0]
    group_count = route_row.shape[0]
    experts = router_w.shape[1]
    capacity = 2 * group_count // experts
    own_hot = own_routing(route_row, tensor_index, own_count, experts)
    gate_grad = jnp.sum(upstream * expert_own, axis=1)
    expert_grad = (gating[:, None] * upstream).astype(jnp.bfloat16)
    logit_grad = gating[:, None] * (own_hot - chances) * gate_grad[:, None]
    router_grad = jnp.dot(
        normed_own.astype(jnp.float32).T, logit_grad, precision=lax.Precision.HIGHEST
    )
    router_back = jnp.dot(
        logit_grad, router_w.astype(jnp.float32).T, precision=lax.Precision.HIGHEST
    )
    slots, placing = slot_table(route_row, experts, capacity)
    outgoing = jnp.dot(
        placing, rows_gather(expert_grad), preferred_element_type=jnp.float32
    ).astype(jnp.bfloat16)
    arriving = to_experts(outgoing)
    activated, gate_back = jax.vjp(smooth_gate, before)
    active = activated.astype(jnp.bfloat16)
    expert_w_grad = jnp.einsum("rf,rd->fd", active, arriving, preferred_element_type=jnp.float32)
    active_grad = jnp.einsum("rd,fd->rf", arriving, expert_w, preferred_element_type=jnp.float32)
    before_grad = gate_back(active_grad)[0].astype(jnp.bfloat16)
    in_w_grad = jnp.einsum("rd,rf->df", received, before_grad, preferred_element_type=jnp.float32)
    sent_back = from_experts(
        jnp.einsum("rf,df->rd", before_grad, in_w, preferred_element_type=jnp.float32)
    )
    normed_grad = rows_sum(jnp.take(sent_back, slots, axis=0)) + router_back
    hidden_part, gain_ffn_grad = norm_backward(normed_grad, hidden, scale_ffn, gain_f)
    hidden_grad = upstream + hidden_part
    attended_full = rows_gather(hidden_grad.astype(jnp.bfloat16))
    out_w_grad = jnp.einsum("rk,rd->kd", mixed, attended_full, preferred_element_type=jnp.float32)
    mixed_grad = jnp.einsum(
        "rd,kd->rk", attended_full, out_w, preferred_element_type=jnp.float32
    ).astype(jnp.bfloat16)
    scores = masked_scores(qkv, lengths_row)
    chance_full = jnp.exp(scores - log_total[..., None])
    mixed_heads = split_heads(mixed_grad)
    value_grad = jnp.einsum(
        "hqk,qhd->khd",
        chance_full.astype(jnp.bfloat16),
        mixed_heads,
        preferred_element_type=jnp.float32,
    )
    prob_grad = jnp.einsum(
        "qhd,khd->hqk", mixed_heads, split_heads(qkv[2]), preferred_element_type=jnp.float32
    )
    score_grad = (
        chance_full * (prob_grad - jnp.sum(chance_full * prob_grad, axis=-1, keepdims=True))
    ).astype(jnp.bfloat16)
    factor = 1.0 / math.sqrt(HD)
    query_grad = (
        jnp.einsum(
            "hqk,khd->qhd", score_grad, split_heads(qkv[1]), preferred_element_type=jnp.float32
        )
        * factor
    )
    key_grad = (
        jnp.einsum(
            "hqk,qhd->khd", score_grad, split_heads(qkv[0]), preferred_element_type=jnp.float32
        )
        * factor
    )
    qkv_grad = (
        jnp.stack([query_grad, key_grad, value_grad])
        .reshape(3, group_count, -1)
        .astype(jnp.bfloat16)
    )
    qkv_w_grad = jnp.einsum(
        "rd,crk->cdk", normed_full, qkv_grad, preferred_element_type=jnp.float32
    )
    normed_back = rows_sum(
        jnp.einsum("crk,cdk->rd", qkv_grad, qkv_w, preferred_element_type=jnp.float32)
    )
    input_part, gain_attn_grad = norm_backward(normed_back, inputs, scale_attn, gain_a)
    input_grad = (hidden_grad + input_part).astype(jnp.bfloat16)
    return (
        input_grad,
        (qkv_w_grad, out_w_grad),
        (gain_attn_grad, gain_ffn_grad, router_grad),
        (in_w_grad, expert_w_grad),
    )


def shards(
    x_in, d_out, lengths, routes, gain_attn, w_qkv, w_attn_out, gain_ffn, w_router, w_in, w_exp_out
):
    section_index = lax.axis_index("section")
    tensor_index = lax.axis_index("tensor")
    micro = x_in.shape[0]
    own_count = x_in.shape[1]
    width = x_in.shape[2]
    qkv_w, out_w = (
        lax.all_gather(w_qkv[0], "dp", axis=1, tiled=True),
        lax.all_gather(w_attn_out[0], "dp", axis=1, tiled=True),
    )
    params = (
        gain_attn[0].astype(jnp.float32),
        gain_ffn[0].astype(jnp.float32),
        qkv_w,
        out_w,
        w_router[0],
        w_in[0, 0],
        w_exp_out[0, 0],
    )
    route_all = routes[0, :, :, 0]
    length_all = lengths[:, 0]

    def batch_inputs(tick_source):
        batch_index = jnp.clip(tick_source - section_index, 0, micro - 1)
        lengths_row = lax.dynamic_index_in_dim(length_all, batch_index, 0, keepdims=False)
        route_row = lax.dynamic_index_in_dim(route_all, batch_index, 0, keepdims=False)
        return (lengths_row, route_row)

    states = []
    results = []
    incoming = jnp.zeros((own_count, width), jnp.bfloat16)
    for moment in range(micro + 1):
        fresh = x_in[min(moment, micro - 1)]
        inputs = jnp.where(section_index == 0, fresh, incoming).astype(jnp.float32)
        lengths_row, route_row = batch_inputs(moment)
        state, result = forward_tick(inputs, params, lengths_row, route_row, tensor_index)
        states.append(state)
        results.append(result)
        if moment < micro:
            incoming = from_behind(result, "section", 1)
    stacked = jax.tree.map(lambda *items: jnp.stack(items), *states)
    input_grads = []
    attn_sums = None
    small_sums = None
    expert_sums = None
    incoming_grad = jnp.zeros((own_count, width), jnp.bfloat16)
    for moment in range(micro + 1):
        fresh = d_out[min(moment, micro - 1)]
        upstream = jnp.where(section_index == 1, fresh, incoming_grad).astype(jnp.float32)
        usable = jnp.where(section_index == 1, moment < micro, moment >= 1)
        upstream = upstream * usable.astype(jnp.float32)
        source = jnp.clip(jnp.where(section_index == 1, moment + 1, moment - 1), 0, micro)
        state = jax.tree.map(
            lambda arr: lax.dynamic_index_in_dim(arr, source, 0, keepdims=False), stacked
        )
        lengths_row, route_row = batch_inputs(source)
        input_grad, attn_grads, small_grads, expert_grads = backward_tick(
            upstream, state, params, lengths_row, route_row, tensor_index
        )
        input_grads.append(input_grad)
        if moment == 0:
            attn_sums, small_sums, expert_sums = (attn_grads, small_grads, expert_grads)
        else:
            attn_sums = jax.tree.map(lambda total, extra: total + extra, attn_sums, attn_grads)
            small_sums = jax.tree.map(lambda total, extra: total + extra, small_sums, small_grads)
            expert_sums = jax.tree.map(
                lambda total, extra: total + extra, expert_sums, expert_grads
            )
        if moment < micro:
            incoming_grad = from_behind(input_grad, "section", -1)
    qkv_grad, out_grad = (
        sent_and_summed(attn_sums[0].astype(jnp.bfloat16), "dp", 1),
        sent_and_summed(attn_sums[1].astype(jnp.bfloat16), "dp", 1),
    )
    gain_a_grad, gain_f_grad, router_grad = lax.psum(small_sums, ("dp", "tensor"))
    section_out = lax.dynamic_slice_in_dim(jnp.stack(results), section_index, micro, 0)[None]
    section_in_grad = lax.dynamic_slice_in_dim(jnp.stack(input_grads), 1 - section_index, micro, 0)[
        None
    ]
    in_w_grad, expert_w_grad = expert_sums
    return (
        section_out,
        section_in_grad,
        gain_a_grad[None],
        qkv_grad[None],
        out_grad[None],
        gain_f_grad[None],
        router_grad[None],
        in_w_grad[None, None],
        expert_w_grad[None, None],
    )


def solution(mesh):
    in_specs = (
        P(None, ("dp", "tensor"), None),
        P(None, ("dp", "tensor"), None),
        P(None, "dp", None),
        P("section", None, "dp", None),
        P("section", None),
        P("section", None, "dp", "tensor"),
        P("section", "tensor", "dp"),
        P("section", None),
        P("section", None, None),
        P("section", "dp", None, "tensor"),
        P("section", "dp", "tensor", None),
    )
    out_specs = (
        P("section", None, ("dp", "tensor"), None),
        P("section", None, ("dp", "tensor"), None),
        P("section", None),
        P("section", None, "dp", "tensor"),
        P("section", "tensor", "dp"),
        P("section", None),
        P("section", None, None),
        P("section", "dp", None, "tensor"),
        P("section", "dp", "tensor", None),
    )
    return jax.shard_map(shards, mesh=mesh, in_specs=in_specs, out_specs=out_specs, check_vma=False)
```

profile of v0, /device:TPU:0, one launch (start us, length us, event | category | flops | bytes accessed | tf_op | source)
XLA Modules:
  0.0 1464.2 jit_solution(18086190445385715363)
XLA Ops:
  12.7 8.5 all_gather.66
  24.1 18.7 %all-gather.1 = bf16[1,384,768]{1,2,0:T(8,128)(2,1)S(1)} all-gather(bf16[1,384,96]{1,2,0:T(8,128)(2,1)} %param.19), channel_id=3, replica_groups=mesh['section'=2,'dp'=8,'tensor'=2] {'dp'}, dimensions={2}, use_global_device_ids=true | all-gather | bytes 663552 | tf_op jit(solution)/shard_map/all_gather | solution.py:272
  55.2 11.7 reduce-scatter.21.cloned.1.call-done
  69.9 7.3 all_gather.69
  77.6 25.4 %all_to_all.220 = bf16[8,64,768]{2,1,0:T(8,128)(2,1)S(1)} all-to-all(bf16[8,64,768]{2,1,0:T(8,128)(2,1)S(1)} %bitcast.1339), channel_id=1, replica_groups=mesh['section'=2,'dp'=8,'tensor'=2] {'dp'}, dimensions={0} | all-to-all | bytes 1572864 | tf_op jit(solution)/shard_map/all_to_all | solution.py:43
  113.3 20.8 %all-to-all-done.1 = bf16[8,64,768]{2,1,0:T(8,128)(2,1)} async-done(((bf16[8,64,768]{2,1,0:T(8,128)(2,1)}), bf16[8,64,768]{2,1,0:T(8,128)(2,1)}, u32[]{:S(2)}, u32[]{:S(2)}) %all-to-all-start.1) | async-done | bytes 786464 | tf_op jit(solution)/shard_map/all_to_all | solution.py:47
  141.2 9.4 reduce-scatter.23.cloned.1.call-done
  162.8 6.9 all_gather.70
  180.8 12.8 reduce-scatter.25.cloned.1.call-done
  196.4 7.3 all_gather.71
  204.1 25.4 %all_to_all.221 = bf16[8,64,768]{2,1,0:T(8,128)(2,1)S(1)} all-to-all(bf16[8,64,768]{2,1,0:T(8,128)(2,1)S(1)} %bitcast.1340), channel_id=1, replica_groups=mesh['section'=2,'dp'=8,'tensor'=2] {'dp'}, dimensions={0} | all-to-all | bytes 1572864 | tf_op jit(solution)/shard_map/all_to_all | solution.py:43
  240.3 20.3 %all-to-all-done.3 = bf16[8,64,768]{2,1,0:T(8,128)(2,1)} async-done(((bf16[8,64,768]{2,1,0:T(8,128)(2,1)}), bf16[8,64,768]{2,1,0:T(8,128)(2,1)}, u32[]{:S(2)}, u32[]{:S(2)}) %all-to-all-start.3) | async-done | bytes 786464 | tf_op jit(solution)/shard_map/all_to_all | solution.py:47
  289.2 6.4 all_gather.72
  307.8 12.8 reduce-scatter.29.cloned.1.call-done
  323.5 7.3 all_gather.73
  331.2 25.6 %all_to_all.222 = bf16[8,64,768]{2,1,0:T(8,128)(2,1)S(1)} all-to-all(bf16[8,64,768]{2,1,0:T(8,128)(2,1)S(1)} %bitcast.1341), channel_id=1, replica_groups=mesh['section'=2,'dp'=8,'tensor'=2] {'dp'}, dimensions={0} | all-to-all | bytes 1572864 | tf_op jit(solution)/shard_map/all_to_all | solution.py:43
  367.6 20.3 %all-to-all-done.5 = bf16[8,64,768]{2,1,0:T(8,128)(2,1)} async-done(((bf16[8,64,768]{2,1,0:T(8,128)(2,1)}), bf16[8,64,768]{2,1,0:T(8,128)(2,1)}, u32[]{:S(2)}, u32[]{:S(2)}) %all-to-all-start.5) | async-done | bytes 786464 | tf_op jit(solution)/shard_map/all_to_all | solution.py:47
  396.3 8.2 reduce-scatter.31.cloned.1.call-done
  416.4 6.4 all_gather.74
  442.9 5.8 reduce-scatter.33.cloned.1.call-done
  452.1 7.3 all_gather.75
  460.4 25.3 %all_to_all.223 = bf16[8,64,768]{2,1,0:T(8,128)(2,1)S(1)} all-to-all(bf16[8,64,768]{2,1,0:T(8,128)(2,1)S(1)} %bitcast.1342), channel_id=1, replica_groups=mesh['section'=2,'dp'=8,'tensor'=2] {'dp'}, dimensions={0} | all-to-all | bytes 1572864 | tf_op jit(solution)/shard_map/all_to_all | solution.py:43
  545.9 6.4 all_gather.76
  570.4 7.9 reduce-scatter.37.cloned.1.call-done
  582.4 7.3 all_gather.77
  607.2 10.0 all-to-all-done.8
  637.6 12.1 all-to-all-done.9
  669.8 7.3 all_gather.78
  692.4 12.7 all-to-all-done.10
  705.2 5.7 fusion.6
  730.9 7.6 all-to-all-done.11
  748.6 6.5 reduce-scatter.41.cloned.1.call-done
  759.3 7.4 all_gather.79
  789.6 7.3 reduce-scatter.43.cloned.1.call-done
  803.1 6.1 collective-permute-done.4
  811.0 6.4 all_gather.80
  817.8 25.5 %all_to_all.224 = bf16[8,64,768]{2,1,0:T(8,128)(2,1)S(1)} all-to-all(bf16[8,64,768]{2,1,0:T(8,128)(2,1)S(1)} %bitcast.1343), channel_id=1, replica_groups=mesh['section'=2,'dp'=8,'tensor'=2] {'dp'}, dimensions={0} | all-to-all | bytes 1572864 | tf_op jit(solution)/shard_map/all_to_all | solution.py:43
  855.3 20.3 %all-to-all-done.13 = bf16[8,64,768]{2,1,0:T(8,128)(2,1)} async-done(((bf16[8,64,768]{2,1,0:T(8,128)(2,1)}), bf16[8,64,768]{2,1,0:T(8,128)(2,1)}, u32[]{:S(2)}, u32[]{:S(2)}) %all-to-all-start.13) | async-done | bytes 786464 | tf_op jit(solution)/shard_map/all_to_all | solution.py:47
  894.4 7.3 all_gather.81
  926.4 5.4 reduce-scatter.47.cloned.1.call-done
  938.1 6.0 collective-permute-done.5
  946.0 6.5 all_gather.82
  952.8 25.3 %all_to_all.225 = bf16[8,64,768]{2,1,0:T(8,128)(2,1)S(1)} all-to-all(bf16[8,64,768]{2,1,0:T(8,128)(2,1)S(1)} %bitcast.1344), channel_id=1, replica_groups=mesh['section'=2,'dp'=8,'tensor'=2] {'dp'}, dimensions={0} | all-to-all | bytes 1572864 | tf_op jit(solution)/shard_map/all_to_all | solution.py:43
  994.2 16.2 %all-to-all-done.15 = bf16[8,64,768]{2,1,0:T(8,128)(2,1)} async-done(((bf16[8,64,768]{2,1,0:T(8,128)(2,1)}), bf16[8,64,768]{2,1,0:T(8,128)(2,1)}, u32[]{:S(2)}, u32[]{:S(2)}) %all-to-all-start.15) | async-done | bytes 786464 | tf_op jit(solution)/shard_map/all_to_all | solution.py:47
  1029.2 7.3 all_gather.83
  1058.3 8.4 reduce-scatter.51.cloned.1.call-done
  1072.9 6.0 collective-permute-done.6
  1081.4 6.4 all_gather.84
  1104.3 10.6 all-to-all-done.16
  1114.9 5.7 fusion.27
  1158.2 6.1 fusion.202
  1171.2 7.4 all_gather.85
  1214.4 5.9 fusion.200
  1223.3 6.4 all_gather.86
  1248.7 5.8 fusion.198
  1256.7 5.7 fusion.34
  1269.2 5.3 fusion.345
  1282.2 6.0 fusion.196
  1295.4 5.3 fusion.343
  1312.5 7.2 all_gather.87
  1340.8 7.4 fusion.244
  1360.0 12.0 add_bitcast_fusion
  1373.7 11.3 add_bitcast_fusion.1
  1388.6 61.0 %all-reduce = (f32[1,768]{1,0:T(1,128)}, f32[1,768]{1,0:T(1,128)}, f32[1,768,8]{1,2,0:T(8,128)}) all-reduce(f32[1,768]{1,0:T(1,128)S(1)} %broadcast_in_dim.106, f32[1,768]{1,0:T(1,128)S(1)} %broadcast_in_dim.109, f32[1,768,8]{1,2,0:T(8,128)S(1)} %copy-done.105), channel_id=1, replica_groups=mesh['section'=2,'dp'=8,'tensor'=2] {'dp','tensor'}, use_global_device_ids=true, to_apply=%region_130.132 | all-reduce | flops 7680 | bytes 61440 | tf_op jit(solution)/shard_map/psum | solution.py:338
  (949 shorter events, 726.1 us)
Async XLA Ops:
  7.2 95.8 %copy-start = (bf16[1,1,768,1536]{3,2,1,0:T(8,128)(2,1)S(1)}, bf16[1,1,768,1536]{3,2,1,0:T(8,128)(2,1)}, u32[]{:S(2)}) copy-start(bf16[1,1,768,1536]{3,2,1,0:T(8,128)(2,1)} %param.22) | copy-start | bytes 7077892
  7.2 36.4 %all-gather.4.cloned.1.call-start = ((), (), s32[]{:S(2)}) async-start(), calls=%async_computation.62 | async-start | bytes 1990656 | tf_op jit(solution)/shard_map/all_gather | solution.py:271
  7.9 59.0 %reduce-scatter.21.cloned.1.call-start = ((), (), s32[]{:S(2)}) async-start(), calls=%async_computation.42 | async-start | bytes 589824 | tf_op jit(solution)/shard_map/reduce_scatter | solution.py:37
  21.2 26.2 %copy-start.66 = (bf16[256,768]{1,0:T(8,128)(2,1)}, bf16[256,768]{1,0:T(8,128)(2,1)S(1)}, u32[]{:S(2)}) copy-start(bf16[256,768]{1,0:T(8,128)(2,1)S(1)} %all_gather.66) | copy-start | bytes 1179652
  55.1 51.0 %copy-start.73 = (f32[768]{0:T(1024)}, f32[768]{0:T(1024)S(1)}, u32[]{:S(2)}) copy-start(f32[768]{0:T(1024)S(1)} %convert_reduce_fusion.12) | copy-start | bytes 9220
  68.1 38.0 %copy-start.180 = (f32[128]{0:T(128)}, f32[128]{0:T(128)S(1)}, u32[]{:S(2)}) copy-start(f32[128]{0:T(128)S(1)} %multiply_reduce_fusion.9) | copy-start | bytes 1540
  108.9 25.2 %all-to-all-start.1 = ((bf16[8,64,768]{2,1,0:T(8,128)(2,1)}), bf16[8,64,768]{2,1,0:T(8,128)(2,1)}, u32[]{:S(2)}, u32[]{:S(2)}) async-start(bf16[8,64,768]{2,1,0:T(8,128)(2,1)} %bitcast.1405), calls=%async_computation.2 | async-start | bytes 1572864 | tf_op jit(solution)/shard_map/all_to_all | solution.py:47
  113.2 37.5 %reduce-scatter.23.cloned.1.call-start = ((), (), s32[]{:S(2)}) async-start(), calls=%async_computation.43 | async-start | bytes 589824 | tf_op jit(solution)/shard_map/reduce_scatter | solution.py:37
  139.5 54.1 %reduce-scatter.25.cloned.1.call-start = ((), (), s32[]{:S(2)}) async-start(), calls=%async_computation.44 | async-start | bytes 589824 | tf_op jit(solution)/shard_map/reduce_scatter | solution.py:37
  150.7 19.0 %copy-start.1 = (bf16[1,3,768,384]{3,2,1,0:T(8,128)(2,1)S(1)}, bf16[1,3,768,384]{3,2,1,0:T(8,128)(2,1)}, u32[]{:S(2)}) copy-start(bf16[1,3,768,384]{3,2,1,0:T(8,128)(2,1)} %all-gather.4.cloned.1.call-done) | copy-start | bytes 5308420
  152.6 7.5 collective-permute-start
  177.0 19.4 %copy-start.110 = (f32[6,256]{1,0:T(8,128)}, f32[6,256]{1,0:T(8,128)S(1)}, u32[]{:S(2)}) copy-start(f32[6,256]{1,0:T(8,128)S(1)} %exponential_reduce_fusion.3) | copy-start | bytes 18436
  194.7 37.9 %copy-start.182 = (f32[128]{0:T(128)}, f32[128]{0:T(128)S(1)}, u32[]{:S(2)}) copy-start(f32[128]{0:T(128)S(1)} %multiply_reduce_fusion.8) | copy-start | bytes 1540
  235.4 25.2 %all-to-all-start.3 = ((bf16[8,64,768]{2,1,0:T(8,128)(2,1)}), bf16[8,64,768]{2,1,0:T(8,128)(2,1)}, u32[]{:S(2)}, u32[]{:S(2)}) async-start(bf16[8,64,768]{2,1,0:T(8,128)(2,1)} %bitcast.1410), calls=%async_computation.6 | async-start | bytes 1572864 | tf_op jit(solution)/shard_map/all_to_all | solution.py:47
  239.7 37.6 %reduce-scatter.27.cloned.1.call-start = ((), (), s32[]{:S(2)}) async-start(), calls=%async_computation.45 | async-start | bytes 589824 | tf_op jit(solution)/shard_map/reduce_scatter | solution.py:37
  266.1 54.5 %reduce-scatter.29.cloned.1.call-start = ((), (), s32[]{:S(2)}) async-start(), calls=%async_computation.46 | async-start | bytes 589824 | tf_op jit(solution)/shard_map/reduce_scatter | solution.py:37
  277.3 18.4 %copy-start.2 = (bf16[1,3,768,384]{3,2,1,0:T(8,128)(2,1)S(1)}, bf16[1,3,768,384]{3,2,1,0:T(8,128)(2,1)}, u32[]{:S(2)}) copy-start(bf16[1,3,768,384]{3,2,1,0:T(8,128)(2,1)} %all-gather.4.cloned.1.call-done) | copy-start | bytes 5308420
  279.1 7.5 collective-permute-start.1
  304.1 19.4 %copy-start.111 = (f32[6,256]{1,0:T(8,128)}, f32[6,256]{1,0:T(8,128)S(1)}, u32[]{:S(2)}) copy-start(f32[6,256]{1,0:T(8,128)S(1)} %exponential_reduce_fusion.2) | copy-start | bytes 18436
  321.7 38.1 %copy-start.184 = (f32[128]{0:T(128)}, f32[128]{0:T(128)S(1)}, u32[]{:S(2)}) copy-start(f32[128]{0:T(128)S(1)} %multiply_reduce_fusion.7) | copy-start | bytes 1540
  362.7 25.2 %all-to-all-start.5 = ((bf16[8,64,768]{2,1,0:T(8,128)(2,1)}), bf16[8,64,768]{2,1,0:T(8,128)(2,1)}, u32[]{:S(2)}, u32[]{:S(2)}) async-start(bf16[8,64,768]{2,1,0:T(8,128)(2,1)} %bitcast.1411), calls=%async_computation.10 | async-start | bytes 1572864 | tf_op jit(solution)/shard_map/all_to_all | solution.py:47
  366.9 37.6 %reduce-scatter.31.cloned.1.call-start = ((), (), s32[]{:S(2)}) async-start(), calls=%async_computation.47 | async-start | bytes 589824 | tf_op jit(solution)/shard_map/reduce_scatter | solution.py:37
  393.3 55.4 %reduce-scatter.33.cloned.1.call-start = ((), (), s32[]{:S(2)}) async-start(), calls=%async_computation.48 | async-start | bytes 589824 | tf_op jit(solution)/shard_map/reduce_scatter | solution.py:37
  406.4 7.5 collective-permute-start.2
  415.6 118.3 %copy-start.6 = (bf16[128,768]{1,0:T(8,128)(2,1)}, bf16[128,768]{1,0:T(8,128)(2,1)S(1)}, u32[]{:S(2)}) copy-start(bf16[128,768]{1,0:T(8,128)(2,1)S(1)} %get-tuple-element.78) | copy-start | bytes 589828
  491.6 25.2 %all-to-all-start.7 = ((bf16[8,64,768]{2,1,0:T(8,128)(2,1)}), bf16[8,64,768]{2,1,0:T(8,128)(2,1)}, u32[]{:S(2)}, u32[]{:S(2)}) async-start(bf16[8,64,768]{2,1,0:T(8,128)(2,1)} %bitcast.1407), calls=%async_computation.14 | async-start | bytes 1572864 | tf_op jit(solution)/shard_map/all_to_all | solution.py:47
  495.8 38.1 %reduce-scatter.35.cloned.1.call-start = ((), (), s32[]{:S(2)}) async-start(), calls=%async_computation.49 | async-start | bytes 589824 | tf_op jit(solution)/shard_map/reduce_scatter | solution.py:37
  522.2 56.1 %reduce-scatter.37.cloned.1.call-start = ((), (), s32[]{:S(2)}) async-start(), calls=%async_computation.50 | async-start | bytes 589824 | tf_op jit(solution)/shard_map/reduce_scatter | solution.py:37
  533.9 18.5 %copy-start.4 = (bf16[1,3,768,384]{3,2,1,0:T(8,128)(2,1)S(1)}, bf16[1,3,768,384]{3,2,1,0:T(8,128)(2,1)}, u32[]{:S(2)}) copy-start(bf16[1,3,768,384]{3,2,1,0:T(8,128)(2,1)} %all-gather.4.cloned.1.call-done) | copy-start | bytes 5308420
  535.9 7.5 collective-permute-start.3
  591.6 25.7 %all-to-all-start.8 = ((bf16[8,64,768]{2,1,0:T(8,128)(2,1)}), bf16[8,64,768]{2,1,0:T(8,128)(2,1)}, u32[]{:S(2)}, u32[]{:S(2)}) async-start(bf16[8,64,768]{2,1,0:T(8,128)(2,1)} %bitcast.1336), calls=%async_computation.17 | async-start | bytes 1572864 | tf_op jit(solution)/shard_map/all_to_all | solution.py:43
  624.5 25.2 %all-to-all-start.9 = ((bf16[8,64,768]{2,1,0:T(8,128)(2,1)}), bf16[8,64,768]{2,1,0:T(8,128)(2,1)}, u32[]{:S(2)}, u32[]{:S(2)}) async-start(bf16[8,64,768]{2,1,0:T(8,128)(2,1)} %bitcast.1408), calls=%async_computation.18 | async-start | bytes 1572864 | tf_op jit(solution)/shard_map/all_to_all | solution.py:47
  628.7 37.6 %reduce-scatter.39.cloned.1.call-start = ((), (), s32[]{:S(2)}) async-start(), calls=%async_computation.51 | async-start | bytes 589824 | tf_op jit(solution)/shard_map/reduce_scatter | solution.py:37
  679.1 26.1 %all-to-all-start.10 = ((bf16[8,64,768]{2,1,0:T(8,128)(2,1)}), bf16[8,64,768]{2,1,0:T(8,128)(2,1)}, u32[]{:S(2)}, u32[]{:S(2)}) async-start(bf16[8,64,768]{2,1,0:T(8,128)(2,1)} %bitcast.1337), calls=%async_computation.20 | async-start | bytes 1572864 | tf_op jit(solution)/shard_map/all_to_all | solution.py:43
  713.2 25.2 %all-to-all-start.11 = ((bf16[8,64,768]{2,1,0:T(8,128)(2,1)}), bf16[8,64,768]{2,1,0:T(8,128)(2,1)}, u32[]{:S(2)}, u32[]{:S(2)}) async-start(bf16[8,64,768]{2,1,0:T(8,128)(2,1)} %bitcast.1403), calls=%async_computation.21 | async-start | bytes 1572864 | tf_op jit(solution)/shard_map/all_to_all | solution.py:47
  717.5 37.6 %reduce-scatter.41.cloned.1.call-start = ((), (), s32[]{:S(2)}) async-start(), calls=%async_computation.52 | async-start | bytes 589824 | tf_op jit(solution)/shard_map/reduce_scatter | solution.py:37
  743.9 52.9 %reduce-scatter.43.cloned.1.call-start = ((), (), s32[]{:S(2)}) async-start(), calls=%async_computation.53 | async-start | bytes 589824 | tf_op jit(solution)/shard_map/reduce_scatter | solution.py:37
  780.2 18.4 %copy-start.68 = (f32[128,768]{1,0:T(8,128)S(1)}, f32[128,768]{1,0:T(8,128)}, u32[]{:S(2)}) copy-start(f32[128,768]{1,0:T(8,128)} %get-tuple-element.84) | copy-start | bytes 1179652
  800.6 8.5 collective-permute-start.4
  803.1 40.3 %copy-start.195 = (bf16[1,1,1536,768]{3,2,1,0:T(8,128)(2,1)S(1)}, bf16[1,1,1536,768]{3,2,1,0:T(8,128)(2,1)}, u32[]{:S(2)}) copy-start(bf16[1,1,1536,768]{3,2,1,0:T(8,128)(2,1)} %param.23) | copy-start | bytes 7077892
  850.4 25.2 %all-to-all-start.13 = ((bf16[8,64,768]{2,1,0:T(8,128)(2,1)}), bf16[8,64,768]{2,1,0:T(8,128)(2,1)}, u32[]{:S(2)}, u32[]{:S(2)}) async-start(bf16[8,64,768]{2,1,0:T(8,128)(2,1)} %bitcast.1412), calls=%async_computation.25 | async-start | bytes 1572864 | tf_op jit(solution)/shard_map/all_to_all | solution.py:47
  854.6 35.6 %reduce-scatter.45.cloned.1.call-start = ((), (), s32[]{:S(2)}) async-start(), calls=%async_computation.54 | async-start | bytes 589824 | tf_op jit(solution)/shard_map/reduce_scatter | solution.py:37
  879.9 51.9 %reduce-scatter.47.cloned.1.call-start = ((), (), s32[]{:S(2)}) async-start(), calls=%async_computation.55 | async-start | bytes 589824 | tf_op jit(solution)/shard_map/reduce_scatter | solution.py:37
  915.2 18.4 %copy-start.70 = (f32[128,768]{1,0:T(8,128)S(1)}, f32[128,768]{1,0:T(8,128)}, u32[]{:S(2)}) copy-start(f32[128,768]{1,0:T(8,128)} %get-tuple-element.68) | copy-start | bytes 1179652
  935.6 8.5 collective-permute-start.5
  938.1 40.0 %copy-start.196 = (bf16[1,1,1536,768]{3,2,1,0:T(8,128)(2,1)S(1)}, bf16[1,1,1536,768]{3,2,1,0:T(8,128)(2,1)}, u32[]{:S(2)}) copy-start(bf16[1,1,1536,768]{3,2,1,0:T(8,128)(2,1)} %param.23) | copy-start | bytes 7077892
  985.2 25.2 %all-to-all-start.15 = ((bf16[8,64,768]{2,1,0:T(8,128)(2,1)}), bf16[8,64,768]{2,1,0:T(8,128)(2,1)}, u32[]{:S(2)}, u32[]{:S(2)}) async-start(bf16[8,64,768]{2,1,0:T(8,128)(2,1)} %bitcast.1406), calls=%async_computation.29 | async-start | bytes 1572864 | tf_op jit(solution)/shard_map/all_to_all | solution.py:47
  989.4 35.6 %reduce-scatter.49.cloned.1.call-start = ((), (), s32[]{:S(2)}) async-start(), calls=%async_computation.56 | async-start | bytes 589824 | tf_op jit(solution)/shard_map/reduce_scatter | solution.py:37
  1014.8 51.9 %reduce-scatter.51.cloned.1.call-start = ((), (), s32[]{:S(2)}) async-start(), calls=%async_computation.57 | async-start | bytes 589824 | tf_op jit(solution)/shard_map/reduce_scatter | solution.py:37
  1050.0 18.4 %copy-start.69 = (f32[128,768]{1,0:T(8,128)S(1)}, f32[128,768]{1,0:T(8,128)}, u32[]{:S(2)}) copy-start(f32[128,768]{1,0:T(8,128)} %get-tuple-element.60) | copy-start | bytes 1179652
  1066.6 21.2 %copy-start.138 = (s32[256]{0:T(256)S(1)}, s32[256]{0:T(256)}, u32[]{:S(2)}) copy-start(s32[256]{0:T(256)} %copy-done.137) | copy-start | bytes 3076
  1070.4 8.5 collective-permute-start.6
  1089.1 25.8 %all-to-all-start.16 = ((bf16[8,64,768]{2,1,0:T(8,128)(2,1)}), bf16[8,64,768]{2,1,0:T(8,128)(2,1)}, u32[]{:S(2)}, u32[]{:S(2)}) async-start(bf16[8,64,768]{2,1,0:T(8,128)(2,1)} %bitcast.1335), calls=%async_computation.32 | async-start | bytes 1572864 | tf_op jit(solution)/shard_map/all_to_all | solution.py:43
  1123.0 27.6 %all-to-all-start.17 = ((bf16[8,64,768]{2,1,0:T(8,128)(2,1)}), bf16[8,64,768]{2,1,0:T(8,128)(2,1)}, u32[]{:S(2)}, u32[]{:S(2)}) async-start(bf16[8,64,768]{2,1,0:T(8,128)(2,1)} %bitcast.1404), calls=%async_computation.33 | async-start | bytes 1572864 | tf_op jit(solution)/shard_map/all_to_all | solution.py:47
  1127.3 39.7 %reduce-scatter.53.cloned.1.call-start = ((), (), s32[]{:S(2)}) async-start(), calls=%async_computation.58 | async-start | bytes 589824 | tf_op jit(solution)/shard_map/reduce_scatter | solution.py:37
  1154.3 54.7 %reduce-scatter.55.cloned.1.call-start = ((), (), s32[]{:S(2)}) async-start(), calls=%async_computation.59 | async-start | bytes 589824 | tf_op jit(solution)/shard_map/reduce_scatter | solution.py:37
  1212.8 8.6 collective-permute-start.7
  1231.0 25.7 %all-to-all-start.18 = ((bf16[8,64,768]{2,1,0:T(8,128)(2,1)}), bf16[8,64,768]{2,1,0:T(8,128)(2,1)}, u32[]{:S(2)}, u32[]{:S(2)}) async-start(bf16[8,64,768]{2,1,0:T(8,128)(2,1)} %bitcast.1338), calls=%async_computation.36 | async-start | bytes 1572864 | tf_op jit(solution)/shard_map/all_to_all | solution.py:43
  1264.7 25.2 %all-to-all-start.19 = ((bf16[8,64,768]{2,1,0:T(8,128)(2,1)}), bf16[8,64,768]{2,1,0:T(8,128)(2,1)}, u32[]{:S(2)}, u32[]{:S(2)}) async-start(bf16[8,64,768]{2,1,0:T(8,128)(2,1)} %bitcast.1409), calls=%async_computation.37 | async-start | bytes 1572864 | tf_op jit(solution)/shard_map/all_to_all | solution.py:47
  1268.9 39.4 %reduce-scatter.57.cloned.1.call-start = ((), (), s32[]{:S(2)}) async-start(), calls=%async_computation.60 | async-start | bytes 589824 | tf_op jit(solution)/shard_map/reduce_scatter | solution.py:37
  1329.6 25.2 %all-to-all-start.21 = ((bf16[8,384,96]{1,2,0:T(8,128)(2,1)}), bf16[8,384,96]{1,2,0:T(8,128)(2,1)S(1)}, u32[]{:S(2)}, u32[]{:S(2)}) async-start(bf16[8,384,96]{1,2,0:T(8,128)(2,1)} %bitcast.354), calls=%async_computation.41 | async-start | bytes 1179648 | tf_op jit(solution)/shard_map/all_to_all | solution.py:28
  1354.9 99.5 %all-to-all-start.20 = ((bf16[8,3,96,384]{3,2,1,0:T(8,128)(2,1)}), bf16[8,3,96,384]{3,2,1,0:T(8,128)(2,1)}, u32[]{:S(2)}, u32[]{:S(2)}) async-start(bf16[8,3,96,384]{3,2,1,0:T(8,128)(2,1)} %copy.341), calls=%async_computation.40 | async-start | bytes 3538944 | tf_op jit(solution)/shard_map/all_to_all | solution.py:28
  1360.0 27.3 %reduce-scatter.59.cloned.1.call-start = ((), (), s32[]{:S(2)}) async-start(), calls=%async_computation.61 | async-start | bytes 589824 | tf_op jit(solution)/shard_map/reduce_scatter | solution.py:37
  1373.7 76.0 %copy-start.67 = (f32[128,768]{1,0:T(8,128)S(1)}, f32[128,768]{1,0:T(8,128)}, u32[]{:S(2)}) copy-start(f32[128,768]{1,0:T(8,128)} %get-tuple-element.44) | copy-start | bytes 1179652
  (178 other events, 1007.6 us)
Sparse Core Ops, SparseCore 0:
  9.6 33.8 all-gather.3
  54.3 12.5 reduce-scatter.20
  139.6 11.0 reduce-scatter.22
  179.4 14.1 reduce-scatter.24
  266.2 11.0 reduce-scatter.26
  306.5 14.1 reduce-scatter.28
  393.5 11.0 reduce-scatter.30
  434.5 14.1 reduce-scatter.32
  522.4 11.5 reduce-scatter.34
  564.1 14.1 reduce-scatter.36
  655.2 11.0 reduce-scatter.38
  744.0 10.9 reduce-scatter.40
  783.7 13.1 reduce-scatter.42
  880.0 10.1 reduce-scatter.44
  918.7 13.1 reduce-scatter.46
  1014.9 10.1 reduce-scatter.48
  1053.5 13.1 reduce-scatter.50
  1154.4 12.5 reduce-scatter.52
  1195.8 13.1 reduce-scatter.54
  1295.5 12.2 reduce-scatter.56
  1373.7 13.6 reduce-scatter.58
where the time goes:
time: 1480 us; the launch traced here: 1460 us
  blocking collectives  373 us (25%)
  waiting for transfers between devices  309 us (21%)
  matrix products  276 us (19%)
  other arithmetic  218 us (15%)
  local copies, waits for them, and re-layouts  180 us (12%)
  starting transfers between devices  91.8 us (6%)
  between operations  17.2 us (1%)
    all_to_all x6, blocking collectives, to_experts(): return lax.all_to_all(values, 'dp', split_axis=0, concat_axis=0, tiled=True)  153 us
    all_gather x20, blocking collectives, rows_gather(): return lax.all_gather(values, 'tensor', axis=0, tiled=True)  141 us
    all_to_all x10, waiting for transfers between devices, from_experts(): lax.all_to_all(values.astype(jnp.bfloat16), 'dp', split_axis=0, concat_ax...  121 us
    reduce_scatter x20, waiting for transfers between devices, rows_sum(): lax.psum_scatter(values.astype(jnp.bfloat16), 'tensor', scatter_dimension...  121 us
    psum x1, blocking collectives, shards(): lax.psum(small_sums, ('dp', 'tensor'))  61 us
    unnamed x39, other arithmetic  60.1 us
    all_to_all x10, starting transfers between devices, from_experts(): lax.all_to_all(values.astype(jnp.bfloat16), 'dp', split_axis=0, concat_ax...  42.3 us
    dot_general x5, matrix products, backward_tick(): jnp.einsum('rf,rd->fd', active, arriving, preferred_element_type=jnp.floa...  35.7 us
  transfers between devices with their start and end apart: 45, of which 41 were waited for; matrix products, arithmetic and copies ran while one was open for 22% of the time, Pallas kernels for 0%

commit v1 on v0

v1 whole, which is shorter than its diff:
```python
import math

import jax
import jax.numpy as jnp
from jax import lax
from jax.sharding import PartitionSpec as P

HD = 64
EPSILON = 1e-06
NEGATIVE = -1e30
F32 = jnp.float32
BF16 = jnp.bfloat16


def swap(values, axis):
    return lax.ppermute(values, axis, [(0, 1), (1, 0)])


def one_way(values, axis, source, target):
    return lax.ppermute(values, axis, [(source, target)])


def all_to_all(values):
    return lax.all_to_all(values, "dp", split_axis=0, concat_axis=0, tiled=True)


def dot(left, right, left_dim, right_dim):
    return lax.dot_general(
        left, right, (((left_dim,), (right_dim,)), ((), ())), preferred_element_type=F32
    )


def ordered(index, own, other):
    return jnp.where(
        index == 0, jnp.concatenate([own, other], axis=0), jnp.concatenate([other, own], axis=0)
    )


def entry(array, index):
    return lax.dynamic_index_in_dim(array, index, 0, keepdims=False)


def norm_forward(inputs, gain):
    scaling = lax.rsqrt(jnp.mean(inputs * inputs, axis=-1, keepdims=True) + EPSILON)
    return (inputs * scaling * gain, scaling)


def norm_backward(upstream, inputs, scaling, gain):
    weighted = upstream * gain
    gain_grad = jnp.sum(upstream * inputs * scaling, axis=0)
    inner = jnp.mean(weighted * inputs, axis=-1, keepdims=True)
    return (scaling * weighted - inputs * scaling * scaling * scaling * inner, gain_grad)


def sequence_mask(lengths_row, count):
    bounds = jnp.cumsum(lengths_row)
    places = jnp.arange(count, dtype=jnp.int32)
    segment = jnp.sum((places[:, None] >= bounds[None, :]).astype(jnp.int32), axis=1)
    return (segment[:, None] == segment[None, :]) & (places[:, None] >= places[None, :])


def smooth_gate(values):
    return jax.nn.gelu(values, approximate=True)


def routing(route_row, experts):
    count = route_row.shape[0]
    capacity = 2 * count // experts
    hot = route_row[:, None] == jnp.arange(experts, dtype=jnp.int32)[None, :]
    places = jnp.arange(count, dtype=jnp.int32)
    earlier = (places[:, None] > places[None, :]).astype(BF16)
    ranks = dot(earlier, hot.astype(BF16), 1, 0)
    ranking = jnp.sum(ranks * hot.astype(F32), axis=1).astype(jnp.int32)
    slots = route_row * capacity + ranking
    placing = (
        slots[None, :] == jnp.arange(experts * capacity, dtype=jnp.int32)[:, None]
    ).astype(BF16)
    return (hot.astype(F32), placing)


def dispatch(placing, values):
    outgoing = dot(placing, values, 1, 0).astype(BF16)
    received = all_to_all(outgoing)
    return jnp.concatenate([received, swap(received, "tensor")], axis=0)


def collect(placing, partial):
    count = partial.shape[0] // 2
    total = partial[:count] + swap(partial[count:].astype(BF16), "tensor").astype(F32)
    return dot(placing, all_to_all(total.astype(BF16)), 0, 0)


def attention_parts(normed, weights, mask):
    count = normed.shape[0]
    qkvo = dot(normed, weights, 1, 0).astype(BF16).reshape(count, 2, 4, -1)
    query, key, value = (
        qkvo[:, :, part].reshape(count, -1, HD) for part in range(3)
    )
    scores = jnp.einsum("qhd,khd->hqk", query, key, preferred_element_type=F32)
    scores = jnp.where(mask[None], scores * (1.0 / math.sqrt(HD)), NEGATIVE)
    return (query, key, value, scores)


def layer_forward(inputs, params, mask, route_row):
    gain_a, gain_f, weights, router_w, in_w, expert_w = params
    count, width = inputs.shape
    normed, scale_attn = norm_forward(inputs, gain_a)
    normed = normed.astype(BF16)
    query, key, value, scores = attention_parts(normed, weights, mask)
    log_total = jax.nn.logsumexp(scores, axis=-1)
    probs = jnp.exp(scores - log_total[..., None])
    mixed = jnp.einsum("hqk,khd->qhd", probs.astype(BF16), value, preferred_element_type=F32)
    mixed = mixed.reshape(count, -1).astype(BF16)
    out_w = weights.reshape(width, 2, 4, -1)[:, :, 3].reshape(width, -1)
    hidden = inputs + dot(mixed, out_w, 1, 1)
    normed_ffn, scale_ffn = norm_forward(hidden, gain_f)
    normed_ffn = normed_ffn.astype(BF16)
    hot, placing = routing(route_row, router_w.shape[0])
    chances = jax.nn.softmax(dot(normed_ffn, router_w, 1, 1), axis=-1)
    gating = jnp.sum(chances * hot, axis=1)
    received = dispatch(placing, normed_ffn)
    before = dot(received, in_w, 1, 0)
    active = smooth_gate(before).astype(BF16)
    expert_out = collect(placing, dot(active, expert_w, 1, 0))
    result = (hidden + gating[:, None] * expert_out).astype(BF16)
    state = (
        inputs, scale_attn, normed, query, key, value, log_total, mixed, hidden, scale_ffn,
        normed_ffn, received, before, chances, gating, expert_out, hot, placing,
    )
    return (state, result)


def layer_backward(upstream, state, params, mask):
    (
        inputs, scale_attn, normed, query, key, value, log_total, mixed, hidden, scale_ffn,
        normed_ffn, received, before, chances, gating, expert_out, hot, placing,
    ) = state
    gain_a, gain_f, weights, router_w, in_w, expert_w = params
    count, width = inputs.shape
    gate_grad = jnp.sum(upstream * expert_out, axis=1)
    expert_grad = (gating[:, None] * upstream).astype(BF16)
    logit_grad = gating[:, None] * (hot - chances) * gate_grad[:, None]
    router_grad = jnp.dot(logit_grad.T, normed_ffn.astype(F32), precision=lax.Precision.HIGHEST)
    router_back = jnp.dot(logit_grad, router_w.astype(F32), precision=lax.Precision.HIGHEST)
    arriving = dispatch(placing, expert_grad)
    activated, gate_back = jax.vjp(smooth_gate, before)
    active_grad = dot(arriving, expert_w, 1, 1)
    before_grad = gate_back(active_grad)[0].astype(BF16)
    normed_grad = collect(placing, dot(before_grad, in_w, 1, 1)) + router_back
    in_w_grad = dot(received, before_grad, 0, 0)
    expert_w_grad = dot(activated.astype(BF16), arriving, 0, 0)
    hidden_part, gain_ffn_grad = norm_backward(normed_grad, hidden, scale_ffn, gain_f)
    hidden_grad = upstream + hidden_part
    attended_grad = hidden_grad.astype(BF16)
    split = weights.reshape(width, 2, 4, -1)
    out_w = split[:, :, 3].reshape(width, -1)
    mixed_heads = dot(attended_grad, out_w, 1, 0).astype(BF16).reshape(count, -1, HD)
    scores = jnp.einsum("qhd,khd->hqk", query, key, preferred_element_type=F32)
    scores = jnp.where(mask[None], scores * (1.0 / math.sqrt(HD)), NEGATIVE)
    probs = jnp.exp(scores - log_total[..., None])
    value_grad = jnp.einsum(
        "hqk,qhd->khd", probs.astype(BF16), mixed_heads, preferred_element_type=F32
    )
    prob_grad = jnp.einsum("qhd,khd->hqk", mixed_heads, value, preferred_element_type=F32)
    inner = jnp.sum(probs * prob_grad, axis=-1, keepdims=True)
    score_grad = (probs * (prob_grad - inner)).astype(BF16)
    factor = 1.0 / math.sqrt(HD)
    query_grad = jnp.einsum("hqk,khd->qhd", score_grad, key, preferred_element_type=F32) * factor
    key_grad = jnp.einsum("hqk,qhd->khd", score_grad, query, preferred_element_type=F32) * factor
    grads = [
        part.reshape(count, 2, 1, -1).astype(BF16) for part in (query_grad, key_grad, value_grad)
    ]
    qkv_grad = jnp.concatenate(grads, axis=2)
    qkv_w = split[:, :, :3].reshape(width, -1)
    normed_back = dot(qkv_grad.reshape(count, -1), qkv_w, 1, 1)
    qkv_w_grad = dot(normed, qkv_grad.reshape(count, -1), 0, 0).reshape(width, 2, 3, -1)
    out_w_grad = dot(attended_grad, mixed, 0, 0).reshape(width, 2, 1, -1)
    attn_grad = jnp.concatenate([qkv_w_grad, out_w_grad], axis=2).reshape(width, 2, -1)
    input_part, gain_attn_grad = norm_backward(normed_back, inputs, scale_attn, gain_a)
    input_grad = (hidden_grad + input_part).astype(BF16)
    small = jnp.concatenate([gain_attn_grad[None], gain_ffn_grad[None], router_grad], axis=0)
    return (input_grad, attn_grad, small, in_w_grad, expert_w_grad)


def reduce_attention(grad, section):
    width = grad.shape[0]
    count = lax.axis_size("dp")
    mine = grad[:, 0] + swap(grad[:, 1].astype(BF16), "tensor").astype(F32)
    halves = mine.reshape(count, 2, width // count // 2, -1)
    keep = lax.dynamic_index_in_dim(halves, section, 1, keepdims=False)
    send = lax.dynamic_index_in_dim(halves, 1 - section, 1, keepdims=False)
    total = keep + swap(send.astype(BF16), "section").astype(F32)
    return all_to_all(total.astype(BF16)).astype(F32).sum(axis=0)


def pair_up(values, tensor):
    half = values.shape[0] // 2
    halves = values.reshape(2, half, -1)
    own = entry(halves, tensor)
    other = swap(entry(halves, 1 - tensor), "tensor")
    return ordered(tensor, own[None], other[None])


def by_section(pairs, section):
    first, second = pairs
    own = jnp.where(section == 0, first, second)
    other = swap(jnp.where(section == 0, second, first), "section")
    return ordered(section, own, other)


def shards(
    x_in, d_out, lengths, routes, gain_attn, w_qkv, w_attn_out, gain_ffn, w_router, w_in, w_exp_out
):
    section = lax.axis_index("section")
    tensor = lax.axis_index("tensor")
    count = lax.axis_size("dp")
    width = x_in.shape[2]
    rows = 2 * x_in.shape[1]
    own_batch = 2 * section + tensor
    peer_batch = 2 * section + 1 - tensor

    def by_layer(own):
        other = swap(own, "section")
        return [jnp.where(section == layer, own, other) for layer in range(2)]

    packed = jnp.concatenate([w_qkv[0], w_attn_out[0].T[None]], axis=0)
    packed = jnp.moveaxis(packed, 0, 1).reshape(width // count, -1)
    packs = by_layer(packed)
    attn_w = [
        lax.all_gather(
            jnp.concatenate([pack, swap(pack, "tensor")], axis=1), "dp", axis=0, tiled=True
        )
        for pack in packs
    ]
    small = by_layer(jnp.concatenate([gain_attn, gain_ffn, w_router[0].T], axis=0))
    own_route = entry(routes[0, :, :, 0], own_batch)
    other_route = swap(entry(routes[0, :, :, 0], 2 * (1 - section) + tensor), "section")
    route = [jnp.where(section == layer, own_route, other_route) for layer in range(2)]
    in_w = by_layer(w_in[0, 0])
    expert_w = by_layer(w_exp_out[0, 0])
    params = [
        (
            small[layer][0].astype(F32),
            small[layer][1].astype(F32),
            attn_w[layer],
            small[layer][2:],
            in_w[layer],
            expert_w[layer],
        )
        for layer in range(2)
    ]
    mask = sequence_mask(entry(lengths[:, 0], own_batch), rows)

    def whole_group(array):
        return ordered(
            tensor, entry(array, own_batch), swap(entry(array, peer_batch), "tensor")
        )

    first = whole_group(x_in).astype(F32)
    upstream = whole_group(d_out).astype(F32)
    state0, out0 = layer_forward(first, params[0], mask, route[0])
    state1, out1 = layer_forward(out0.astype(F32), params[1], mask, route[1])
    grad1, attn1, small1, in1, expert1 = layer_backward(upstream, state1, params[1], mask)
    grad0, attn0, small0, in0, expert0 = layer_backward(grad1.astype(F32), state0, params[0], mask)
    section_out = by_section([pair_up(out0, tensor), pair_up(out1, tensor)], section)
    section_in_grad = by_section([pair_up(grad0, tensor), pair_up(grad1, tensor)], section)

    def settle(first_grad, second_grad):
        from_second = one_way(first_grad.astype(BF16), "section", 1, 0).astype(F32)
        from_first = one_way(second_grad.astype(BF16), "section", 0, 1).astype(F32)
        return jnp.where(section == 0, first_grad + from_second, second_grad + from_first)

    in_w_grad = settle(in0, in1)
    expert_w_grad = settle(expert0, expert1)
    reduced = [reduce_attention(attn0, section), reduce_attention(attn1, section)]
    own_half = jnp.where(section == 0, reduced[0], reduced[1])
    other_half = swap(
        jnp.where(section == 0, reduced[1], reduced[0]).astype(BF16), "section"
    ).astype(F32)
    attn_grad = ordered(section, own_half, other_half).reshape(width // count, 4, -1)
    qkv_grad = jnp.moveaxis(attn_grad[:, :3], 1, 0)
    out_grad = attn_grad[:, 3].T
    own_small = jnp.where(section == 0, small0, small1)
    own_small = own_small + swap(jnp.where(section == 0, small1, small0), "section")
    own_small = own_small + swap(own_small, "tensor")
    spread = jnp.broadcast_to(own_small[None], (count,) + own_small.shape)
    own_small = jnp.sum(all_to_all(spread), axis=0)
    return (
        section_out[None],
        section_in_grad[None],
        own_small[0][None],
        qkv_grad[None],
        out_grad[None],
        own_small[1][None],
        own_small[2:].T[None],
        in_w_grad[None, None],
        expert_w_grad[None, None],
    )


def solution(mesh):
    in_specs = (
        P(None, ("dp", "tensor"), None),
        P(None, ("dp", "tensor"), None),
        P(None, "dp", None),
        P("section", None, "dp", None),
        P("section", None),
        P("section", None, "dp", "tensor"),
        P("section", "tensor", "dp"),
        P("section", None),
        P("section", None, None),
        P("section", "dp", None, "tensor"),
        P("section", "dp", "tensor", None),
    )
    out_specs = (
        P("section", None, ("dp", "tensor"), None),
        P("section", None, ("dp", "tensor"), None),
        P("section", None),
        P("section", None, "dp", "tensor"),
        P("section", "tensor", "dp"),
        P("section", None),
        P("section", None, None),
        P("section", "dp", None, "tensor"),
        P("section", "dp", "tensor", None),
    )
    return jax.shard_map(shards, mesh=mesh, in_specs=in_specs, out_specs=out_specs, check_vma=False)
```

time: 1480 us -> 845 us (0.57)
  blocking collectives: 373 us -> 0 us
  other arithmetic: 218 us -> 66.6 us
  matrix products: 276 us -> 166 us
  local copies, waits for them, and re-layouts: 180 us -> 126 us
  waiting for transfers between devices: 309 us -> 362 us
    ppermute x8 -> x34, waiting for transfers between devices: 29.3 us -> 226 us  [the longest x30 189 us: swap(): return lax.ppermute(values, axis, [(0, 1), (1, 0)])]
    all_gather x21 -> x0, blocking collectives: 160 us -> none  [the longest x20 141 us: rows_gather(): return lax.all_gather(values, 'tensor', axis=0, tiled=True)]
    all_to_all x6 -> x0, blocking collectives: 153 us -> none  [to_experts(): return lax.all_to_all(values, 'dp', split_axis=0, concat_axis=0, tiled=True)]
    reduce_scatter x20 -> x0, waiting for transfers between devices: 121 us -> none  [rows_sum(): lax.psum_scatter(values.astype(jnp.bfloat16), 'tensor', scatter_dimension...]
    dot_general x120 -> x52, matrix products: 276 us -> 166 us  [the longest x36 136 us: dot(): lax.dot_general(left, right, (((left_dim,), (right_dim,)), ((), ())), pre...]
    psum x1 -> x0, blocking collectives: 61 us -> none  [shards(): lax.psum(small_sums, ('dp', 'tensor'))]
    unnamed x39 -> x7, other arithmetic: 60.1 us -> 1.07 us
    all_to_all x16 -> x11, waiting for transfers between devices: 157 us -> 98.6 us  [all_to_all(): return lax.all_to_all(values, 'dp', split_axis=0, concat_axis=0, tiled=True)]
  transfers between devices with their start and end apart: 45 -> 47, of which waited for: 41 -> 25; matrix products, arithmetic and copies ran while one was open for 22% -> 32% of each run, Pallas kernels for 0% -> 0%
where the time goes in v1:
time: 845 us; the launch traced here: 836 us
  waiting for transfers between devices  362 us (43%)
  matrix products  166 us (20%)
  local copies, waits for them, and re-layouts  126 us (15%)
  starting transfers between devices  99 us (12%)
  other arithmetic  66.6 us (8%)
  between operations  16.3 us (2%)
    ppermute x30, waiting for transfers between devices, swap(): return lax.ppermute(values, axis, [(0, 1), (1, 0)])  189 us
    dot_general x36, matrix products, dot(): lax.dot_general(left, right, (((left_dim,), (right_dim,)), ((), ())), pre...  136 us
    all_to_all x11, waiting for transfers between devices, all_to_all(): return lax.all_to_all(values, 'dp', split_axis=0, concat_axis=0, tiled=True)  98.6 us
    all_to_all x11, starting transfers between devices, all_to_all(): return lax.all_to_all(values, 'dp', split_axis=0, concat_axis=0, tiled=True)  47.3 us
    unnamed x264, local copies, waits for them, and re-layouts  40.4 us
    all_gather x2, waiting for transfers between devices, shards(): lax.all_gather(jnp.concatenate([pack, swap(pack, 'tensor')], axis=1), 'dp...  37.7 us
    ppermute x30, starting transfers between devices, swap(): return lax.ppermute(values, axis, [(0, 1), (1, 0)])  37.3 us
    ppermute x4, waiting for transfers between devices, one_way(): return lax.ppermute(values, axis, [(source, target)])  36.9 us
  transfers between devices with their start and end apart: 47, of which 25 were waited for; matrix products, arithmetic and copies ran while one was open for 32% of the time, Pallas kernels for 0%

profile of v1, /device:TPU:0, one launch (start us, length us, event | category | flops | bytes accessed | tf_op | source)
XLA Modules:
  0.0 835.9 jit_solution(16879730905082561467)
XLA Ops:
  11.4 7.0 collective-permute-done.2
  20.3 6.4 collective-permute-done.3
  36.2 5.9 collective-permute-done.10
  43.0 37.7 %all-gather.3.cloned.1.call-done = bf16[768,3072]{1,0:T(8,128)(2,1)} async-done(((bf16[96,3072]{1,0:T(8,128)(2,1)}), bf16[768,3072]{1,0:T(8,128)(2,1)}) %all-gather.3.cloned.1.call-update) | async-done | bytes 4718608 | tf_op jit(solution)/shard_map/all_gather | solution.py:230
  80.7 3.8 convolution_convert_fusion.1
  94.9 6.6 copy.117
  109.7 4.5 all-to-all-start
  115.7 32.9 %all-to-all-done = bf16[8,64,768]{2,1,0:T(8,128)(2,1)} async-done(((bf16[8,64,768]{2,1,0:T(8,128)(2,1)}), bf16[8,64,768]{2,1,0:T(8,128)(2,1)}, u32[]{:S(2)}, u32[]{:S(2)}) %all-to-all-start) | async-done | bytes 786464 | tf_op jit(solution)/shard_map/all_to_all | solution.py:24
  150.1 18.1 %collective-permute-done.5 = bf16[512,768]{1,0:T(8,128)(2,1)S(1)} collective-permute-done((bf16[512,768]{1,0:T(8,128)(2,1)}, bf16[512,768]{1,0:T(8,128)(2,1)S(1)}, u32[]{:S(2)}, u32[]{:S(2)}) %collective-permute-start.5) | collective-permute-done | bytes 786464 | tf_op jit(solution)/shard_map/ppermute | solution.py:16
  168.3 4.6 fusion.53
  173.0 3.9 fusion.59
  178.5 17.2 %collective-permute-done.8 = bf16[512,768]{1,0:T(8,128)(2,1)S(1)} collective-permute-done((bf16[512,768]{1,0:T(8,128)(2,1)S(1)}, bf16[512,768]{1,0:T(8,128)(2,1)S(1)}, u32[]{:S(2)}, u32[]{:S(2)}) %collective-permute-start.8) | collective-permute-done | bytes 786464 | tf_op jit(solution)/shard_map/ppermute | solution.py:16
  196.7 4.7 all-to-all-start.1
  203.1 6.6 copy.122
  215.5 6.9 all-to-all-done.1
  225.6 5.0 convolution_convert_fusion
  230.6 4.2 reshape.725
  234.8 5.5 fusion.184
  260.3 4.2 all-to-all-start.2
  275.5 10.0 %all-to-all-done.2 = bf16[8,64,768]{2,1,0:T(8,128)(2,1)} async-done(((bf16[8,64,768]{2,1,0:T(8,128)(2,1)}), bf16[8,64,768]{2,1,0:T(8,128)(2,1)}, u32[]{:S(2)}, u32[]{:S(2)}) %all-to-all-start.2) | async-done | bytes 786464 | tf_op jit(solution)/shard_map/all_to_all | solution.py:24
  285.5 4.4 all-to-all-start.4
  291.4 19.4 %all-to-all-done.4 = bf16[8,64,768]{2,1,0:T(8,128)(2,1)} async-done(((bf16[8,64,768]{2,1,0:T(8,128)(2,1)}), bf16[8,64,768]{2,1,0:T(8,128)(2,1)}, u32[]{:S(2)}, u32[]{:S(2)}) %all-to-all-start.4) | async-done | bytes 786464 | tf_op jit(solution)/shard_map/all_to_all | solution.py:24
  312.3 4.9 fusion.51
  317.3 7.3 fusion.61
  325.5 6.1 collective-permute-done.16
  331.5 9.0 %fusion.13 = bf16[1024,1536]{1,0:T(8,128)(2,1)} fusion(f32[1024,1536]{1,0:T(8,128)S(1)} %fusion.51, bf16[512,768]{1,0:T(8,128)(2,1)S(1)} %collective-permute-done.16, bf16[512,768]{1,0:T(8,128)(2,1)} %bitcast.48, bf16[1536,768]{1,0:T(8,128)(2,1)} %collective-permute-done.7, pred[]{:T(512)S(6)} %eq.51, bf16[1,1,1536,768]{3,2,1,0:T(8,128)(2,1)S(1)} %copy-done.110), kind=kOutput, calls=%fused_computation.19 | convolution fusion | flops 2451701760 | bytes 15728641 | tf_op jit(solution)/shard_map/dot_general | solution.py:28
  340.5 6.5 collective-permute-done.12
  348.1 4.2 all-to-all-start.3
  352.3 6.0 fusion.60
  359.9 18.3 %collective-permute-done.17 = bf16[512,768]{1,0:T(8,128)(2,1)S(1)} collective-permute-done((bf16[512,768]{1,0:T(8,128)(2,1)S(1)}, bf16[512,768]{1,0:T(8,128)(2,1)S(1)}, u32[]{:S(2)}, u32[]{:S(2)}) %collective-permute-start.17) | collective-permute-done | bytes 786464 | tf_op jit(solution)/shard_map/ppermute | solution.py:16
  379.3 5.0 all-to-all-start.5
  389.8 15.6 %all-to-all-done.5 = bf16[8,64,768]{2,1,0:T(8,128)(2,1)} async-done(((bf16[8,64,768]{2,1,0:T(8,128)(2,1)}), bf16[8,64,768]{2,1,0:T(8,128)(2,1)}, u32[]{:S(2)}, u32[]{:S(2)}) %all-to-all-start.5) | async-done | bytes 786464 | tf_op jit(solution)/shard_map/all_to_all | solution.py:24
  427.8 4.3 fusion.85
  435.3 4.2 all-to-all-start.6
  441.9 9.9 %fusion.191 = (bf16[1536,768]{1,0:T(8,128)(2,1)}, f32[1536,768]{1,0:T(8,128)}) fusion(bf16[512,768]{1,0:T(8,128)(2,1)} %copy-done.112, bf16[512,768]{1,0:T(8,128)(2,1)} %bitcast.48, f32[1024,1536]{1,0:T(8,128)} %copy-done.114), kind=kOutput, calls=%fused_computation.344 | convolution fusion | flops 2434400256 | bytes 14942208 | tf_op jit(solution)/shard_map/dot_general | solution.py:28
  451.8 8.3 collective-permute-start.33
  467.3 5.6 fusion.40
  472.8 4.0 pad_maximum_fusion.1
  482.2 4.3 copy.169
  487.7 8.5 %fusion.6 = bf16[1024,1536]{1,0:T(8,128)(2,1)S(1)} fusion(f32[1024,1536]{1,0:T(8,128)} %copy-done.113, bf16[512,768]{1,0:T(8,128)(2,1)} %collective-permute-done.18, bf16[512,768]{1,0:T(8,128)(2,1)} %bitcast.61, bf16[1536,768]{1,0:T(8,128)(2,1)} %collective-permute-done.7, pred[]{:T(512)S(6)} %eq.40, bf16[1,1,1536,768]{3,2,1,0:T(8,128)(2,1)} %param.21), kind=kOutput, calls=%fused_computation.12 | convolution fusion | flops 2451701760 | bytes 15728641 | tf_op jit(solution)/shard_map/dot_general | solution.py:28
  500.7 7.2 fusion.189
  510.4 6.2 copy.168
  526.9 30.9 %collective-permute-done.19 = bf16[512,768]{1,0:T(8,128)(2,1)} collective-permute-done((bf16[512,768]{1,0:T(8,128)(2,1)}, bf16[512,768]{1,0:T(8,128)(2,1)}, u32[]{:S(2)}, u32[]{:S(2)}) %collective-permute-start.19) | collective-permute-done | bytes 786464 | tf_op jit(solution)/shard_map/ppermute | solution.py:16
  561.7 5.2 all-to-all-start.7
  571.5 3.8 bitcast_add_fusion
  580.6 7.3 all-to-all-done.7
  609.7 4.1 fusion.42
  613.8 4.0 pad_maximum_fusion
  617.8 3.7 copy-done.4
  625.2 10.1 %fusion.192 = (bf16[1536,768]{1,0:T(8,128)(2,1)}, f32[1536,768]{1,0:T(8,128)}) fusion(bf16[512,768]{1,0:T(8,128)(2,1)} %collective-permute-done.18, bf16[512,768]{1,0:T(8,128)(2,1)} %bitcast.61, f32[1024,1536]{1,0:T(8,128)} %copy-done.113), kind=kOutput, calls=%fused_computation.345 | convolution fusion | flops 2434400256 | bytes 14942208 | tf_op jit(solution)/shard_map/dot_general | solution.py:28
  642.2 3.7 collective-permute-done.23
  650.3 6.0 copy.166
  656.3 22.2 %collective-permute-done.24 = f32[10,768]{1,0:T(8,128)S(1)} collective-permute-done((f32[10,768]{1,0:T(8,128)S(1)}, f32[10,768]{1,0:T(8,128)S(1)}, u32[]{:S(2)}, u32[]{:S(2)}) %collective-permute-start.24) | collective-permute-done | bytes 30752 | tf_op jit(solution)/shard_map/ppermute | solution.py:16
  684.9 5.2 bitcast_add_fusion.1
  690.1 6.5 all-to-all-done.8
  702.2 4.2 collective-permute-start.26
  706.4 7.8 fusion.190
  723.2 36.9 %collective-permute-done.26 = bf16[8,48,1536]{2,1,0:T(8,128)(2,1)S(1)} collective-permute-done((bf16[8,48,1536]{2,1,0:T(8,128)(2,1)S(1)}, bf16[8,48,1536]{2,1,0:T(8,128)(2,1)S(1)}, u32[]{:S(2)}, u32[]{:S(2)}) %collective-permute-start.26) | collective-permute-done | bytes 1179680 | tf_op jit(solution)/shard_map/ppermute | solution.py:16
  761.5 3.8 all-to-all-start.9
  765.4 8.5 %select_bitcast_fusion = f32[1,1,1536,768]{3,2,1,0:T(8,128)} fusion(f32[1536,768]{1,0:T(8,128)} %get-tuple-element.114, bf16[1536,768]{1,0:T(8,128)(2,1)} %collective-permute-done.33, f32[1536,768]{1,0:T(8,128)} %get-tuple-element.116, bf16[1536,768]{1,0:T(8,128)(2,1)} %collective-permute-done.32, pred[]{:T(512)S(6)} %eq.40), kind=kLoop, calls=%fused_computation.24 | loop fusion | flops 5898240 | bytes 18874368 | tf_op jit(solution)/shard_map/broadcast_in_dim | solution.py:297
  773.9 9.4 %collective-permute-done.31 = bf16[768,1536]{1,0:T(8,128)(2,1)} collective-permute-done((bf16[768,1536]{1,0:T(8,128)(2,1)}, bf16[768,1536]{1,0:T(8,128)(2,1)}, u32[]{:S(2)}, u32[]{:S(2)}) %collective-permute-start.31) | collective-permute-done | bytes 2359328 | tf_op jit(solution)/shard_map/ppermute | solution.py:20
  783.3 27.5 %collective-permute-done.30 = bf16[768,1536]{1,0:T(8,128)(2,1)} collective-permute-done((bf16[768,1536]{1,0:T(8,128)(2,1)}, bf16[768,1536]{1,0:T(8,128)(2,1)}, u32[]{:S(2)}, u32[]{:S(2)}) %collective-permute-start.30) | collective-permute-done | bytes 2359328 | tf_op jit(solution)/shard_map/ppermute | solution.py:20
  810.8 6.0 select_bitcast_fusion.1
  821.9 5.0 collective-permute-done.29
  (476 shorter events, 232.8 us)
Async XLA Ops:
  7.2 73.4 %all-gather.3.cloned.1.call-start = ((), (), s32[]{:S(2)}) async-start(), calls=%async_computation.11 | async-start | bytes 5308416 | tf_op jit(solution)/shard_map/all_gather | solution.py:230
  8.4 10.0 %collective-permute-start.2 = (bf16[96,1536]{1,0:T(8,128)(2,1)S(1)}, bf16[96,1536]{1,0:T(8,128)(2,1)S(1)}, u32[]{:S(2)}, u32[]{:S(2)}) collective-permute-start(bf16[96,1536]{1,0:T(8,128)(2,1)S(1)} %bitcast.336), channel_id=1, source_target_pairs={{0,16},{16,0},{1,17},{17,1},{2,18},{18,2},{3,19},{19,3},{4,20},{20... | collective-permute-start | bytes 884744 | tf_op jit(solution)/shard_map/ppermute | solution.py:16
  18.5 8.3 collective-permute-start.3
  27.6 175.4 %all-gather.5.cloned.1.call-start = ((), (), s32[]{:S(2)}) async-start(), calls=%async_computation.12 | async-start | bytes 5308416 | tf_op jit(solution)/shard_map/all_gather | solution.py:230
  27.7 79.0 %copy-start.36 = (bf16[128,768]{1,0:T(8,128)(2,1)}, bf16[128,768]{1,0:T(8,128)(2,1)S(1)}, u32[]{:S(2)}) copy-start(bf16[128,768]{1,0:T(8,128)(2,1)S(1)} %get-tuple-element.67) | copy-start | bytes 589828
  27.7 8.2 collective-permute-start
  29.3 5.4 collective-permute-start.1
  30.8 3.6 collective-permute-start.4
  31.4 118.8 %collective-permute-start.6 = (bf16[768,1536]{1,0:T(8,128)(2,1)}, bf16[768,1536]{1,0:T(8,128)(2,1)}, u32[]{:S(2)}, u32[]{:S(2)}) collective-permute-start(bf16[768,1536]{1,0:T(8,128)(2,1)} %bitcast.352), channel_id=1, source_target_pairs={{0,16},{16,0},{1,17},{17,1},{2,18},{18,2},{3,19},{19,3},{4,20},{20... | collective-permute-start | bytes 7077896 | tf_op jit(solution)/shard_map/ppermute | solution.py:16
  33.3 72.6 %copy-start.22 = (pred[256,256]{0,1:T(8,128)(4,1)}, pred[256,256]{0,1:T(8,128)(4,1)S(1)}, u32[]{:S(2)}) copy-start(pred[256,256]{0,1:T(8,128)(4,1)S(1)} %fusion.108) | copy-start | bytes 196612
  34.5 167.1 %copy-start.89 = (s32[256]{0:T(256)}, s32[256]{0:T(256)S(1)}, u32[]{:S(2)}) copy-start(s32[256]{0:T(256)S(1)} %get-tuple-element.84) | copy-start | bytes 3076
  34.7 73.7 %copy-start.83 = (s32[256]{0:T(256)}, s32[256]{0:T(256)S(1)}, u32[]{:S(2)}) copy-start(s32[256]{0:T(256)S(1)} %convert_add_fusion.5) | copy-start | bytes 3076
  35.4 45.3 %copy-start.71 = (bf16[10,768]{1,0:T(8,128)(2,1)}, bf16[10,768]{1,0:T(8,128)(2,1)S(1)}, u32[]{:S(2)}) copy-start(bf16[10,768]{1,0:T(8,128)(2,1)S(1)} %get-tuple-element.81) | copy-start | bytes 46084
  35.4 6.7 collective-permute-start.10
  35.9 44.8 %copy-start.77 = (f32[768]{0:T(1024)}, f32[768]{0:T(1024)S(1)}, u32[]{:S(2)}) copy-start(f32[768]{0:T(1024)S(1)} %get-tuple-element.47) | copy-start | bytes 9220
  35.9 71.5 %copy-start.72 = (f32[768]{0:T(1024)}, f32[768]{0:T(1024)S(1)}, u32[]{:S(2)}) copy-start(f32[768]{0:T(1024)S(1)} %get-tuple-element.46) | copy-start | bytes 9220
  35.9 44.7 %copy-start.39 = (bf16[128,768]{1,0:T(8,128)(2,1)}, bf16[128,768]{1,0:T(8,128)(2,1)S(1)}, u32[]{:S(2)}) copy-start(bf16[128,768]{1,0:T(8,128)(2,1)S(1)} %collective-permute-done) | copy-start | bytes 589828
  36.1 44.5 %copy-start.105 = (f32[256]{0:T(256)}, f32[256]{0:T(256)S(1)}, u32[]{:S(2)}) copy-start(f32[256]{0:T(256)S(1)} %add_rsqrt_fusion.3) | copy-start | bytes 3076
  108.4 103.7 %copy-start.20 = (bf16[256,768]{1,0:T(8,128)(2,1)}, bf16[256,768]{1,0:T(8,128)(2,1)S(1)}, u32[]{:S(2)}) copy-start(bf16[256,768]{1,0:T(8,128)(2,1)S(1)} %multiply_convert_fusion.5) | copy-start | bytes 1179652
  109.7 39.0 %all-to-all-start = ((bf16[8,64,768]{2,1,0:T(8,128)(2,1)}), bf16[8,64,768]{2,1,0:T(8,128)(2,1)}, u32[]{:S(2)}, u32[]{:S(2)}) async-start(bf16[8,64,768]{2,1,0:T(8,128)(2,1)} %bitcast.317), calls=%async_computation | async-start | bytes 1572864 | tf_op jit(solution)/shard_map/all_to_all | solution.py:24
  114.2 58.7 %collective-permute-start.7 = (bf16[1536,768]{1,0:T(8,128)(2,1)}, bf16[1536,768]{1,0:T(8,128)(2,1)}, u32[]{:S(2)}, u32[]{:S(2)}) collective-permute-start(bf16[1536,768]{1,0:T(8,128)(2,1)} %bitcast.351), channel_id=1, source_target_pairs={{0,16},{16,0},{1,17},{17,1},{2,18},{18,2},{3,19},{19,3},{4,20},{20... | collective-permute-start | bytes 7077896 | tf_op jit(solution)/shard_map/ppermute | solution.py:16
  148.7 19.6 %collective-permute-start.5 = (bf16[512,768]{1,0:T(8,128)(2,1)}, bf16[512,768]{1,0:T(8,128)(2,1)S(1)}, u32[]{:S(2)}, u32[]{:S(2)}) collective-permute-start(bf16[512,768]{1,0:T(8,128)(2,1)} %bitcast.21), channel_id=1, source_target_pairs={{0,1},{1,0},{2,3},{3,2},{4,5},{5,4},{6,7},{7,6},{8,9},{9,8},{10,11... | collective-permute-start | bytes 2359304 | tf_op jit(solution)/shard_map/ppermute | solution.py:16
  176.9 18.7 %collective-permute-start.8 = (bf16[512,768]{1,0:T(8,128)(2,1)S(1)}, bf16[512,768]{1,0:T(8,128)(2,1)S(1)}, u32[]{:S(2)}, u32[]{:S(2)}) collective-permute-start(bf16[512,768]{1,0:T(8,128)(2,1)S(1)} %slice.222), channel_id=1, source_target_pairs={{0,1},{1,0},{2,3},{3,2},{4,5},{5,4},{6,7},{7,6},{8,9},{9,8},{10,11... | collective-permute-start | bytes 2359304 | tf_op jit(solution)/shard_map/ppermute | solution.py:16
  196.7 25.7 %all-to-all-start.1 = ((bf16[8,64,768]{2,1,0:T(8,128)(2,1)}), bf16[8,64,768]{2,1,0:T(8,128)(2,1)}, u32[]{:S(2)}, u32[]{:S(2)}) async-start(bf16[8,64,768]{2,1,0:T(8,128)(2,1)} %bitcast.313), calls=%async_computation.1 | async-start | bytes 1572864 | tf_op jit(solution)/shard_map/all_to_all | solution.py:24
  203.0 54.2 %copy-start.74 = (f32[768]{0:T(1024)}, f32[768]{0:T(1024)S(1)}, u32[]{:S(2)}) copy-start(f32[768]{0:T(1024)S(1)} %get-tuple-element.44) | copy-start | bytes 9220
  260.3 25.2 %all-to-all-start.2 = ((bf16[8,64,768]{2,1,0:T(8,128)(2,1)}), bf16[8,64,768]{2,1,0:T(8,128)(2,1)}, u32[]{:S(2)}, u32[]{:S(2)}) async-start(bf16[8,64,768]{2,1,0:T(8,128)(2,1)} %bitcast.314), calls=%async_computation.2 | async-start | bytes 1572864 | tf_op jit(solution)/shard_map/all_to_all | solution.py:24
  265.6 7.2 collective-permute-start.15
  285.5 25.4 %all-to-all-start.4 = ((bf16[8,64,768]{2,1,0:T(8,128)(2,1)}), bf16[8,64,768]{2,1,0:T(8,128)(2,1)}, u32[]{:S(2)}, u32[]{:S(2)}) async-start(bf16[8,64,768]{2,1,0:T(8,128)(2,1)} %bitcast.338), calls=%async_computation.4 | async-start | bytes 1572864 | tf_op jit(solution)/shard_map/all_to_all | solution.py:24
  289.9 22.5 %collective-permute-start.11 = (bf16[512,768]{1,0:T(8,128)(2,1)}, bf16[512,768]{1,0:T(8,128)(2,1)}, u32[]{:S(2)}, u32[]{:S(2)}) collective-permute-start(bf16[512,768]{1,0:T(8,128)(2,1)} %bitcast.37), channel_id=1, source_target_pairs={{0,1},{1,0},{2,3},{3,2},{4,5},{5,4},{6,7},{7,6},{8,9},{9,8},{10,11... | collective-permute-start | bytes 2359304 | tf_op jit(solution)/shard_map/ppermute | solution.py:16
  310.8 20.7 %collective-permute-start.16 = (bf16[512,768]{1,0:T(8,128)(2,1)}, bf16[512,768]{1,0:T(8,128)(2,1)S(1)}, u32[]{:S(2)}, u32[]{:S(2)}) collective-permute-start(bf16[512,768]{1,0:T(8,128)(2,1)} %bitcast.48), channel_id=1, source_target_pairs={{0,1},{1,0},{2,3},{3,2},{4,5},{5,4},{6,7},{7,6},{8,9},{9,8},{10,11... | collective-permute-start | bytes 2359304 | tf_op jit(solution)/shard_map/ppermute | solution.py:16
  324.7 22.3 %collective-permute-start.12 = (bf16[512,768]{1,0:T(8,128)(2,1)S(1)}, bf16[512,768]{1,0:T(8,128)(2,1)S(1)}, u32[]{:S(2)}, u32[]{:S(2)}) collective-permute-start(bf16[512,768]{1,0:T(8,128)(2,1)S(1)} %slice.221), channel_id=1, source_target_pairs={{0,1},{1,0},{2,3},{3,2},{4,5},{5,4},{6,7},{7,6},{8,9},{9,8},{10,11... | collective-permute-start | bytes 2359304 | tf_op jit(solution)/shard_map/ppermute | solution.py:16
  348.1 31.2 %all-to-all-start.3 = ((bf16[8,64,768]{2,1,0:T(8,128)(2,1)}), bf16[8,64,768]{2,1,0:T(8,128)(2,1)}, u32[]{:S(2)}, u32[]{:S(2)}) async-start(bf16[8,64,768]{2,1,0:T(8,128)(2,1)} %bitcast.315), calls=%async_computation.3 | async-start | bytes 1572864 | tf_op jit(solution)/shard_map/all_to_all | solution.py:24
  358.3 19.9 %collective-permute-start.17 = (bf16[512,768]{1,0:T(8,128)(2,1)S(1)}, bf16[512,768]{1,0:T(8,128)(2,1)S(1)}, u32[]{:S(2)}, u32[]{:S(2)}) collective-permute-start(bf16[512,768]{1,0:T(8,128)(2,1)S(1)} %slice.220), channel_id=1, source_target_pairs={{0,1},{1,0},{2,3},{3,2},{4,5},{5,4},{6,7},{7,6},{8,9},{9,8},{10,11... | collective-permute-start | bytes 2359304 | tf_op jit(solution)/shard_map/ppermute | solution.py:16
  379.3 26.1 %all-to-all-start.5 = ((bf16[8,64,768]{2,1,0:T(8,128)(2,1)}), bf16[8,64,768]{2,1,0:T(8,128)(2,1)}, u32[]{:S(2)}, u32[]{:S(2)}) async-start(bf16[8,64,768]{2,1,0:T(8,128)(2,1)} %bitcast.316), calls=%async_computation.5 | async-start | bytes 1572864 | tf_op jit(solution)/shard_map/all_to_all | solution.py:24
  435.3 31.4 %all-to-all-start.6 = ((bf16[8,64,768]{2,1,0:T(8,128)(2,1)}), bf16[8,64,768]{2,1,0:T(8,128)(2,1)}, u32[]{:S(2)}, u32[]{:S(2)}) async-start(bf16[8,64,768]{2,1,0:T(8,128)(2,1)} %bitcast.311), calls=%async_computation.6 | async-start | bytes 1572864 | tf_op jit(solution)/shard_map/all_to_all | solution.py:24
  440.3 128.5 %collective-permute-start.9 = (bf16[128,768]{1,0:T(8,128)(2,1)}, bf16[128,768]{1,0:T(8,128)(2,1)}, u32[]{:S(2)}, u32[]{:S(2)}) collective-permute-start(bf16[128,768]{1,0:T(8,128)(2,1)} %get-tuple-element.74), channel_id=1, source_target_pairs={{0,1},{1,0},{2,3},{3,2},{4,5},{5,4},{6,7},{7,6},{8,9},{9,8},{10,11... | collective-permute-start | bytes 589832 | tf_op jit(solution)/shard_map/ppermute | solution.py:16
  451.8 313.6 %collective-permute-start.33 = (bf16[1536,768]{1,0:T(8,128)(2,1)}, bf16[1536,768]{1,0:T(8,128)(2,1)}, u32[]{:S(2)}, u32[]{:S(2)}) collective-permute-start(bf16[1536,768]{1,0:T(8,128)(2,1)} %get-tuple-element.113), channel_id=1, source_target_pairs={{0,16},{1,17},{2,18},{3,19},{4,20},{5,21},{6,22},{7,23},{8,24},{9,... | collective-permute-start | bytes 7077896 | tf_op jit(solution)/shard_map/ppermute | solution.py:20
  466.8 21.0 %collective-permute-start.18 = (bf16[512,768]{1,0:T(8,128)(2,1)}, bf16[512,768]{1,0:T(8,128)(2,1)}, u32[]{:S(2)}, u32[]{:S(2)}) collective-permute-start(bf16[512,768]{1,0:T(8,128)(2,1)} %bitcast.61), channel_id=1, source_target_pairs={{0,1},{1,0},{2,3},{3,2},{4,5},{5,4},{6,7},{7,6},{8,9},{9,8},{10,11... | collective-permute-start | bytes 2359304 | tf_op jit(solution)/shard_map/ppermute | solution.py:16
  486.4 85.0 %collective-permute-start.27 = (bf16[768,1536]{1,0:T(8,128)(2,1)}, bf16[768,1536]{1,0:T(8,128)(2,1)}, u32[]{:S(2)}, u32[]{:S(2)}) collective-permute-start(bf16[768,1536]{1,0:T(8,128)(2,1)} %bitcast.318), channel_id=1, source_target_pairs={{0,1},{1,0},{2,3},{3,2},{4,5},{5,4},{6,7},{7,6},{8,9},{9,8},{10,11... | collective-permute-start | bytes 7077896 | tf_op jit(solution)/shard_map/ppermute | solution.py:16
  500.0 57.8 %collective-permute-start.19 = (bf16[512,768]{1,0:T(8,128)(2,1)}, bf16[512,768]{1,0:T(8,128)(2,1)}, u32[]{:S(2)}, u32[]{:S(2)}) collective-permute-start(bf16[512,768]{1,0:T(8,128)(2,1)} %slice.219), channel_id=1, source_target_pairs={{0,1},{1,0},{2,3},{3,2},{4,5},{5,4},{6,7},{7,6},{8,9},{9,8},{10,11... | collective-permute-start | bytes 2359304 | tf_op jit(solution)/shard_map/ppermute | solution.py:16
  519.9 182.3 %collective-permute-start.21 = (bf16[128,768]{1,0:T(8,128)(2,1)}, bf16[128,768]{1,0:T(8,128)(2,1)}, u32[]{:S(2)}, u32[]{:S(2)}) collective-permute-start(bf16[128,768]{1,0:T(8,128)(2,1)} %get-tuple-element.72), channel_id=1, source_target_pairs={{0,1},{1,0},{2,3},{3,2},{4,5},{5,4},{6,7},{7,6},{8,9},{9,8},{10,11... | collective-permute-start | bytes 589832 | tf_op jit(solution)/shard_map/ppermute | solution.py:16
  557.8 11.1 %collective-permute-start.13 = (bf16[128,768]{1,0:T(8,128)(2,1)}, bf16[128,768]{1,0:T(8,128)(2,1)}, u32[]{:S(2)}, u32[]{:S(2)}) collective-permute-start(bf16[128,768]{1,0:T(8,128)(2,1)} %get-tuple-element.76), channel_id=1, source_target_pairs={{0,1},{1,0},{2,3},{3,2},{4,5},{5,4},{6,7},{7,6},{8,9},{9,8},{10,11... | collective-permute-start | bytes 589832 | tf_op jit(solution)/shard_map/ppermute | solution.py:16
  561.7 26.2 %all-to-all-start.7 = ((bf16[8,64,768]{2,1,0:T(8,128)(2,1)}), bf16[8,64,768]{2,1,0:T(8,128)(2,1)}, u32[]{:S(2)}, u32[]{:S(2)}) async-start(bf16[8,64,768]{2,1,0:T(8,128)(2,1)} %bitcast.312), calls=%async_computation.7 | async-start | bytes 1572864 | tf_op jit(solution)/shard_map/all_to_all | solution.py:24
  571.4 142.8 %collective-permute-start.14 = (bf16[2,128,768]{2,1,0:T(8,128)(2,1)}, bf16[2,128,768]{2,1,0:T(8,128)(2,1)}, u32[]{:S(2)}, u32[]{:S(2)}) collective-permute-start(bf16[2,128,768]{2,1,0:T(8,128)(2,1)} %get-tuple-element.65), channel_id=1, source_target_pairs={{0,16},{16,0},{1,17},{17,1},{2,18},{18,2},{3,19},{19,3},{4,20},{20... | collective-permute-start | bytes 1179656 | tf_op jit(solution)/shard_map/ppermute | solution.py:16
  578.6 56.7 %collective-permute-start.28 = (bf16[8,48,1536]{2,1,0:T(8,128)(2,1)}, bf16[8,48,1536]{2,1,0:T(8,128)(2,1)}, u32[]{:S(2)}, u32[]{:S(2)}) collective-permute-start(bf16[8,48,1536]{2,1,0:T(8,128)(2,1)} %fusion.39), channel_id=1, source_target_pairs={{0,16},{16,0},{1,17},{17,1},{2,18},{18,2},{3,19},{19,3},{4,20},{20... | collective-permute-start | bytes 3538952 | tf_op jit(solution)/shard_map/ppermute | solution.py:16
  624.4 59.7 %collective-permute-start.25 = (bf16[768,1536]{1,0:T(8,128)(2,1)}, bf16[768,1536]{1,0:T(8,128)(2,1)S(1)}, u32[]{:S(2)}, u32[]{:S(2)}) collective-permute-start(bf16[768,1536]{1,0:T(8,128)(2,1)} %bitcast.319), channel_id=1, source_target_pairs={{0,1},{1,0},{2,3},{3,2},{4,5},{5,4},{6,7},{7,6},{8,9},{9,8},{10,11... | collective-permute-start | bytes 7077896 | tf_op jit(solution)/shard_map/ppermute | solution.py:16
  641.8 4.2 collective-permute-start.23
  646.0 32.6 %collective-permute-start.24 = (f32[10,768]{1,0:T(8,128)S(1)}, f32[10,768]{1,0:T(8,128)S(1)}, u32[]{:S(2)}, u32[]{:S(2)}) collective-permute-start(f32[10,768]{1,0:T(8,128)S(1)} %select_add_fusion), channel_id=1, source_target_pairs={{0,1},{1,0},{2,3},{3,2},{4,5},{5,4},{6,7},{7,6},{8,9},{9,8},{10,11... | collective-permute-start | bytes 92168 | tf_op jit(solution)/shard_map/ppermute | solution.py:16
  678.6 86.8 %collective-permute-start.32 = (bf16[1536,768]{1,0:T(8,128)(2,1)}, bf16[1536,768]{1,0:T(8,128)(2,1)}, u32[]{:S(2)}, u32[]{:S(2)}) collective-permute-start(bf16[1536,768]{1,0:T(8,128)(2,1)} %get-tuple-element.115), channel_id=1, source_target_pairs={{16,0},{17,1},{18,2},{19,3},{20,4},{21,5},{22,6},{23,7},{24,8},{25... | collective-permute-start | bytes 7077896 | tf_op jit(solution)/shard_map/ppermute | solution.py:20
  680.7 15.9 %all-to-all-start.8 = ((f32[8,10,768]{2,1,0:T(8,128)}), f32[8,10,768]{2,1,0:T(8,128)S(1)}, u32[]{:S(2)}, u32[]{:S(2)}) async-start(f32[8,10,768]{2,1,0:T(8,128)} %broadcast_in_dim.53), calls=%async_computation.8 | async-start | bytes 786432 | tf_op jit(solution)/shard_map/all_to_all | solution.py:24
  684.1 33.5 %collective-permute-start.20 = (bf16[128,768]{1,0:T(8,128)(2,1)}, bf16[128,768]{1,0:T(8,128)(2,1)}, u32[]{:S(2)}, u32[]{:S(2)}) collective-permute-start(bf16[128,768]{1,0:T(8,128)(2,1)} %get-tuple-element.70), channel_id=1, source_target_pairs={{0,1},{1,0},{2,3},{3,2},{4,5},{5,4},{6,7},{7,6},{8,9},{9,8},{10,11... | collective-permute-start | bytes 589832 | tf_op jit(solution)/shard_map/ppermute | solution.py:16
  696.6 65.0 %all-to-all-start.10 = ((bf16[8,48,1536]{2,1,0:T(8,128)(2,1)}), bf16[8,48,1536]{2,1,0:T(8,128)(2,1)S(1)}, u32[]{:S(2)}, u32[]{:S(2)}) async-start(bf16[8,48,1536]{2,1,0:T(8,128)(2,1)} %fusion.20), calls=%async_computation.10 | async-start | bytes 2359296 | tf_op jit(solution)/shard_map/all_to_all | solution.py:24
  700.2 60.0 %slice-start.12 = ((s8[4718592]{0:T(1024)(128)(4,1)}), s8[4194304]{0:T(1024)(128)(4,1)S(1)}, s32[]{:S(2)}) async-start(s8[4718592]{0:T(1024)(128)(4,1)} %bitcast.290), calls=%async_computation.25 | async-start | bytes 8388608
  702.2 58.0 %slice-start.13 = ((s8[4718592]{0:T(1024)(128)(4,1)}), s8[524288]{0:T(1024)(128)(4,1)S(1)}, s32[]{:S(2)}) async-start(s8[4718592]{0:T(1024)(128)(4,1)} %bitcast.290), calls=%async_computation.26 | async-start | bytes 1048576
  702.2 57.9 %collective-permute-start.26 = (bf16[8,48,1536]{2,1,0:T(8,128)(2,1)S(1)}, bf16[8,48,1536]{2,1,0:T(8,128)(2,1)S(1)}, u32[]{:S(2)}, u32[]{:S(2)}) collective-permute-start(bf16[8,48,1536]{2,1,0:T(8,128)(2,1)S(1)} %fusion.38), channel_id=1, source_target_pairs={{0,16},{16,0},{1,17},{17,1},{2,18},{18,2},{3,19},{19,3},{4,20},{20... | collective-permute-start | bytes 3538952 | tf_op jit(solution)/shard_map/ppermute | solution.py:16
  714.2 69.2 %collective-permute-start.31 = (bf16[768,1536]{1,0:T(8,128)(2,1)}, bf16[768,1536]{1,0:T(8,128)(2,1)}, u32[]{:S(2)}, u32[]{:S(2)}) collective-permute-start(bf16[768,1536]{1,0:T(8,128)(2,1)} %get-tuple-element.109), channel_id=1, source_target_pairs={{0,16},{1,17},{2,18},{3,19},{4,20},{5,21},{6,22},{7,23},{8,24},{9,... | collective-permute-start | bytes 7077896 | tf_op jit(solution)/shard_map/ppermute | solution.py:20
  717.6 93.2 %collective-permute-start.30 = (bf16[768,1536]{1,0:T(8,128)(2,1)}, bf16[768,1536]{1,0:T(8,128)(2,1)}, u32[]{:S(2)}, u32[]{:S(2)}) collective-permute-start(bf16[768,1536]{1,0:T(8,128)(2,1)} %get-tuple-element.111), channel_id=1, source_target_pairs={{16,0},{17,1},{18,2},{19,3},{20,4},{21,5},{22,6},{23,7},{24,8},{25... | collective-permute-start | bytes 7077896 | tf_op jit(solution)/shard_map/ppermute | solution.py:20
  760.1 60.1 %collective-permute-start.22 = (bf16[2,128,768]{2,1,0:T(8,128)(2,1)}, bf16[2,128,768]{2,1,0:T(8,128)(2,1)S(1)}, u32[]{:S(2)}, u32[]{:S(2)}) collective-permute-start(bf16[2,128,768]{2,1,0:T(8,128)(2,1)} %get-tuple-element.59), channel_id=1, source_target_pairs={{0,16},{16,0},{1,17},{17,1},{2,18},{18,2},{3,19},{19,3},{4,20},{20... | collective-permute-start | bytes 1179656 | tf_op jit(solution)/shard_map/ppermute | solution.py:16
  761.5 59.9 %all-to-all-start.9 = ((bf16[8,48,1536]{2,1,0:T(8,128)(2,1)}), bf16[8,48,1536]{2,1,0:T(8,128)(2,1)S(1)}, u32[]{:S(2)}, u32[]{:S(2)}) async-start(bf16[8,48,1536]{2,1,0:T(8,128)(2,1)} %fusion.21), calls=%async_computation.9 | async-start | bytes 2359296 | tf_op jit(solution)/shard_map/all_to_all | solution.py:24
  765.4 45.4 %slice-start.6 = ((s8[4718592]{0:T(1024)(128)(4,1)}), s8[4194304]{0:T(1024)(128)(4,1)S(1)}, s32[]{:S(2)}) async-start(s8[4718592]{0:T(1024)(128)(4,1)} %bitcast.281), calls=%async_computation.19 | async-start | bytes 8388608
  765.4 45.4 %slice-start.8 = ((s8[4718592]{0:T(1024)(128)(4,1)}), s8[4194304]{0:T(1024)(128)(4,1)S(1)}, s32[]{:S(2)}) async-start(s8[4718592]{0:T(1024)(128)(4,1)} %bitcast.283), calls=%async_computation.21 | async-start | bytes 8388608
  765.4 45.4 %slice-start.7 = ((s8[4718592]{0:T(1024)(128)(4,1)}), s8[524288]{0:T(1024)(128)(4,1)S(1)}, s32[]{:S(2)}) async-start(s8[4718592]{0:T(1024)(128)(4,1)} %bitcast.281), calls=%async_computation.20 | async-start | bytes 1048576
  765.4 45.4 %slice-start.9 = ((s8[4718592]{0:T(1024)(128)(4,1)}), s8[524288]{0:T(1024)(128)(4,1)S(1)}, s32[]{:S(2)}) async-start(s8[4718592]{0:T(1024)(128)(4,1)} %bitcast.283), calls=%async_computation.22 | async-start | bytes 1048576
  821.6 5.2 collective-permute-start.29
  (112 other events, 741.0 us)
Sparse Core Ops, SparseCore 0:
  27.7 52.8 all-gather.2
  82.9 65.9 all-gather.4

commit v2 on v1

v2 whole, which is shorter than its diff:
```python
import functools
import math

import jax
import jax.numpy as jnp
from jax import lax
from jax.experimental import pallas as pl
from jax.experimental.pallas import tpu as pltpu
from jax.sharding import PartitionSpec as P

HD = 64
EPSILON = 1e-06
NEGATIVE = -1e30
F32 = jnp.float32
BF16 = jnp.bfloat16


def swap(values, axis):
    return lax.ppermute(values, axis, [(0, 1), (1, 0)])


def one_way(values, axis, source, target):
    return lax.ppermute(values, axis, [(source, target)])


def all_to_all(values):
    return lax.all_to_all(values, "dp", split_axis=0, concat_axis=0, tiled=True)


def dot(left, right, left_dim, right_dim):
    return lax.dot_general(
        left, right, (((left_dim,), (right_dim,)), ((), ())), preferred_element_type=F32
    )


def ordered(index, own, other):
    return jnp.where(
        index == 0, jnp.concatenate([own, other], axis=0), jnp.concatenate([other, own], axis=0)
    )


def entry(array, index):
    return lax.dynamic_index_in_dim(array, index, 0, keepdims=False)


def norm_forward(inputs, gain):
    scaling = lax.rsqrt(jnp.mean(inputs * inputs, axis=-1, keepdims=True) + EPSILON)
    return (inputs * scaling * gain, scaling)


def smooth_gate(values):
    return jax.nn.gelu(values, approximate=True)


def routing(route_row, experts):
    count = route_row.shape[0]
    capacity = 2 * count // experts
    hot = route_row[:, None] == jnp.arange(experts, dtype=jnp.int32)[None, :]
    places = jnp.arange(count, dtype=jnp.int32)
    earlier = (places[:, None] > places[None, :]).astype(BF16)
    ranks = dot(earlier, hot.astype(BF16), 1, 0)
    ranking = jnp.sum(ranks * hot.astype(F32), axis=1).astype(jnp.int32)
    slots = route_row * capacity + ranking
    placing = (
        slots[None, :] == jnp.arange(experts * capacity, dtype=jnp.int32)[:, None]
    ).astype(BF16)
    return (hot.astype(F32), placing)


LANES = 128


def head_lanes(count):
    return lax.broadcasted_iota(jnp.int32, (count, LANES), 1) // HD


def attention_bias(seg_col, seg_row, count):
    rows = lax.broadcasted_iota(jnp.int32, (count, count), 0)
    cols = lax.broadcasted_iota(jnp.int32, (count, count), 1)
    return jnp.where((seg_col == seg_row) & (rows >= cols), 0.0, NEGATIVE)


def forward_kernel(
    a_ref, w_ref, gain_ref, router_ref, seg_col_ref, seg_row_ref, route_ref, placing_ref,
    xn_ref, qkv_ref, lse_ref, o_ref, h_ref, hn_ref, chances_ref, gate_ref, out_ref, *, experts,
):
    count, width = a_ref.shape
    part = width // 2
    pairs = part // LANES
    a = a_ref[...].astype(F32)
    xn = norm_forward(a, gain_ref[0:1, :])[0].astype(BF16)
    xn_ref[...] = xn
    bias = attention_bias(seg_col_ref[...], seg_row_ref[...], count)
    lanes = head_lanes(count)
    scale = 1.0 / math.sqrt(HD)
    for half in range(2):
        base = half * 3 * part
        qkv_ref[:, base:base + 3 * part] = dot(
            xn, w_ref[:, half * 4 * part:half * 4 * part + 3 * part], 1, 0
        ).astype(BF16)
    attended = a
    lse = jnp.zeros((count, LANES), F32)
    for half in range(2):
        base = half * 3 * part
        for pair in range(pairs):
            at = base + pair * LANES
            query = qkv_ref[:, at:at + LANES]
            key = qkv_ref[:, at + part:at + part + LANES]
            value = qkv_ref[:, at + 2 * part:at + 2 * part + LANES]
            mixed = None
            for head in range(2):
                own = jnp.where(lanes == head, query, jnp.zeros_like(query))
                scores = dot(own, key, 1, 1) * scale + bias
                top = jnp.max(scores, axis=-1, keepdims=True)
                weight = jnp.exp(scores - top)
                total = jnp.sum(weight, axis=-1, keepdims=True)
                probs = (weight * (1.0 / total)).astype(BF16)
                number = (half * pairs + pair) * 2 + head
                lse = jnp.where(
                    lax.broadcasted_iota(jnp.int32, lse.shape, 1) == number,
                    top + jnp.log(total), lse,
                )
                part_out = dot(probs, value, 1, 0)
                mixed = part_out if head == 0 else jnp.where(lanes == 0, mixed, part_out)
            o_at = half * part + pair * LANES
            o_ref[:, o_at:o_at + LANES] = mixed.astype(BF16)
        attended = attended + dot(
            o_ref[:, half * part:(half + 1) * part],
            w_ref[:, half * 4 * part + 3 * part:(half + 1) * 4 * part], 1, 1,
        )
    lse_ref[...] = lse
    h_ref[...] = attended
    hn = norm_forward(attended, gain_ref[1:2, :])[0].astype(BF16)
    hn_ref[...] = hn
    logits = dot(hn, router_ref[...], 1, 1)
    lane = lax.broadcasted_iota(jnp.int32, logits.shape, 1)
    logits = jnp.where(lane < experts, logits, NEGATIVE)
    raised = jnp.exp(logits - jnp.max(logits, axis=-1, keepdims=True))
    chances = raised * (1.0 / jnp.sum(raised, axis=-1, keepdims=True))
    chances_ref[...] = chances
    gate_ref[...] = jnp.sum(
        jnp.where(lane == route_ref[...], chances, 0.0), axis=-1, keepdims=True
    )
    out_ref[...] = dot(placing_ref[...], hn, 1, 0).astype(BF16)


def backward_kernel(
    back_ref, taking_ref, dz_ref, y_ref, a_ref, h_ref, hn_ref, qkv_ref, lse_ref, chances_ref,
    gate_ref, w_ref, gain_ref, router_ref, seg_col_ref, seg_row_ref, route_ref,
    da_ref, dqkv_ref, dattn_ref, small_ref, g_router_ref,
):
    count, width = a_ref.shape
    part = width // 2
    pairs = part // LANES
    dz = dz_ref[...].astype(F32)
    hidden = h_ref[...]
    chances = chances_ref[...]
    gate_grad = jnp.sum(dz * y_ref[...], axis=-1, keepdims=True)
    lane = lax.broadcasted_iota(jnp.int32, chances.shape, 1)
    hot = jnp.where(lane == route_ref[...], 1.0, 0.0)
    logit_grad = gate_ref[...] * (hot - chances) * gate_grad
    g_router_ref[...] = lax.dot_general(
        logit_grad, hn_ref[...].astype(F32), (((0,), (0,)), ((), ())),
        preferred_element_type=F32, precision=lax.Precision.HIGHEST,
    )
    hn_grad = dot(taking_ref[...], back_ref[...], 1, 0) + lax.dot_general(
        logit_grad, router_ref[...].astype(F32), (((1,), (0,)), ((), ())),
        preferred_element_type=F32, precision=lax.Precision.HIGHEST,
    )

    def norm_back(upstream, inputs, gain):
        scaling = lax.rsqrt(jnp.mean(inputs * inputs, axis=-1, keepdims=True) + EPSILON)
        weighted = upstream * gain
        scaled = inputs * scaling
        inner = jnp.mean(weighted * inputs, axis=-1, keepdims=True)
        return (
            scaling * weighted - scaled * (scaling * scaling * inner),
            jnp.sum(upstream * scaled, axis=0, keepdims=True),
        )

    hidden_part, gain_f_grad = norm_back(hn_grad, hidden, gain_ref[1:2, :])
    hidden_grad = dz + hidden_part
    attended_grad = hidden_grad.astype(BF16)
    dattn_ref[...] = attended_grad
    bias = attention_bias(seg_col_ref[...], seg_row_ref[...], count)
    lanes = head_lanes(count)
    scale = 1.0 / math.sqrt(HD)
    normed_grad = jnp.zeros((count, width), F32)
    for half in range(2):
        base = half * 3 * part
        mixed_grad = dot(
            attended_grad, w_ref[:, half * 4 * part + 3 * part:(half + 1) * 4 * part], 1, 0
        ).astype(BF16)
        for pair in range(pairs):
            at = base + pair * LANES
            query = qkv_ref[:, at:at + LANES]
            key = qkv_ref[:, at + part:at + part + LANES]
            value = qkv_ref[:, at + 2 * part:at + 2 * part + LANES]
            grad = mixed_grad[:, pair * LANES:(pair + 1) * LANES]
            dq = dk = dv = None
            for head in range(2):
                number = (half * pairs + pair) * 2 + head
                zero = jnp.zeros_like(query)
                own_q = jnp.where(lanes == head, query, zero)
                own_g = jnp.where(lanes == head, grad, zero)
                scores = dot(own_q, key, 1, 1) * scale + bias
                probs = jnp.exp(scores - lse_ref[:, number:number + 1])
                prob_grad = dot(own_g, value, 1, 1)
                inner = jnp.sum(probs * prob_grad, axis=-1, keepdims=True)
                score_grad = (probs * (prob_grad - inner)).astype(BF16)
                head_dv = dot(probs.astype(BF16), own_g, 0, 0)
                head_dk = dot(score_grad, own_q, 0, 0)
                head_dq = dot(score_grad, key, 1, 0)
                if head == 0:
                    dq, dk, dv = (head_dq, head_dk, head_dv)
                else:
                    dq = jnp.where(lanes == 0, dq, head_dq)
                    dk = dk + head_dk
                    dv = dv + head_dv
            dqkv_ref[:, at:at + LANES] = (dq * scale).astype(BF16)
            dqkv_ref[:, at + part:at + part + LANES] = (dk * scale).astype(BF16)
            dqkv_ref[:, at + 2 * part:at + 2 * part + LANES] = dv.astype(BF16)
        normed_grad = normed_grad + dot(
            dqkv_ref[:, base:base + 3 * part],
            w_ref[:, half * 4 * part:half * 4 * part + 3 * part], 1, 1,
        )
    input_part, gain_a_grad = norm_back(normed_grad, a_ref[...].astype(F32), gain_ref[0:1, :])
    small_ref[0:1, :] = gain_a_grad
    small_ref[1:2, :] = gain_f_grad
    da_ref[...] = (hidden_grad + input_part).astype(BF16)


def kernel_call(kernel, outs, flops, *args):
    moved = sum(math.prod(v.shape) * v.dtype.itemsize for v in (*args, *outs))
    return pl.pallas_call(
        kernel,
        out_shape=outs,
        in_specs=[pl.BlockSpec(memory_space=pltpu.VMEM)] * len(args),
        out_specs=[pl.BlockSpec(memory_space=pltpu.VMEM)] * len(outs),
        compiler_params=pltpu.CompilerParams(vmem_limit_bytes=48 * 1024 * 1024),
        cost_estimate=pl.CostEstimate(flops=flops, bytes_accessed=moved, transcendentals=0),
    )(*args)


def layer_start(inputs, params, segments, route_col, placing):
    gains, weights, router_w, experts = params
    count, width = inputs.shape
    struct = jax.ShapeDtypeStruct
    outs = [
        struct((count, width), BF16),
        struct((count, 3 * width), BF16),
        struct((count, LANES), F32),
        struct((count, width), BF16),
        struct((count, width), F32),
        struct((count, width), BF16),
        struct((count, LANES), F32),
        struct((count, 1), F32),
        struct((placing.shape[0], width), BF16),
    ]
    return kernel_call(
        functools.partial(forward_kernel, experts=experts), outs, 3 * 10**9,
        inputs, weights, gains, router_w, *segments, route_col, placing,
    )


def layer_end(back, taking, upstream, expert_out, inputs, state, params, segments, route_col):
    gains, weights, router_w, experts = params
    normed, qkv, lse, mixed, hidden, normed_ffn, chances, gate = state
    count, width = inputs.shape
    struct = jax.ShapeDtypeStruct
    outs = [
        struct((count, width), BF16),
        struct((count, 3 * width), BF16),
        struct((count, width), BF16),
        struct((2, width), F32),
        struct((LANES, width), F32),
    ]
    return kernel_call(
        backward_kernel, outs, 5 * 10**9,
        back, taking, upstream, expert_out, inputs, hidden, normed_ffn, qkv, lse, chances,
        gate, weights, gains, router_w, *segments, route_col,
    )

def attention_grads(normed, qkv_grad, mixed, attended_grad, section):
    width = normed.shape[1]
    part = width // 2

    def both(left, right):
        left = jnp.concatenate([left, swap(left, "tensor")], axis=0)
        wide = right.shape[1] // 2
        right = jnp.concatenate([right[:, :wide], swap(right[:, wide:], "tensor")], axis=0)
        return across(dot(left, right, 0, 0), section)

    return jnp.concatenate([both(normed, qkv_grad), both(attended_grad, mixed)], axis=1)


def across(grad, section):
    width = grad.shape[0]
    count = lax.axis_size("dp")
    halves = grad.reshape(count, 2, width // count // 2, -1)
    keep = lax.dynamic_index_in_dim(halves, section, 1, keepdims=False)
    send = lax.dynamic_index_in_dim(halves, 1 - section, 1, keepdims=False)
    total = keep + swap(send.astype(BF16), "section").astype(F32)
    return all_to_all(total.astype(BF16)).astype(F32).sum(axis=0)


def pair_up(values, tensor):
    half = values.shape[0] // 2
    halves = values.reshape(2, half, -1)
    own = entry(halves, tensor)
    other = swap(entry(halves, 1 - tensor), "tensor")
    return ordered(tensor, own[None], other[None])


def by_section(pairs, section):
    first, second = pairs
    own = jnp.where(section == 0, first, second)
    other = swap(jnp.where(section == 0, second, first), "section")
    return ordered(section, own, other)


def gelu_pair(before, active_grad):
    activated, back = jax.vjp(smooth_gate, before)
    return (activated.astype(BF16), back(active_grad)[0].astype(BF16))


def shards(
    x_in, d_out, lengths, routes, gain_attn, w_qkv, w_attn_out, gain_ffn, w_router, w_in, w_exp_out
):
    section = lax.axis_index("section")
    tensor = lax.axis_index("tensor")
    count = lax.axis_size("dp")
    width = x_in.shape[2]
    rows = 2 * x_in.shape[1]
    experts = w_router.shape[2]
    own_batch = 2 * section + tensor
    peer_batch = 2 * section + 1 - tensor

    def by_layer(own):
        other = swap(own, "section")
        return [jnp.where(section == layer, own, other) for layer in range(2)]

    packed = jnp.concatenate([w_qkv[0], w_attn_out[0].T[None]], axis=0)
    packed = jnp.moveaxis(packed, 0, 1).reshape(width // count, -1)
    beside = by_layer(packed)
    cross = lax.ppermute(packed, ("section", "tensor"), [(0, 3), (1, 2), (2, 1), (3, 0)])
    above = swap(packed, "tensor")
    beyond = [jnp.where(section == layer, above, cross) for layer in range(2)]
    attn_w = [
        lax.all_gather(
            jnp.concatenate([beside[layer], beyond[layer]], axis=1), "dp", axis=0, tiled=True
        )
        for layer in range(2)
    ]
    small = by_layer(jnp.concatenate([gain_attn, gain_ffn, w_router[0].T], axis=0))
    own_route = entry(routes[0, :, :, 0], own_batch)
    other_route = swap(entry(routes[0, :, :, 0], 2 * (1 - section) + tensor), "section")
    route = [jnp.where(section == layer, own_route, other_route) for layer in range(2)]
    placing = [routing(row, experts)[1] for row in route]
    taking = [table.T for table in placing]
    route_col = [row[:, None] for row in route]
    in_w = by_layer(w_in[0, 0])
    expert_w = by_layer(w_exp_out[0, 0])
    params = [
        (
            small[layer][:2].astype(F32),
            attn_w[layer],
            jnp.pad(small[layer][2:], ((0, LANES - experts), (0, 0))),
            experts,
        )
        for layer in range(2)
    ]
    bounds = jnp.cumsum(entry(lengths[:, 0], own_batch))
    places = jnp.arange(rows, dtype=jnp.int32)
    segment = jnp.sum((places[:, None] >= bounds[None, :]).astype(jnp.int32), axis=1)
    segments = (segment[:, None], segment[None, :])

    def whole_group(array):
        return ordered(
            tensor, entry(array, own_batch), swap(entry(array, peer_batch), "tensor")
        )

    def spread(outgoing):
        received = all_to_all(outgoing)
        return jnp.concatenate([received, swap(received, "tensor")], axis=0)

    def gathered(partial):
        half = partial.shape[0] // 2
        total = partial[:half] + swap(partial[half:].astype(BF16), "tensor").astype(F32)
        return all_to_all(total.astype(BF16))

    inputs = [whole_group(x_in), None]
    upstream = [None, whole_group(d_out)]
    states, received, before, expert_out, outs = ([], [], [], [], [])
    for layer in range(2):
        *state, outgoing = layer_start(
            inputs[layer], params[layer], segments, route_col[layer], placing[layer]
        )
        states.append(state)
        received.append(spread(outgoing))
        before.append(dot(received[layer], in_w[layer], 1, 0))
        active = smooth_gate(before[layer]).astype(BF16)
        back = gathered(dot(active, expert_w[layer], 1, 0))
        expert_out.append(dot(taking[layer], back, 1, 0))
        outs.append((state[4] + state[7] * expert_out[layer]).astype(BF16))
        if layer == 0:
            inputs[1] = outs[0]
    section_out = by_section([pair_up(out, tensor) for out in outs], section)
    arriving, active, before_grad = ([None, None], [None, None], [None, None])
    input_grads, attn_grads, smalls = ([None, None], [None, None], [None, None])
    for layer in (1, 0):
        state = states[layer]
        expert_grad = (state[7] * upstream[layer].astype(F32)).astype(BF16)
        arriving[layer] = spread(dot(placing[layer], expert_grad, 1, 0).astype(BF16))
        active[layer], before_grad[layer] = gelu_pair(
            before[layer], dot(arriving[layer], expert_w[layer], 1, 1)
        )
        back = gathered(dot(before_grad[layer], in_w[layer], 1, 1))
        input_grads[layer], qkv_grad, attended_grad, gains, g_router = layer_end(
            back, taking[layer], upstream[layer], expert_out[layer], inputs[layer], state,
            params[layer], segments, route_col[layer],
        )
        attn_grads[layer] = attention_grads(state[0], qkv_grad, state[3], attended_grad, section)
        smalls[layer] = jnp.concatenate([gains, g_router[:experts]], axis=0)
        if layer == 1:
            upstream[0] = input_grads[1]
    section_in_grad = by_section([pair_up(grad, tensor) for grad in input_grads], section)

    def own_layer(pair):
        return jnp.where(section == 0, pair[0], pair[1])

    def other_layer(pair):
        return jnp.where(section == 0, pair[1], pair[0])

    def from_other(pair):
        return jnp.where(
            section == 0, one_way(pair[0], "section", 1, 0), one_way(pair[1], "section", 0, 1)
        )

    far_rows = from_other(received)
    far_grads = from_other(arriving)
    far_before = dot(far_rows, w_in[0, 0], 1, 0)
    far_active, far_before_grad = gelu_pair(far_before, dot(far_grads, w_exp_out[0, 0], 1, 1))
    in_w_grad = dot(own_layer(received), own_layer(before_grad), 0, 0) + dot(
        far_rows, far_before_grad, 0, 0
    )
    expert_w_grad = dot(own_layer(active), own_layer(arriving), 0, 0) + dot(
        far_active, far_grads, 0, 0
    )
    own_half = own_layer(attn_grads)
    other_half = swap(other_layer(attn_grads).astype(BF16), "section").astype(F32)
    joined = ordered(section, own_half, other_half)
    part = width // 2
    qkv_grad = jnp.stack([joined[:, part * kind:part * (kind + 1)] for kind in range(3)])
    out_grad = joined[:, 3 * part:].T
    own_small = own_layer(smalls) + swap(other_layer(smalls), "section")
    own_small = own_small + swap(own_small, "tensor")
    copies = jnp.broadcast_to(own_small[None], (count,) + own_small.shape)
    own_small = jnp.sum(all_to_all(copies), axis=0)
    return (
        section_out[None],
        section_in_grad[None],
        own_small[0][None],
        qkv_grad[None],
        out_grad[None],
        own_small[1][None],
        own_small[2:].T[None],
        in_w_grad[None, None],
        expert_w_grad[None, None],
    )


def solution(mesh):
    in_specs = (
        P(None, ("dp", "tensor"), None),
        P(None, ("dp", "tensor"), None),
        P(None, "dp", None),
        P("section", None, "dp", None),
        P("section", None),
        P("section", None, "dp", "tensor"),
        P("section", "tensor", "dp"),
        P("section", None),
        P("section", None, None),
        P("section", "dp", None, "tensor"),
        P("section", "dp", "tensor", None),
    )
    out_specs = (
        P("section", None, ("dp", "tensor"), None),
        P("section", None, ("dp", "tensor"), None),
        P("section", None),
        P("section", None, "dp", "tensor"),
        P("section", "tensor", "dp"),
        P("section", None),
        P("section", None, None),
        P("section", "dp", None, "tensor"),
        P("section", "dp", "tensor", None),
    )
    return jax.shard_map(shards, mesh=mesh, in_specs=in_specs, out_specs=out_specs, check_vma=False)
```

time: 845 us -> 692 us (0.82)
  local copies, waits for them, and re-layouts: 126 us -> 48.6 us
  matrix products: 166 us -> 114 us
  waiting for transfers between devices: 362 us -> 310 us
  Pallas kernels: 0 us -> 39.2 us
  other arithmetic: 66.6 us -> 36.2 us
  starting transfers between devices: 99 us -> 119 us
    pallas_call x0 -> x4, Pallas kernels: none -> 39.2 us  [kernel_call(): pl.pallas_call(kernel, out_shape=outs, in_specs=[pl.BlockSpec(memory_spac...]
    ppermute x4, waiting for transfers between devices: 36.9 us -> 0.01 us  [one_way(): return lax.ppermute(values, axis, [(source, target)])]
    ppermute x30 -> x37, waiting for transfers between devices: 189 us -> 154 us  [swap(): return lax.ppermute(values, axis, [(0, 1), (1, 0)])]
    dot_general x16 -> x0, matrix products: 29.6 us -> none  [the longest x2 5.44 us: layer_backward(): jnp.einsum('qhd,khd->hqk', mixed_heads, value, preferred_element_type=F32)]
    slice x19 -> x12, local copies, waits for them, and re-layouts: 35.2 us -> 6.27 us  [the longest x4 4.58 us: both(): right[:, :wide]]
    dot_general x36 -> x23, matrix products: 136 us -> 114 us  [dot(): lax.dot_general(left, right, (((left_dim,), (right_dim,)), ((), ())), pre...]
    ppermute x30 -> x37, starting transfers between devices: 37.3 us -> 57.1 us  [swap(): return lax.ppermute(values, axis, [(0, 1), (1, 0)])]
    convert_element_type x10 -> x4, local copies, waits for them, and re-layouts: 15.9 us -> 2.07 us  [across(): total = keep + swap(send.astype(BF16), 'section').astype(F32)]
  transfers between devices with their start and end apart: 47 -> 57, of which waited for: 25 -> 26; matrix products, arithmetic and copies ran while one was open for 32% -> 23% of each run, Pallas kernels for 0% -> 5%
where the time goes in v2:
time: 692 us; the launch traced here: 682 us
  waiting for transfers between devices  310 us (45%)
  starting transfers between devices  119 us (17%)
  matrix products  114 us (16%)
  local copies, waits for them, and re-layouts  48.6 us (7%)
  Pallas kernels  39.2 us (6%)
  other arithmetic  36.2 us (5%)
  between operations  15.5 us (2%)
    ppermute x37, waiting for transfers between devices, swap(): return lax.ppermute(values, axis, [(0, 1), (1, 0)])  154 us
    dot_general x23, matrix products, dot(): lax.dot_general(left, right, (((left_dim,), (right_dim,)), ((), ())), pre...  114 us
    all_to_all x13, waiting for transfers between devices, all_to_all(): return lax.all_to_all(values, 'dp', split_axis=0, concat_axis=0, tiled=True)  110 us
    ppermute x37, starting transfers between devices, swap(): return lax.ppermute(values, axis, [(0, 1), (1, 0)])  57.1 us
    all_to_all x13, starting transfers between devices, all_to_all(): return lax.all_to_all(values, 'dp', split_axis=0, concat_axis=0, tiled=True)  53.6 us
    all_gather x2, waiting for transfers between devices, shards(): lax.all_gather(jnp.concatenate([beside[layer], beyond[layer]], axis=1), '...  45.5 us
    pallas_call x4, Pallas kernels, kernel_call(): pl.pallas_call(kernel, out_shape=outs, in_specs=[pl.BlockSpec(memory_spac...  39.2 us
    unnamed x188, local copies, waits for them, and re-layouts  33.4 us
  transfers between devices with their start and end apart: 57, of which 26 were waited for; matrix products, arithmetic and copies ran while one was open for 23% of the time, Pallas kernels for 5%

profile of v2, /device:TPU:0, one launch (start us, length us, event | category | flops | bytes accessed | tf_op | source)
XLA Modules:
  0.0 681.9 jit_solution(12584389325573986048)
XLA Ops:
  8.4 3.0 collective-permute-start.1
  12.9 6.3 collective-permute-done.1
  19.3 6.9 %collective-permute-done.2 = bf16[96,1536]{1,0:T(8,128)(2,1)S(1)} collective-permute-done((bf16[96,1536]{1,0:T(8,128)(2,1)S(1)}, bf16[96,1536]{1,0:T(8,128)(2,1)S(1)}, u32[]{:S(2)}, u32[]{:S(2)}) %collective-permute-start.2) | collective-permute-done | bytes 294944 | tf_op jit(solution)/shard_map/ppermute | solution.py:19
  33.8 45.5 %all-gather.3.cloned.1.call-done.w_ref = bf16[768,3072]{1,0:T(8,128)(2,1)} async-done(((bf16[96,3072]{1,0:T(8,128)(2,1)}), bf16[768,3072]{1,0:T(8,128)(2,1)}) %all-gather.3.cloned.1.call-update) | async-done | bytes 4718608 | tf_op jit(solution)/shard_map/all_gather | solution.py:350
  79.3 7.8 %shard_map.178 = (bf16[256,768]{1,0:T(8,128)(2,1)}, bf16[256,2304]{1,0:T(8,128)(2,1)S(1)}, f32[256,128]{1,0:T(8,128)S(1)}, bf16[256,768]{1,0:T(8,128)(2,1)S(1)},...) custom-call(bf16[256,768]{1,0:T(8,128)(2,1)S(1)} %maximum_select_fus, ...), custom_call_target="tpu_custom_call" | custom-call | flops 3000000000 | bytes 9775104 | tf_op jit(solution)/shard_map/pallas_call | solution.py:235
  88.7 4.2 all-to-all-start
  94.5 39.8 %all-to-all-done = bf16[8,64,768]{2,1,0:T(8,128)(2,1)} async-done(((bf16[8,64,768]{2,1,0:T(8,128)(2,1)}), bf16[8,64,768]{2,1,0:T(8,128)(2,1)}, u32[]{:S(2)}, u32[]{:S(2)}) %all-to-all-start) | async-done | bytes 786464 | tf_op jit(solution)/shard_map/all_to_all | solution.py:27
  135.8 18.2 %collective-permute-done.6 = bf16[512,768]{1,0:T(8,128)(2,1)S(1)} collective-permute-done((bf16[512,768]{1,0:T(8,128)(2,1)}, bf16[512,768]{1,0:T(8,128)(2,1)S(1)}, u32[]{:S(2)}, u32[]{:S(2)}) %collective-permute-start.6) | collective-permute-done | bytes 786464 | tf_op jit(solution)/shard_map/ppermute | solution.py:19
  154.0 4.7 fusion.49
  158.8 3.9 fusion.51
  164.2 17.1 %collective-permute-done.9 = bf16[512,768]{1,0:T(8,128)(2,1)S(1)} collective-permute-done((bf16[512,768]{1,0:T(8,128)(2,1)S(1)}, bf16[512,768]{1,0:T(8,128)(2,1)S(1)}, u32[]{:S(2)}, u32[]{:S(2)}) %collective-permute-start.9) | collective-permute-done | bytes 786464 | tf_op jit(solution)/shard_map/ppermute | solution.py:19
  182.4 4.0 all-to-all-start.1
  187.1 20.2 %all-to-all-done.1 = bf16[8,64,768]{2,1,0:T(8,128)(2,1)S(1)} async-done(((bf16[8,64,768]{2,1,0:T(8,128)(2,1)}), bf16[8,64,768]{2,1,0:T(8,128)(2,1)S(1)}, u32[]{:S(2)}, u32[]{:S(2)}) %all-to-all-start.1) | async-done | bytes 786464 | tf_op jit(solution)/shard_map/all_to_all | solution.py:27
  209.8 7.8 %shard_map.179 = (bf16[256,768]{1,0:T(8,128)(2,1)}, bf16[256,2304]{1,0:T(8,128)(2,1)S(1)}, f32[256,128]{1,0:T(8,128)S(1)}, bf16[256,768]{1,0:T(8,128)(2,1)S(1)},...) custom-call(bf16[256,768]{1,0:T(8,128)(2,1)S(1)} %get-tuple-element., ...), custom_call_target="tpu_custom_call" | custom-call | flops 3000000000 | bytes 9775104 | tf_op jit(solution)/shard_map/pallas_call | solution.py:235
  222.3 4.2 all-to-all-start.2
  229.1 5.7 collective-permute-done.15
  236.4 11.1 %all-to-all-done.2 = bf16[8,64,768]{2,1,0:T(8,128)(2,1)} async-done(((bf16[8,64,768]{2,1,0:T(8,128)(2,1)}), bf16[8,64,768]{2,1,0:T(8,128)(2,1)}, u32[]{:S(2)}, u32[]{:S(2)}) %all-to-all-start.2) | async-done | bytes 786464 | tf_op jit(solution)/shard_map/all_to_all | solution.py:27
  247.5 4.2 all-to-all-start.4
  253.3 19.4 %all-to-all-done.4 = bf16[8,64,768]{2,1,0:T(8,128)(2,1)} async-done(((bf16[8,64,768]{2,1,0:T(8,128)(2,1)}), bf16[8,64,768]{2,1,0:T(8,128)(2,1)}, u32[]{:S(2)}, u32[]{:S(2)}) %all-to-all-start.4) | async-done | bytes 786464 | tf_op jit(solution)/shard_map/all_to_all | solution.py:27
  274.2 4.9 fusion.53
  279.2 7.3 %fusion.55 = f32[1024,768]{1,0:T(8,128)S(1)} fusion(bf16[1536,768]{1,0:T(8,128)(2,1)} %collective-permute-done.8, pred[]{:T(512)S(6)} %eq.52, bf16[1,1,1536,768]{3,2,1,0:T(8,128)(2,1)S(1)} %copy-done.89, f32[1024,1536]{1,0:T(8,128)S(1)} %fusion.53), kind=kOutput, calls=%fused_computation.93 | convolution fusion | flops 2431254528 | bytes 14155777 | tf_op jit(solution)/shard_map/dot_general | solution.py:31
  287.3 6.1 collective-permute-done.16
  293.4 8.8 %fusion.13 = bf16[1024,1536]{1,0:T(8,128)(2,1)} fusion(f32[1024,1536]{1,0:T(8,128)S(1)} %fusion.53, bf16[1536,768]{1,0:T(8,128)(2,1)} %collective-permute-done.8, pred[]{:T(512)S(6)} %eq.52, bf16[1,1,1536,768]{3,2,1,0:T(8,128)(2,1)S(1)} %copy-done.89, bf16[512,768]{1,0:T(8,128)(2,1)S(1)} %collective-permute-done.16, bf16[512,768]{1,0:T(8,128)(2,1)} %bitcast.38), kind=kOutput, calls=%fused_computation.19 | convolution fusion | flops 2451701760 | bytes 15728641 | tf_op jit(solution)/shard_map/dot_general | solution.py:31
  302.2 6.7 collective-permute-done.12
  309.9 3.5 all-to-all-start.3
  313.4 6.0 fusion.52
  321.1 18.4 %collective-permute-done.17 = bf16[512,768]{1,0:T(8,128)(2,1)S(1)} collective-permute-done((bf16[512,768]{1,0:T(8,128)(2,1)S(1)}, bf16[512,768]{1,0:T(8,128)(2,1)S(1)}, u32[]{:S(2)}, u32[]{:S(2)}) %collective-permute-start.17) | collective-permute-done | bytes 786464 | tf_op jit(solution)/shard_map/ppermute | solution.py:19
  341.4 4.9 all-to-all-start.5
  357.9 9.4 %all-to-all-done.5 = bf16[8,64,768]{2,1,0:T(8,128)(2,1)S(1)} async-done(((bf16[8,64,768]{2,1,0:T(8,128)(2,1)}), bf16[8,64,768]{2,1,0:T(8,128)(2,1)S(1)}, u32[]{:S(2)}, u32[]{:S(2)}) %all-to-all-start.5) | async-done | bytes 786464 | tf_op jit(solution)/shard_map/all_to_all | solution.py:27
  378.3 11.8 %shard_map.180 = (bf16[256,768]{1,0:T(8,128)(2,1)S(1)}, bf16[256,2304]{1,0:T(8,128)(2,1)}, bf16[256,768]{1,0:T(8,128)(2,1)S(1)}, f32[2,768]{1,0:T(2,128)S(1)}, f32[128,768]{1,0:T(8,128)S(1)}) custom-call(bf16[512,768]{1,0:T(8,128)(2,1)S(1)} %bitcast.161, bf16[256,512]{1,0:T(8,128)(2,1)S(1)} %copy-done.11, bf16[256,768]{1,0:T(8,128)(2,1)S(1)} %maximum_select_fusion.6.dz_ref, ...), custom_call_target="tpu_custom_call" | custom-call | flops 5000000000 | bytes 12533760 | tf_op jit(solution)/shard_map/pallas_call | solution.py:235
  396.9 3.8 all-to-all-start.6
  403.9 6.7 collective-permute-done.32
  412.1 2.7 fusion.42
  416.0 4.5 collective-permute-start.33
  420.5 5.5 collective-permute-done.34
  428.5 4.5 collective-permute-start.36
  433.0 2.6 pad_maximum_fusion.1
  443.1 3.6 collective-permute-done.36
  446.7 3.2 collective-permute-start.39
  451.9 3.4 all-to-all-start.12
  457.9 2.8 fusion.28
  464.4 9.6 %fusion.6 = bf16[1024,1536]{1,0:T(8,128)(2,1)} fusion(f32[1024,1536]{1,0:T(8,128)} %copy-done.91, bf16[1536,768]{1,0:T(8,128)(2,1)} %collective-permute-done.8, pred[]{:T(512)S(6)} %eq.44, bf16[1,1,1536,768]{3,2,1,0:T(8,128)(2,1)S(1)} %copy-done.90, bf16[512,768]{1,0:T(8,128)(2,1)} %collective-permute-done.18, bf16[512,768]{1,0:T(8,128)(2,1)S(1)} %bitcast.172), kind=kOutput, calls=%fused_computation.12 | convolution fusion | flops 2451701760 | bytes 15728641 | tf_op jit(solution)/shard_map/dot_general | solution.py:31
  474.8 5.0 all-to-all-start.11
  479.8 5.4 fusion.48
  485.3 5.3 collective-permute-start.14
  491.1 6.1 fusion.72
  499.3 23.6 %collective-permute-done.14 = bf16[2,128,768]{2,1,0:T(8,128)(2,1)S(1)} collective-permute-done((bf16[2,128,768]{2,1,0:T(8,128)(2,1)S(1)}, bf16[2,128,768]{2,1,0:T(8,128)(2,1)S(1)}, u32[]{:S(2)}, u32[]{:S(2)}) %collective-permute-start.14) | collective-permute-done | bytes 393248 | tf_op jit(solution)/shard_map/ppermute | solution.py:19
  527.2 4.0 all-to-all-start.7
  533.1 13.5 %fusion.26 = f32[768,1536]{1,0:T(8,128)} fusion(f32[1024,1536]{1,0:T(8,128)} %fusion.72, bf16[1024,768]{1,0:T(8,128)(2,1)} %collective-permute-done.38, bf16[1024,768]{1,0:T(8,128)(2,1)} %collective-permute-done.39, pred[]{:T(512)S(6)} %eq.44, bf16[1024,768]{1,0:T(8,128)(2,1)} %collective-permute-done.40, bf16[1024,768]{1,0:T(8,128)(2,1)} %collective-permute-done.41, ...), kind=kOutput, calls=%fused_computation.37 | convolution fusion | flops 4864868352 | bytes 19660800 | tf_op jit(solution)/shard_map/dot_general | solution.py:31
  546.6 5.0 all-to-all-done.7
  559.7 11.9 %shard_map.181 = (bf16[256,768]{1,0:T(8,128)(2,1)S(1)}, bf16[256,2304]{1,0:T(8,128)(2,1)}, bf16[256,768]{1,0:T(8,128)(2,1)}, f32[2,768]{1,0:T(2,128)S(1)}, f32[128,768]{1,0:T(8,128)S(1)}) custom-call(bf16[512,768]{1,0:T(8,128)(2,1)S(1)} %bitcast.162, bf16[256,512]{1,0:T(8,128)(2,1)S(1)} %copy-done.10, bf16[256,768]{1,0:T(8,128)(2,1)S(1)} %get-tuple-element.47.dz_ref, ...), custom_call_target="tpu_custom_call" | custom-call | flops 5000000000 | bytes 12533760 | tf_op jit(solution)/shard_map/pallas_call | solution.py:235
  579.2 9.2 %fusion.23 = f32[1536,768]{1,0:T(8,128)} fusion(f32[1024,1536]{1,0:T(8,128)} %fusion.72, bf16[1024,768]{1,0:T(8,128)(2,1)} %collective-permute-done.40, bf16[1024,768]{1,0:T(8,128)(2,1)} %collective-permute-done.41, pred[]{:T(512)S(6)} %eq.44), kind=kOutput, calls=%fused_computation.34 | convolution fusion | flops 2430861312 | bytes 14155777 | tf_op jit(solution)/shard_map/dot_general | solution.py:31
  588.4 10.1 %collective-permute-done.24 = f32[10,768]{1,0:T(8,128)S(1)} collective-permute-done((f32[10,768]{1,0:T(8,128)S(1)}, f32[10,768]{1,0:T(8,128)S(1)}, u32[]{:S(2)}, u32[]{:S(2)}) %collective-permute-start.24) | collective-permute-done | bytes 30752 | tf_op jit(solution)/shard_map/ppermute | solution.py:19
  600.8 3.5 all-to-all-start.8
  606.5 2.7 fusion.38
  612.8 11.1 %add_bitcast_fusion = f32[1,1,1536,768]{3,2,1,0:T(8,128)} fusion(f32[1536,768]{1,0:T(8,128)S(1)} %copy-done.93, pred[]{:T(512)S(6)} %eq.44, bf16[512,768]{1,0:T(8,128)(2,1)} %collective-permute-done.18, bf16[512,768]{1,0:T(8,128)(2,1)S(1)} %bitcast.173, bf16[512,768]{1,0:T(8,128)(2,1)S(1)} %copy-done.65, bf16[512,768]{1,0:T(8,128)(2,1)} %bitcast.38, ...), kind=kOutput, calls=%fused_computation.30 | convolution fusion | flops 2454061056 | bytes 25165824 | tf_op jit(solution)/shard_map/dot_general | solution.py:31
  625.3 5.3 all-to-all-start.10
  630.6 3.8 collective-permute-done.27
  634.4 2.8 fusion.29
  637.3 3.8 all-to-all-done.10
  641.1 3.6 all-to-all-start.9
  644.7 8.9 %add_bitcast_fusion.1 = f32[1,1,768,1536]{3,2,1,0:T(8,128)} fusion(f32[768,1536]{1,0:T(8,128)} %fusion.26, bf16[1024,1536]{1,0:T(8,128)(2,1)} %fusion.6, bf16[1024,1536]{1,0:T(8,128)(2,1)} %fusion.13, pred[]{:T(512)S(6)} %eq.44, bf16[512,768]{1,0:T(8,128)(2,1)} %collective-permute-done.11, bf16[512,768]{1,0:T(8,128)(2,1)} %bitcast.27, ...), kind=kOutput, calls=%fused_computation.31 | convolution fusion | flops 2425749504 | bytes 18874368 | tf_op jit(solution)/shard_map/dot_general | solution.py:31
  655.4 9.8 %collective-permute-done.22 = bf16[2,128,768]{2,1,0:T(8,128)(2,1)S(1)} collective-permute-done((bf16[2,128,768]{2,1,0:T(8,128)(2,1)S(1)}, bf16[2,128,768]{2,1,0:T(8,128)(2,1)S(1)}, u32[]{:S(2)}, u32[]{:S(2)}) %collective-permute-start.22) | collective-permute-done | bytes 393248 | tf_op jit(solution)/shard_map/ppermute | solution.py:19
  668.3 5.0 collective-permute-done.37
  (352 shorter events, 132.3 us)
Async XLA Ops:
  7.2 72.1 %all-gather.3.cloned.1.call-start = ((), (), s32[]{:S(2)}) async-start(), calls=%async_computation.13 | async-start | bytes 5308416 | tf_op jit(solution)/shard_map/all_gather | solution.py:350
  8.4 10.8 %collective-permute-start.1 = (bf16[96,1536]{1,0:T(8,128)(2,1)S(1)}, bf16[96,1536]{1,0:T(8,128)(2,1)S(1)}, u32[]{:S(2)}, u32[]{:S(2)}) collective-permute-start(bf16[96,1536]{1,0:T(8,128)(2,1)S(1)} %bitcast.184), channel_id=1, source_target_pairs={{0,16},{16,0},{1,17},{17,1},{2,18},{18,2},{3,19},{19,3},{4,20},{20... | collective-permute-start | bytes 884744 | tf_op jit(solution)/shard_map/ppermute | solution.py:19
  11.4 14.8 %collective-permute-start.2 = (bf16[96,1536]{1,0:T(8,128)(2,1)S(1)}, bf16[96,1536]{1,0:T(8,128)(2,1)S(1)}, u32[]{:S(2)}, u32[]{:S(2)}) collective-permute-start(bf16[96,1536]{1,0:T(8,128)(2,1)S(1)} %bitcast.185), channel_id=1, source_target_pairs={{0,1},{1,0},{2,3},{3,2},{4,5},{5,4},{6,7},{7,6},{8,9},{9,8},{10,11... | collective-permute-start | bytes 884744 | tf_op jit(solution)/shard_map/ppermute | solution.py:19
  12.9 13.3 %collective-permute-start.3 = (bf16[96,1536]{1,0:T(8,128)(2,1)S(1)}, bf16[96,1536]{1,0:T(8,128)(2,1)S(1)}, u32[]{:S(2)}, u32[]{:S(2)}) collective-permute-start(bf16[96,1536]{1,0:T(8,128)(2,1)S(1)} %bitcast.186), channel_id=1, source_target_pairs={{0,17},{1,16},{16,1},{17,0},{2,19},{3,18},{18,3},{19,2},{4,21},{5,... | collective-permute-start | bytes 884744 | tf_op jit(solution)/shard_map/ppermute | solution.py:346
  27.1 182.7 %all-gather.5.cloned.1.call-start = ((), (), s32[]{:S(2)}) async-start(), calls=%async_computation.14 | async-start | bytes 5308416 | tf_op jit(solution)/shard_map/all_gather | solution.py:350
  27.3 6.5 collective-permute-start
  28.9 4.7 collective-permute-start.4
  29.5 3.7 collective-permute-start.5
  31.0 104.9 %collective-permute-start.7 = (bf16[768,1536]{1,0:T(8,128)(2,1)}, bf16[768,1536]{1,0:T(8,128)(2,1)}, u32[]{:S(2)}, u32[]{:S(2)}) collective-permute-start(bf16[768,1536]{1,0:T(8,128)(2,1)} %bitcast.204), channel_id=1, source_target_pairs={{0,16},{16,0},{1,17},{17,1},{2,18},{18,2},{3,19},{19,3},{4,20},{20... | collective-permute-start | bytes 7077896 | tf_op jit(solution)/shard_map/ppermute | solution.py:19
  32.7 177.1 %copy-start.30 = (s32[256]{0:T(256)}, s32[256]{0:T(256)S(1)}, u32[]{:S(2)}) copy-start(s32[256]{0:T(256)S(1)} %convert_reduce_fusion.4) | copy-start | bytes 3076
  32.8 177.0 %copy-start.16 = (s32[256,1]{1,0:T(8,128)}, s32[256,1]{1,0:T(8,128)S(1)}, u32[]{:S(2)}) copy-start(s32[256,1]{1,0:T(8,128)S(1)} %copy.40.seg_col_ref) | copy-start | bytes 3076
  33.4 174.8 %copy-start.76 = (s32[256]{0:T(256)}, s32[256]{0:T(256)S(1)}, u32[]{:S(2)}) copy-start(s32[256]{0:T(256)S(1)} %convert_add_fusion.1) | copy-start | bytes 3076
  88.7 70.0 %copy-start.37 = (bf16[256,768]{1,0:T(8,128)(2,1)}, bf16[256,768]{1,0:T(8,128)(2,1)S(1)}, u32[]{:S(2)}) copy-start(bf16[256,768]{1,0:T(8,128)(2,1)S(1)} %get-tuple-element.48.hn_ref) | copy-start | bytes 1179652
  88.7 70.0 %copy-start.43 = (f32[256,128]{1,0:T(8,128)}, f32[256,128]{1,0:T(8,128)S(1)}, u32[]{:S(2)}) copy-start(f32[256,128]{1,0:T(8,128)S(1)} %get-tuple-element.51.chances_ref) | copy-start | bytes 393220
  88.7 98.2 %copy-start.21 = (f32[256,1]{1,0:T(8,128)}, f32[256,1]{1,0:T(8,128)S(1)}, u32[]{:S(2)}) copy-start(f32[256,1]{1,0:T(8,128)S(1)} %get-tuple-element.38.gate_ref) | copy-start | bytes 3076
  88.7 45.6 %all-to-all-start = ((bf16[8,64,768]{2,1,0:T(8,128)(2,1)}), bf16[8,64,768]{2,1,0:T(8,128)(2,1)}, u32[]{:S(2)}, u32[]{:S(2)}) async-start(bf16[8,64,768]{2,1,0:T(8,128)(2,1)} %bitcast.16), calls=%async_computation | async-start | bytes 1572864 | tf_op jit(solution)/shard_map/all_to_all | solution.py:27
  93.0 65.8 %collective-permute-start.8 = (bf16[1536,768]{1,0:T(8,128)(2,1)}, bf16[1536,768]{1,0:T(8,128)(2,1)}, u32[]{:S(2)}, u32[]{:S(2)}) collective-permute-start(bf16[1536,768]{1,0:T(8,128)(2,1)} %bitcast.205), channel_id=1, source_target_pairs={{0,16},{16,0},{1,17},{17,1},{2,18},{18,2},{3,19},{19,3},{4,20},{20... | collective-permute-start | bytes 7077896 | tf_op jit(solution)/shard_map/ppermute | solution.py:19
  134.4 19.7 %collective-permute-start.6 = (bf16[512,768]{1,0:T(8,128)(2,1)}, bf16[512,768]{1,0:T(8,128)(2,1)S(1)}, u32[]{:S(2)}, u32[]{:S(2)}) collective-permute-start(bf16[512,768]{1,0:T(8,128)(2,1)} %bitcast.17), channel_id=1, source_target_pairs={{0,1},{1,0},{2,3},{3,2},{4,5},{5,4},{6,7},{7,6},{8,9},{9,8},{10,11... | collective-permute-start | bytes 2359304 | tf_op jit(solution)/shard_map/ppermute | solution.py:19
  162.7 18.7 %collective-permute-start.9 = (bf16[512,768]{1,0:T(8,128)(2,1)S(1)}, bf16[512,768]{1,0:T(8,128)(2,1)S(1)}, u32[]{:S(2)}, u32[]{:S(2)}) collective-permute-start(bf16[512,768]{1,0:T(8,128)(2,1)S(1)} %slice.165), channel_id=1, source_target_pairs={{0,1},{1,0},{2,3},{3,2},{4,5},{5,4},{6,7},{7,6},{8,9},{9,8},{10,11... | collective-permute-start | bytes 2359304 | tf_op jit(solution)/shard_map/ppermute | solution.py:19
  182.4 24.9 %all-to-all-start.1 = ((bf16[8,64,768]{2,1,0:T(8,128)(2,1)}), bf16[8,64,768]{2,1,0:T(8,128)(2,1)S(1)}, u32[]{:S(2)}, u32[]{:S(2)}) async-start(bf16[8,64,768]{2,1,0:T(8,128)(2,1)} %bitcast.20), calls=%async_computation.1 | async-start | bytes 1572864 | tf_op jit(solution)/shard_map/all_to_all | solution.py:27
  187.1 60.4 %copy-start.83 = (f32[256]{0:T(256)}, f32[256]{0:T(256)S(1)}, u32[]{:S(2)}) copy-start(f32[256]{0:T(256)S(1)} %reduce) | copy-start | bytes 3076
  222.3 25.2 %all-to-all-start.2 = ((bf16[8,64,768]{2,1,0:T(8,128)(2,1)}), bf16[8,64,768]{2,1,0:T(8,128)(2,1)}, u32[]{:S(2)}, u32[]{:S(2)}) async-start(bf16[8,64,768]{2,1,0:T(8,128)(2,1)} %bitcast.26), calls=%async_computation.2 | async-start | bytes 1572864 | tf_op jit(solution)/shard_map/all_to_all | solution.py:27
  227.6 7.2 %collective-permute-start.15 = (bf16[128,768]{1,0:T(8,128)(2,1)S(1)}, bf16[128,768]{1,0:T(8,128)(2,1)S(1)}, u32[]{:S(2)}, u32[]{:S(2)}) collective-permute-start(bf16[128,768]{1,0:T(8,128)(2,1)S(1)} %get-tuple-element.72), channel_id=1, source_target_pairs={{0,1},{1,0},{2,3},{3,2},{4,5},{5,4},{6,7},{7,6},{8,9},{9,8},{10,11... | collective-permute-start | bytes 589832 | tf_op jit(solution)/shard_map/ppermute | solution.py:19
  247.5 25.2 %all-to-all-start.4 = ((bf16[8,64,768]{2,1,0:T(8,128)(2,1)}), bf16[8,64,768]{2,1,0:T(8,128)(2,1)}, u32[]{:S(2)}, u32[]{:S(2)}) async-start(bf16[8,64,768]{2,1,0:T(8,128)(2,1)} %bitcast.169), calls=%async_computation.4 | async-start | bytes 1572864 | tf_op jit(solution)/shard_map/all_to_all | solution.py:27
  251.7 22.5 %collective-permute-start.11 = (bf16[512,768]{1,0:T(8,128)(2,1)}, bf16[512,768]{1,0:T(8,128)(2,1)}, u32[]{:S(2)}, u32[]{:S(2)}) collective-permute-start(bf16[512,768]{1,0:T(8,128)(2,1)} %bitcast.27), channel_id=1, source_target_pairs={{0,1},{1,0},{2,3},{3,2},{4,5},{5,4},{6,7},{7,6},{8,9},{9,8},{10,11... | collective-permute-start | bytes 2359304 | tf_op jit(solution)/shard_map/ppermute | solution.py:19
  272.7 20.7 %collective-permute-start.16 = (bf16[512,768]{1,0:T(8,128)(2,1)}, bf16[512,768]{1,0:T(8,128)(2,1)S(1)}, u32[]{:S(2)}, u32[]{:S(2)}) collective-permute-start(bf16[512,768]{1,0:T(8,128)(2,1)} %bitcast.38), channel_id=1, source_target_pairs={{0,1},{1,0},{2,3},{3,2},{4,5},{5,4},{6,7},{7,6},{8,9},{9,8},{10,11... | collective-permute-start | bytes 2359304 | tf_op jit(solution)/shard_map/ppermute | solution.py:19
  286.5 22.3 %collective-permute-start.12 = (bf16[512,768]{1,0:T(8,128)(2,1)S(1)}, bf16[512,768]{1,0:T(8,128)(2,1)S(1)}, u32[]{:S(2)}, u32[]{:S(2)}) collective-permute-start(bf16[512,768]{1,0:T(8,128)(2,1)S(1)} %slice.164), channel_id=1, source_target_pairs={{0,1},{1,0},{2,3},{3,2},{4,5},{5,4},{6,7},{7,6},{8,9},{9,8},{10,11... | collective-permute-start | bytes 2359304 | tf_op jit(solution)/shard_map/ppermute | solution.py:19
  309.9 30.6 %all-to-all-start.3 = ((bf16[8,64,768]{2,1,0:T(8,128)(2,1)}), bf16[8,64,768]{2,1,0:T(8,128)(2,1)S(1)}, u32[]{:S(2)}, u32[]{:S(2)}) async-start(bf16[8,64,768]{2,1,0:T(8,128)(2,1)} %bitcast.178), calls=%async_computation.3 | async-start | bytes 1572864 | tf_op jit(solution)/shard_map/all_to_all | solution.py:27
  319.5 19.9 %collective-permute-start.17 = (bf16[512,768]{1,0:T(8,128)(2,1)S(1)}, bf16[512,768]{1,0:T(8,128)(2,1)S(1)}, u32[]{:S(2)}, u32[]{:S(2)}) collective-permute-start(bf16[512,768]{1,0:T(8,128)(2,1)S(1)} %slice.163), channel_id=1, source_target_pairs={{0,1},{1,0},{2,3},{3,2},{4,5},{5,4},{6,7},{7,6},{8,9},{9,8},{10,11... | collective-permute-start | bytes 2359304 | tf_op jit(solution)/shard_map/ppermute | solution.py:19
  341.4 25.9 %all-to-all-start.5 = ((bf16[8,64,768]{2,1,0:T(8,128)(2,1)}), bf16[8,64,768]{2,1,0:T(8,128)(2,1)S(1)}, u32[]{:S(2)}, u32[]{:S(2)}) async-start(bf16[8,64,768]{2,1,0:T(8,128)(2,1)} %bitcast.175), calls=%async_computation.5 | async-start | bytes 1572864 | tf_op jit(solution)/shard_map/all_to_all | solution.py:27
  348.8 255.4 %collective-permute-start.29 = (bf16[256,384]{1,0:T(8,128)(2,1)}, bf16[256,384]{1,0:T(8,128)(2,1)}, u32[]{:S(2)}, u32[]{:S(2)}) collective-permute-start(bf16[256,384]{1,0:T(8,128)(2,1)} %get-tuple-element.86), channel_id=1, source_target_pairs={{0,1},{1,0},{2,3},{3,2},{4,5},{5,4},{6,7},{7,6},{8,9},{9,8},{10,11... | collective-permute-start | bytes 589832 | tf_op jit(solution)/shard_map/ppermute | solution.py:19
  353.7 84.3 %collective-permute-start.10 = (bf16[128,768]{1,0:T(8,128)(2,1)}, bf16[128,768]{1,0:T(8,128)(2,1)}, u32[]{:S(2)}, u32[]{:S(2)}) collective-permute-start(bf16[128,768]{1,0:T(8,128)(2,1)} %get-tuple-element.93), channel_id=1, source_target_pairs={{0,1},{1,0},{2,3},{3,2},{4,5},{5,4},{6,7},{7,6},{8,9},{9,8},{10,11... | collective-permute-start | bytes 589832 | tf_op jit(solution)/shard_map/ppermute | solution.py:19
  354.2 48.1 %collective-permute-start.31 = (bf16[256,768]{1,0:T(8,128)(2,1)}, bf16[256,768]{1,0:T(8,128)(2,1)}, u32[]{:S(2)}, u32[]{:S(2)}) collective-permute-start(bf16[256,768]{1,0:T(8,128)(2,1)} %get-tuple-element.61), channel_id=1, source_target_pairs={{0,1},{1,0},{2,3},{3,2},{4,5},{5,4},{6,7},{7,6},{8,9},{9,8},{10,11... | collective-permute-start | bytes 1179656 | tf_op jit(solution)/shard_map/ppermute | solution.py:19
  394.1 16.6 %collective-permute-start.32 = (bf16[256,1152]{1,0:T(8,128)(2,1)}, bf16[256,1152]{1,0:T(8,128)(2,1)}, u32[]{:S(2)}, u32[]{:S(2)}) collective-permute-start(bf16[256,1152]{1,0:T(8,128)(2,1)} %get-tuple-element.68), channel_id=1, source_target_pairs={{0,1},{1,0},{2,3},{3,2},{4,5},{5,4},{6,7},{7,6},{8,9},{9,8},{10,11... | collective-permute-start | bytes 1769480 | tf_op jit(solution)/shard_map/ppermute | solution.py:19
  396.9 42.4 %all-to-all-start.6 = ((bf16[8,64,768]{2,1,0:T(8,128)(2,1)}), bf16[8,64,768]{2,1,0:T(8,128)(2,1)S(1)}, u32[]{:S(2)}, u32[]{:S(2)}) async-start(bf16[8,64,768]{2,1,0:T(8,128)(2,1)} %bitcast.41), calls=%async_computation.6 | async-start | bytes 1572864 | tf_op jit(solution)/shard_map/all_to_all | solution.py:27
  400.7 15.3 %collective-permute-start.35 = (bf16[256,384]{1,0:T(8,128)(2,1)S(1)}, bf16[256,384]{1,0:T(8,128)(2,1)S(1)}, u32[]{:S(2)}, u32[]{:S(2)}) collective-permute-start(bf16[256,384]{1,0:T(8,128)(2,1)S(1)} %get-tuple-element.88), channel_id=1, source_target_pairs={{0,1},{1,0},{2,3},{3,2},{4,5},{5,4},{6,7},{7,6},{8,9},{9,8},{10,11... | collective-permute-start | bytes 589832 | tf_op jit(solution)/shard_map/ppermute | solution.py:19
  402.4 36.9 %collective-permute-start.13 = (bf16[128,768]{1,0:T(8,128)(2,1)S(1)}, bf16[128,768]{1,0:T(8,128)(2,1)}, u32[]{:S(2)}, u32[]{:S(2)}) collective-permute-start(bf16[128,768]{1,0:T(8,128)(2,1)S(1)} %get-tuple-element.95), channel_id=1, source_target_pairs={{0,1},{1,0},{2,3},{3,2},{4,5},{5,4},{6,7},{7,6},{8,9},{9,8},{10,11... | collective-permute-start | bytes 589832 | tf_op jit(solution)/shard_map/ppermute | solution.py:19
  410.6 15.4 %collective-permute-start.34 = (bf16[256,768]{1,0:T(8,128)(2,1)S(1)}, bf16[256,768]{1,0:T(8,128)(2,1)S(1)}, u32[]{:S(2)}, u32[]{:S(2)}) collective-permute-start(bf16[256,768]{1,0:T(8,128)(2,1)S(1)} %copy-done.34), channel_id=1, source_target_pairs={{0,1},{1,0},{2,3},{3,2},{4,5},{5,4},{6,7},{7,6},{8,9},{9,8},{10,11... | collective-permute-start | bytes 1179656 | tf_op jit(solution)/shard_map/ppermute | solution.py:19
  416.0 39.3 %collective-permute-start.33 = (bf16[8,48,1152]{2,1,0:T(8,128)(2,1)}, bf16[8,48,1152]{2,1,0:T(8,128)(2,1)}, u32[]{:S(2)}, u32[]{:S(2)}) collective-permute-start(bf16[8,48,1152]{2,1,0:T(8,128)(2,1)} %fusion.57), channel_id=1, source_target_pairs={{0,16},{16,0},{1,17},{17,1},{2,18},{18,2},{3,19},{19,3},{4,20},{20... | collective-permute-start | bytes 2654216 | tf_op jit(solution)/shard_map/ppermute | solution.py:19
  428.5 18.2 %collective-permute-start.36 = (bf16[8,48,384]{2,1,0:T(8,128)(2,1)}, bf16[8,48,384]{2,1,0:T(8,128)(2,1)}, u32[]{:S(2)}, u32[]{:S(2)}) collective-permute-start(bf16[8,48,384]{2,1,0:T(8,128)(2,1)} %fusion.91), channel_id=1, source_target_pairs={{0,16},{16,0},{1,17},{17,1},{2,18},{18,2},{3,19},{19,3},{4,20},{20... | collective-permute-start | bytes 884744 | tf_op jit(solution)/shard_map/ppermute | solution.py:19
  438.0 47.3 %collective-permute-start.38 = (bf16[1024,768]{1,0:T(8,128)(2,1)}, bf16[1024,768]{1,0:T(8,128)(2,1)}, u32[]{:S(2)}, u32[]{:S(2)}) collective-permute-start(bf16[1024,768]{1,0:T(8,128)(2,1)} %pad_maximum_fusion), channel_id=1, source_target_pairs={{16,0},{17,1},{18,2},{19,3},{20,4},{21,5},{22,6},{23,7},{24,8},{25... | collective-permute-start | bytes 4718600 | tf_op jit(solution)/shard_map/ppermute | solution.py:23
  439.3 21.4 %collective-permute-start.18 = (bf16[512,768]{1,0:T(8,128)(2,1)S(1)}, bf16[512,768]{1,0:T(8,128)(2,1)}, u32[]{:S(2)}, u32[]{:S(2)}) collective-permute-start(bf16[512,768]{1,0:T(8,128)(2,1)S(1)} %bitcast.170), channel_id=1, source_target_pairs={{0,1},{1,0},{2,3},{3,2},{4,5},{5,4},{6,7},{7,6},{8,9},{9,8},{10,11... | collective-permute-start | bytes 2359304 | tf_op jit(solution)/shard_map/ppermute | solution.py:19
  446.7 43.9 %collective-permute-start.39 = (bf16[1024,768]{1,0:T(8,128)(2,1)}, bf16[1024,768]{1,0:T(8,128)(2,1)}, u32[]{:S(2)}, u32[]{:S(2)}) collective-permute-start(bf16[1024,768]{1,0:T(8,128)(2,1)} %pad_maximum_fusion.1), channel_id=1, source_target_pairs={{0,16},{1,17},{2,18},{3,19},{4,20},{5,21},{6,22},{7,23},{8,24},{9,... | collective-permute-start | bytes 4718600 | tf_op jit(solution)/shard_map/ppermute | solution.py:23
  451.9 22.2 %all-to-all-start.12 = ((bf16[8,48,384]{2,1,0:T(8,128)(2,1)}), bf16[8,48,384]{2,1,0:T(8,128)(2,1)S(1)}, u32[]{:S(2)}, u32[]{:S(2)}) async-start(bf16[8,48,384]{2,1,0:T(8,128)(2,1)} %fusion.74), calls=%async_computation.12 | async-start | bytes 589824 | tf_op jit(solution)/shard_map/all_to_all | solution.py:27
  455.3 77.8 %collective-permute-start.41 = (bf16[1024,768]{1,0:T(8,128)(2,1)}, bf16[1024,768]{1,0:T(8,128)(2,1)}, u32[]{:S(2)}, u32[]{:S(2)}) collective-permute-start(bf16[1024,768]{1,0:T(8,128)(2,1)} %pad_maximum_fusion.2), channel_id=1, source_target_pairs={{0,16},{1,17},{2,18},{3,19},{4,20},{5,21},{6,22},{7,23},{8,24},{9,... | collective-permute-start | bytes 4718600 | tf_op jit(solution)/shard_map/ppermute | solution.py:23
  463.1 70.0 %collective-permute-start.40 = (bf16[1024,768]{1,0:T(8,128)(2,1)}, bf16[1024,768]{1,0:T(8,128)(2,1)}, u32[]{:S(2)}, u32[]{:S(2)}) collective-permute-start(bf16[1024,768]{1,0:T(8,128)(2,1)} %pad_maximum_fusion.3), channel_id=1, source_target_pairs={{16,0},{17,1},{18,2},{19,3},{20,4},{21,5},{22,6},{23,7},{24,8},{25... | collective-permute-start | bytes 4718600 | tf_op jit(solution)/shard_map/ppermute | solution.py:23
  474.8 51.5 %all-to-all-start.11 = ((bf16[8,48,1152]{2,1,0:T(8,128)(2,1)}), bf16[8,48,1152]{2,1,0:T(8,128)(2,1)S(1)}, u32[]{:S(2)}, u32[]{:S(2)}) async-start(bf16[8,48,1152]{2,1,0:T(8,128)(2,1)} %fusion.28), calls=%async_computation.11 | async-start | bytes 1769472 | tf_op jit(solution)/shard_map/all_to_all | solution.py:27
  485.3 37.6 %collective-permute-start.14 = (bf16[2,128,768]{2,1,0:T(8,128)(2,1)S(1)}, bf16[2,128,768]{2,1,0:T(8,128)(2,1)S(1)}, u32[]{:S(2)}, u32[]{:S(2)}) collective-permute-start(bf16[2,128,768]{2,1,0:T(8,128)(2,1)S(1)} %copy-done.70), channel_id=1, source_target_pairs={{0,16},{16,0},{1,17},{17,1},{2,18},{18,2},{3,19},{19,3},{4,20},{20... | collective-permute-start | bytes 1179656 | tf_op jit(solution)/shard_map/ppermute | solution.py:19
  490.6 34.6 %collective-permute-start.19 = (bf16[512,768]{1,0:T(8,128)(2,1)S(1)}, bf16[512,768]{1,0:T(8,128)(2,1)S(1)}, u32[]{:S(2)}, u32[]{:S(2)}) collective-permute-start(bf16[512,768]{1,0:T(8,128)(2,1)S(1)} %slice.162), channel_id=1, source_target_pairs={{0,1},{1,0},{2,3},{3,2},{4,5},{5,4},{6,7},{7,6},{8,9},{9,8},{10,11... | collective-permute-start | bytes 2359304 | tf_op jit(solution)/shard_map/ppermute | solution.py:19
  522.9 83.5 %collective-permute-start.25 = (bf16[256,768]{1,0:T(8,128)(2,1)}, bf16[256,768]{1,0:T(8,128)(2,1)}, u32[]{:S(2)}, u32[]{:S(2)}) collective-permute-start(bf16[256,768]{1,0:T(8,128)(2,1)} %get-tuple-element.57), channel_id=1, source_target_pairs={{0,1},{1,0},{2,3},{3,2},{4,5},{5,4},{6,7},{7,6},{8,9},{9,8},{10,11... | collective-permute-start | bytes 1179656 | tf_op jit(solution)/shard_map/ppermute | solution.py:19
  527.2 24.5 %all-to-all-start.7 = ((bf16[8,64,768]{2,1,0:T(8,128)(2,1)}), bf16[8,64,768]{2,1,0:T(8,128)(2,1)S(1)}, u32[]{:S(2)}, u32[]{:S(2)}) async-start(bf16[8,64,768]{2,1,0:T(8,128)(2,1)} %bitcast.177), calls=%async_computation.7 | async-start | bytes 1572864 | tf_op jit(solution)/shard_map/all_to_all | solution.py:27
  571.7 6.0 collective-permute-start.23
  574.2 30.0 %collective-permute-start.28 = (bf16[256,768]{1,0:T(8,128)(2,1)}, bf16[256,768]{1,0:T(8,128)(2,1)S(1)}, u32[]{:S(2)}, u32[]{:S(2)}) collective-permute-start(bf16[256,768]{1,0:T(8,128)(2,1)} %get-tuple-element.59), channel_id=1, source_target_pairs={{0,1},{1,0},{2,3},{3,2},{4,5},{5,4},{6,7},{7,6},{8,9},{9,8},{10,11... | collective-permute-start | bytes 1179656 | tf_op jit(solution)/shard_map/ppermute | solution.py:19
  577.0 29.4 %collective-permute-start.26 = (bf16[256,1152]{1,0:T(8,128)(2,1)S(1)}, bf16[256,1152]{1,0:T(8,128)(2,1)}, u32[]{:S(2)}, u32[]{:S(2)}) collective-permute-start(bf16[256,1152]{1,0:T(8,128)(2,1)S(1)} %get-tuple-element.66), channel_id=1, source_target_pairs={{0,1},{1,0},{2,3},{3,2},{4,5},{5,4},{6,7},{7,6},{8,9},{9,8},{10,11... | collective-permute-start | bytes 1769480 | tf_op jit(solution)/shard_map/ppermute | solution.py:19
  577.7 20.8 %collective-permute-start.24 = (f32[10,768]{1,0:T(8,128)S(1)}, f32[10,768]{1,0:T(8,128)S(1)}, u32[]{:S(2)}, u32[]{:S(2)}) collective-permute-start(f32[10,768]{1,0:T(8,128)S(1)} %fusion.99), channel_id=1, source_target_pairs={{0,1},{1,0},{2,3},{3,2},{4,5},{5,4},{6,7},{7,6},{8,9},{9,8},{10,11... | collective-permute-start | bytes 92168 | tf_op jit(solution)/shard_map/ppermute | solution.py:19
  598.5 55.0 %collective-permute-start.21 = (bf16[128,768]{1,0:T(8,128)(2,1)S(1)}, bf16[128,768]{1,0:T(8,128)(2,1)S(1)}, u32[]{:S(2)}, u32[]{:S(2)}) collective-permute-start(bf16[128,768]{1,0:T(8,128)(2,1)S(1)} %copy-done.74), channel_id=1, source_target_pairs={{0,1},{1,0},{2,3},{3,2},{4,5},{5,4},{6,7},{7,6},{8,9},{9,8},{10,11... | collective-permute-start | bytes 589832 | tf_op jit(solution)/shard_map/ppermute | solution.py:19
  600.8 24.5 %all-to-all-start.8 = ((f32[8,10,768]{2,1,0:T(8,128)}), f32[8,10,768]{2,1,0:T(8,128)S(1)}, u32[]{:S(2)}, u32[]{:S(2)}) async-start(f32[8,10,768]{2,1,0:T(8,128)} %broadcast_in_dim.27), calls=%async_computation.8 | async-start | bytes 786432 | tf_op jit(solution)/shard_map/all_to_all | solution.py:27
  606.0 18.5 %collective-permute-start.30 = (bf16[8,48,384]{2,1,0:T(8,128)(2,1)S(1)}, bf16[8,48,384]{2,1,0:T(8,128)(2,1)S(1)}, u32[]{:S(2)}, u32[]{:S(2)}) collective-permute-start(bf16[8,48,384]{2,1,0:T(8,128)(2,1)S(1)} %fusion.90), channel_id=1, source_target_pairs={{0,16},{16,0},{1,17},{17,1},{2,18},{18,2},{3,19},{19,3},{4,20},{20... | collective-permute-start | bytes 884744 | tf_op jit(solution)/shard_map/ppermute | solution.py:19
  611.0 23.4 %collective-permute-start.27 = (bf16[8,48,1152]{2,1,0:T(8,128)(2,1)S(1)}, bf16[8,48,1152]{2,1,0:T(8,128)(2,1)}, u32[]{:S(2)}, u32[]{:S(2)}) collective-permute-start(bf16[8,48,1152]{2,1,0:T(8,128)(2,1)S(1)} %fusion.56), channel_id=1, source_target_pairs={{0,16},{16,0},{1,17},{17,1},{2,18},{18,2},{3,19},{19,3},{4,20},{20... | collective-permute-start | bytes 2654216 | tf_op jit(solution)/shard_map/ppermute | solution.py:19
  623.9 29.7 %collective-permute-start.20 = (bf16[128,768]{1,0:T(8,128)(2,1)S(1)}, bf16[128,768]{1,0:T(8,128)(2,1)S(1)}, u32[]{:S(2)}, u32[]{:S(2)}) collective-permute-start(bf16[128,768]{1,0:T(8,128)(2,1)S(1)} %get-tuple-element.89), channel_id=1, source_target_pairs={{0,1},{1,0},{2,3},{3,2},{4,5},{5,4},{6,7},{7,6},{8,9},{9,8},{10,11... | collective-permute-start | bytes 589832 | tf_op jit(solution)/shard_map/ppermute | solution.py:19
  625.3 15.8 %all-to-all-start.10 = ((bf16[8,48,384]{2,1,0:T(8,128)(2,1)}), bf16[8,48,384]{2,1,0:T(8,128)(2,1)S(1)}, u32[]{:S(2)}, u32[]{:S(2)}) async-start(bf16[8,48,384]{2,1,0:T(8,128)(2,1)} %fusion.75), calls=%async_computation.10 | async-start | bytes 589824 | tf_op jit(solution)/shard_map/all_to_all | solution.py:27
  641.1 26.6 %all-to-all-start.9 = ((bf16[8,48,1152]{2,1,0:T(8,128)(2,1)}), bf16[8,48,1152]{2,1,0:T(8,128)(2,1)S(1)}, u32[]{:S(2)}, u32[]{:S(2)}) async-start(bf16[8,48,1152]{2,1,0:T(8,128)(2,1)} %fusion.29), calls=%async_computation.9 | async-start | bytes 1769472 | tf_op jit(solution)/shard_map/all_to_all | solution.py:27
  653.7 11.5 %collective-permute-start.22 = (bf16[2,128,768]{2,1,0:T(8,128)(2,1)S(1)}, bf16[2,128,768]{2,1,0:T(8,128)(2,1)S(1)}, u32[]{:S(2)}, u32[]{:S(2)}) collective-permute-start(bf16[2,128,768]{2,1,0:T(8,128)(2,1)S(1)} %get-tuple-element.70), channel_id=1, source_target_pairs={{0,16},{16,0},{1,17},{17,1},{2,18},{18,2},{3,19},{19,3},{4,20},{20... | collective-permute-start | bytes 1179656 | tf_op jit(solution)/shard_map/ppermute | solution.py:19
  667.8 5.5 collective-permute-start.37
  (87 other events, 1088.9 us)
Sparse Core Ops, SparseCore 0:
  27.3 52.0 all-gather.2
  81.5 67.0 all-gather.4

commit v3 on v2

v3 whole, which is shorter than its diff:
```python
import functools
import math

import jax
import jax.numpy as jnp
from jax import lax
from jax.experimental import pallas as pl
from jax.experimental.pallas import tpu as pltpu
from jax.sharding import PartitionSpec as P

HD = 64
LANES = 128
EPSILON = 1e-06
NEGATIVE = -1e30
F32 = jnp.float32
BF16 = jnp.bfloat16
CUBIC = 0.044715
SLOPE = math.sqrt(2.0 / math.pi)


def swap(values, axis):
    return lax.ppermute(values, axis, [(0, 1), (1, 0)])


def one_way(values, axis, source, target):
    return lax.ppermute(values, axis, [(source, target)])


def all_to_all(values):
    return lax.all_to_all(values, "dp", split_axis=0, concat_axis=0, tiled=True)


def after(value, *anchors):
    return lax.optimization_barrier((value, anchors))[0]


def dot(left, right, left_dim, right_dim):
    return lax.dot_general(
        left, right, (((left_dim,), (right_dim,)), ((), ())), preferred_element_type=F32
    )


def ordered(index, own, other):
    return jnp.where(
        index == 0, jnp.concatenate([own, other], axis=0), jnp.concatenate([other, own], axis=0)
    )


def entry(array, index):
    return lax.dynamic_index_in_dim(array, index, 0, keepdims=False)


def norm_forward(inputs, gain):
    scaling = lax.rsqrt(jnp.mean(inputs * inputs, axis=-1, keepdims=True) + EPSILON)
    return inputs * scaling * gain


def norm_back(upstream, inputs, gain):
    scaling = lax.rsqrt(jnp.mean(inputs * inputs, axis=-1, keepdims=True) + EPSILON)
    weighted = upstream * gain
    scaled = inputs * scaling
    inner = jnp.mean(weighted * inputs, axis=-1, keepdims=True)
    return (
        scaling * weighted - scaled * (scaling * scaling * inner),
        jnp.sum(upstream * scaled, axis=0, keepdims=True),
    )


def smooth_gate(values):
    return jax.nn.gelu(values, approximate=True)


def routing(route_row, experts):
    count = route_row.shape[0]
    capacity = 2 * count // experts
    hot = route_row[:, None] == jnp.arange(experts, dtype=jnp.int32)[None, :]
    places = jnp.arange(count, dtype=jnp.int32)
    earlier = (places[:, None] > places[None, :]).astype(BF16)
    ranks = dot(earlier, hot.astype(BF16), 1, 0)
    ranking = jnp.sum(ranks * hot.astype(F32), axis=1).astype(jnp.int32)
    slots = route_row * capacity + ranking
    places = jnp.arange(experts * capacity, dtype=jnp.int32)
    return (
        (slots[None, :] == places[:, None]).astype(BF16),
        (slots[:, None] == places[None, :]).astype(BF16),
    )


def head_lanes(count):
    return lax.broadcasted_iota(jnp.int32, (count, LANES), 1) // HD


def attention_bias(seg_col, seg_row, count):
    rows = lax.broadcasted_iota(jnp.int32, (count, count), 0)
    cols = lax.broadcasted_iota(jnp.int32, (count, count), 1)
    return jnp.where((seg_col == seg_row) & (rows >= cols), 0.0, NEGATIVE)


def expert_chances(rows, router, experts):
    logits = dot(rows, router, 1, 1)
    lane = lax.broadcasted_iota(jnp.int32, logits.shape, 1)
    logits = jnp.where(lane < experts, logits, NEGATIVE)
    raised = jnp.exp(logits - jnp.max(logits, axis=-1, keepdims=True))
    return raised * (1.0 / jnp.sum(raised, axis=-1, keepdims=True))


def forward_kernel(get, outs, *, experts, joined):
    (xn_ref, qkv_ref, lse_ref, o_ref, h_ref, gate_ref, out_ref) = outs[:7]
    if joined:
        mixed_in = dot(get("taking")[...], get("back")[...], 1, 0)
        result = (get("h_before")[...] + get("gate_before")[...] * mixed_in).astype(BF16)
        outs[7][...] = result
        a = result.astype(F32)
    else:
        a = get("a")[...].astype(F32)
    count, width = a.shape
    part = width // 2
    pairs = part // LANES
    gains = get("gains")
    xn = norm_forward(a, gains[0:1, :]).astype(BF16)
    xn_ref[...] = xn
    bias = attention_bias(get("seg_col")[...], get("seg_row")[...], count)
    lanes = head_lanes(count)
    scale = 1.0 / math.sqrt(HD)
    w_ref = get("weights")
    for half in range(2):
        base = half * 3 * part
        qkv_ref[:, base:base + 3 * part] = dot(
            xn, w_ref[:, half * 4 * part:half * 4 * part + 3 * part], 1, 0
        ).astype(BF16)
    attended = a
    lse = jnp.zeros((count, LANES), F32)
    for half in range(2):
        base = half * 3 * part
        for pair in range(pairs):
            at = base + pair * LANES
            query = qkv_ref[:, at:at + LANES]
            key = qkv_ref[:, at + part:at + part + LANES]
            value = qkv_ref[:, at + 2 * part:at + 2 * part + LANES]
            mixed = None
            for head in range(2):
                own = jnp.where(lanes == head, query, jnp.zeros_like(query))
                scores = dot(own, key, 1, 1) * scale + bias
                top = jnp.max(scores, axis=-1, keepdims=True)
                weight = jnp.exp(scores - top)
                total = jnp.sum(weight, axis=-1, keepdims=True)
                probs = (weight * (1.0 / total)).astype(BF16)
                number = (half * pairs + pair) * 2 + head
                lse = jnp.where(
                    lax.broadcasted_iota(jnp.int32, lse.shape, 1) == number,
                    top + jnp.log(total), lse,
                )
                part_out = dot(probs, value, 1, 0)
                mixed = part_out if head == 0 else jnp.where(lanes == 0, mixed, part_out)
            o_at = half * part + pair * LANES
            o_ref[:, o_at:o_at + LANES] = mixed.astype(BF16)
        attended = attended + dot(
            o_ref[:, half * part:(half + 1) * part],
            w_ref[:, half * 4 * part + 3 * part:(half + 1) * 4 * part], 1, 1,
        )
    lse_ref[...] = lse
    h_ref[...] = attended
    hn = norm_forward(attended, gains[1:2, :]).astype(BF16)
    out_ref[...] = dot(get("placing")[...], hn, 1, 0).astype(BF16)
    chances = expert_chances(hn, get("router")[...], experts)
    lane = lax.broadcasted_iota(jnp.int32, chances.shape, 1)
    gate_ref[...] = jnp.sum(
        jnp.where(lane == get("route")[...], chances, 0.0), axis=-1, keepdims=True
    )


def backward_kernel(get, outs, *, spread):
    (da_ref, dqkv_ref, dattn_ref, small_ref) = outs[:4]
    hn_grad = dot(get("taking")[...], get("back")[...], 1, 0)
    gains = get("gains")
    dz = get("dz")[...].astype(F32)
    hidden = get("h")[...]
    count, width = hidden.shape
    part = width // 2
    pairs = part // LANES
    hidden_part, gain_f_grad = norm_back(hn_grad, hidden, gains[1:2, :])
    hidden_grad = dz + hidden_part
    attended_grad = hidden_grad.astype(BF16)
    dattn_ref[...] = attended_grad
    bias = attention_bias(get("seg_col")[...], get("seg_row")[...], count)
    lanes = head_lanes(count)
    scale = 1.0 / math.sqrt(HD)
    qkv_ref, lse_ref, w_ref = (get("qkv"), get("lse"), get("weights"))
    normed_grad = jnp.zeros((count, width), F32)
    for half in range(2):
        base = half * 3 * part
        mixed_grad = dot(
            attended_grad, w_ref[:, half * 4 * part + 3 * part:(half + 1) * 4 * part], 1, 0
        ).astype(BF16)
        for pair in range(pairs):
            at = base + pair * LANES
            query = qkv_ref[:, at:at + LANES]
            key = qkv_ref[:, at + part:at + part + LANES]
            value = qkv_ref[:, at + 2 * part:at + 2 * part + LANES]
            grad = mixed_grad[:, pair * LANES:(pair + 1) * LANES]
            dq = dk = dv = None
            for head in range(2):
                number = (half * pairs + pair) * 2 + head
                zero = jnp.zeros_like(query)
                own_q = jnp.where(lanes == head, query, zero)
                own_g = jnp.where(lanes == head, grad, zero)
                scores = dot(own_q, key, 1, 1) * scale + bias
                probs = jnp.exp(scores - lse_ref[:, number:number + 1])
                prob_grad = dot(own_g, value, 1, 1)
                inner = jnp.sum(probs * prob_grad, axis=-1, keepdims=True)
                score_grad = (probs * (prob_grad - inner)).astype(BF16)
                head_dv = dot(probs.astype(BF16), own_g, 0, 0)
                head_dk = dot(score_grad, own_q, 0, 0)
                head_dq = dot(score_grad, key, 1, 0)
                if head == 0:
                    dq, dk, dv = (head_dq, head_dk, head_dv)
                else:
                    dq = jnp.where(lanes == 0, dq, head_dq)
                    dk = dk + head_dk
                    dv = dv + head_dv
            dqkv_ref[:, at:at + LANES] = (dq * scale).astype(BF16)
            dqkv_ref[:, at + part:at + part + LANES] = (dk * scale).astype(BF16)
            dqkv_ref[:, at + 2 * part:at + 2 * part + LANES] = dv.astype(BF16)
        normed_grad = normed_grad + dot(
            dqkv_ref[:, base:base + 3 * part],
            w_ref[:, half * 4 * part:half * 4 * part + 3 * part], 1, 1,
        )
    input_part, gain_a_grad = norm_back(normed_grad, get("a")[...].astype(F32), gains[0:1, :])
    small_ref[0:1, :] = gain_a_grad
    small_ref[1:2, :] = gain_f_grad
    input_grad = (hidden_grad + input_part).astype(BF16)
    da_ref[...] = input_grad
    if spread:
        outs[4][...] = dot(get("placing")[...], input_grad, 1, 0).astype(BF16)


def staged_call(kernel, inputs, outs, flops):
    names = list(inputs)
    args = [inputs[name] for name in names]
    count = len(args)

    def body(*refs):
        sources, targets = (refs[:count], refs[count:count + len(outs)])
        held, marks = (refs[count + len(outs):-1], refs[-1])
        copies = [
            pltpu.make_async_copy(sources[i], held[i], marks.at[i]) for i in range(count)
        ]
        for copy in copies:
            copy.start()
        ready = set()

        def get(name):
            number = names.index(name)
            if number not in ready:
                ready.add(number)
                copies[number].wait()
            return held[number]

        kernel(get, targets)

    moved = sum(math.prod(v.shape) * v.dtype.itemsize for v in (*args, *outs))
    return pl.pallas_call(
        body,
        out_shape=outs,
        in_specs=[pl.BlockSpec(memory_space=pl.ANY)] * count,
        out_specs=[pl.BlockSpec(memory_space=pltpu.VMEM)] * len(outs),
        scratch_shapes=[pltpu.VMEM(v.shape, v.dtype) for v in args]
        + [pltpu.SemaphoreType.DMA((count,))],
        compiler_params=pltpu.CompilerParams(vmem_limit_bytes=40 * 1024 * 1024),
        cost_estimate=pl.CostEstimate(flops=flops, bytes_accessed=moved, transcendentals=0),
    )(*args)


def layer_start(source, params, segments, route_col, placing):
    gains, weights, router_w, experts = params
    joined = "back" in source
    struct = jax.ShapeDtypeStruct
    count = route_col.shape[0]
    width = weights.shape[0]
    outs = [
        struct((count, width), BF16),
        struct((count, 3 * width), BF16),
        struct((count, LANES), F32),
        struct((count, width), BF16),
        struct((count, width), F32),
        struct((count, 1), F32),
        struct((placing.shape[0], width), BF16),
    ]
    if joined:
        outs.append(struct((count, width), BF16))
    inputs = dict(
        source, gains=gains, seg_col=segments[0], seg_row=segments[1], weights=weights,
        placing=placing, router=router_w, route=route_col,
    )
    return staged_call(
        functools.partial(forward_kernel, experts=experts, joined=joined), inputs, outs, 3 * 10**9
    )


def layer_end(back, taking, upstream, inputs, state, params, segments, placing):
    gains, weights = params[:2]
    count, width = inputs.shape
    struct = jax.ShapeDtypeStruct
    outs = [
        struct((count, width), BF16),
        struct((count, 3 * width), BF16),
        struct((count, width), BF16),
        struct((2, width), F32),
    ]
    given = dict(
        taking=taking, back=back, gains=gains, dz=upstream, h=state["h"], seg_col=segments[0],
        seg_row=segments[1], weights=weights, qkv=state["qkv"], lse=state["lse"], a=inputs,
    )
    if placing is not None:
        given["placing"] = placing
        outs.append(struct((placing.shape[0], width), BF16))
    return staged_call(
        functools.partial(backward_kernel, spread=placing is not None), given, outs, 5 * 10**9
    )


def split_dot(left, right, left_dim, right_dim):
    high = left.astype(BF16)
    low = (left - high.astype(F32)).astype(BF16)
    return dot(high, right, left_dim, right_dim) + dot(low, right, left_dim, right_dim)


def expert_kernel(
    rows_ref, dz_ref, in_ref, out_ref, router_ref, hot_ref,
    dx_ref, act_ref, dpre_ref, dy_ref, g_router_ref, chance_ref, gate_ref, total_ref, *, experts,
):
    step = pl.program_id(0)
    rows = rows_ref[...]

    @pl.when(step == 0)
    def _():
        chances = expert_chances(rows, router_ref[...], experts)
        chance_ref[...] = chances
        gate = jnp.sum(chances * hot_ref[...], axis=-1, keepdims=True)
        dy_ref[...] = (gate * dz_ref[...].astype(F32)).astype(BF16)
        gate_ref[...] = jnp.zeros_like(gate_ref)
        total_ref[...] = jnp.zeros_like(total_ref)

    before = dot(rows, in_ref[...], 1, 0)
    square = before * before
    bent = jnp.tanh(SLOPE * before * (1.0 + CUBIC * square))
    lifted = 0.5 * (1.0 + bent)
    act = (before * lifted).astype(BF16)
    slope = lifted + 0.5 * before * (1.0 - bent * bent) * (
        SLOPE * (1.0 + 3.0 * CUBIC * square)
    )
    act_grad = dot(dy_ref[...], out_ref[...], 1, 1)
    dpre = (act_grad * slope).astype(BF16)
    act_ref[...] = act
    dpre_ref[...] = dpre
    gate_ref[...] += jnp.sum(act_grad * act.astype(F32), axis=-1, keepdims=True)
    total_ref[...] += dot(dpre, in_ref[...], 1, 1)

    @pl.when(step == pl.num_programs(0) - 1)
    def _():
        logit_grad = (hot_ref[...] - chance_ref[...]) * gate_ref[...]
        g_router_ref[...] = split_dot(logit_grad, rows, 0, 0)
        dx_ref[...] = (total_ref[...] + split_dot(logit_grad, router_ref[...], 1, 0)).astype(
            dx_ref.dtype
        )


def expert_back(rows, dz, in_w, expert_w, router_w, hot_row, experts, kind):
    count, width = rows.shape
    hidden = in_w.shape[1]
    block = 512
    struct = jax.ShapeDtypeStruct
    whole = pl.BlockSpec((count, width), lambda j: (0, 0))
    wide = pl.BlockSpec((count, block), lambda j: (0, j))
    router_spec = pl.BlockSpec((LANES, width), lambda j: (0, 0))
    return pl.pallas_call(
        functools.partial(expert_kernel, experts=experts),
        grid=(hidden // block,),
        out_shape=[
            struct((count, width), kind),
            struct((count, hidden), BF16),
            struct((count, hidden), BF16),
            struct((count, width), BF16),
            struct((LANES, width), F32),
        ],
        in_specs=[
            whole,
            whole,
            pl.BlockSpec((width, block), lambda j: (0, j)),
            pl.BlockSpec((block, width), lambda j: (j, 0)),
            router_spec,
            pl.BlockSpec((1, LANES), lambda j: (0, 0)),
        ],
        out_specs=[whole, wide, wide, whole, router_spec],
        scratch_shapes=[
            pltpu.VMEM((count, LANES), F32),
            pltpu.VMEM((count, 1), F32),
            pltpu.VMEM((count, width), F32),
        ],
        compiler_params=pltpu.CompilerParams(
            dimension_semantics=("arbitrary",), vmem_limit_bytes=40 * 1024 * 1024
        ),
        cost_estimate=pl.CostEstimate(
            flops=6 * count * width * hidden, bytes_accessed=12 * 10**6, transcendentals=0
        ),
    )(rows, dz, in_w, expert_w, router_w, hot_row)


def exchange_across(grad, section):
    width = grad.shape[0]
    count = lax.axis_size("dp")
    halves = grad.reshape(count, 2, width // count // 2, -1)
    keep = lax.dynamic_index_in_dim(halves, section, 1, keepdims=False)
    send = lax.dynamic_index_in_dim(halves, 1 - section, 1, keepdims=False)
    return (keep + swap(send.astype(BF16), "section").astype(F32)).astype(BF16)


def pair_up(values, tensor):
    half = values.shape[0] // 2
    halves = values.reshape(2, half, -1)
    own = entry(halves, tensor)
    other = swap(entry(halves, 1 - tensor), "tensor")
    return ordered(tensor, own[None], other[None])


def by_section(pairs, section):
    first, second = pairs
    own = jnp.where(section == 0, first, second)
    other = swap(jnp.where(section == 0, second, first), "section")
    return ordered(section, own, other)


def gelu_pair(before, active_grad):
    activated, back = jax.vjp(smooth_gate, before)
    return (activated.astype(BF16), back(active_grad)[0].astype(BF16))


def shards(
    x_in, d_out, lengths, routes, gain_attn, w_qkv, w_attn_out, gain_ffn, w_router, w_in, w_exp_out
):
    section = lax.axis_index("section")
    tensor = lax.axis_index("tensor")
    count = lax.axis_size("dp")
    width = x_in.shape[2]
    part = width // 2
    rows = 2 * x_in.shape[1]
    experts = w_router.shape[2]
    own_batch = 2 * section + tensor
    peer_batch = 2 * section + 1 - tensor

    def of_layer(layer, own, other):
        return jnp.where(section == layer, own, other)

    def by_layer(own):
        other = swap(own, "section")
        return [of_layer(layer, own, other) for layer in range(2)]

    def whole_group(array):
        return ordered(
            tensor, entry(array, own_batch), swap(entry(array, peer_batch), "tensor")
        )

    packed = jnp.concatenate([w_qkv[0], w_attn_out[0].T[None]], axis=0)
    packed = jnp.moveaxis(packed, 0, 1).reshape(width // count, -1)
    small = by_layer(jnp.concatenate([gain_attn, gain_ffn, w_router[0].T], axis=0))
    own_route = entry(routes[0, :, :, 0], own_batch)
    other_route = swap(entry(routes[0, :, :, 0], 2 * (1 - section) + tensor), "section")
    route = [of_layer(layer, own_route, other_route) for layer in range(2)]
    first_pack = of_layer(0, packed, one_way(packed, "section", 0, 1))
    first_beside = swap(first_pack, "tensor")
    first_w = lax.all_gather(
        jnp.concatenate([first_pack, first_beside], axis=1), "dp", axis=0, tiled=True
    )
    x_own = whole_group(x_in)
    own_in, own_out, later_pack, d_last = after(
        (w_in[0, 0], w_exp_out[0, 0], packed, d_out), first_beside
    )
    second_pack = of_layer(1, packed, one_way(later_pack, "section", 1, 0))
    second_pack = jnp.concatenate([second_pack, swap(second_pack, "tensor")], axis=1)
    dz_last = whole_group(d_last)
    in_w = by_layer(own_in)
    expert_w = by_layer(own_out)

    tables = [routing(row, experts) for row in route]
    placing = [table[0] for table in tables]
    taking = [table[1] for table in tables]
    route_col = [row[:, None] for row in route]
    gains = [small[layer][:2].astype(F32) for layer in range(2)]
    router_w = [jnp.pad(small[layer][2:], ((0, LANES - experts), (0, 0))) for layer in range(2)]
    bounds = jnp.cumsum(entry(lengths[:, 0], own_batch))
    places = jnp.arange(rows, dtype=jnp.int32)
    segment = jnp.sum((places[:, None] >= bounds[None, :]).astype(jnp.int32), axis=1)
    segments = (segment[:, None], segment[None, :])
    hot_row = (
        jnp.arange(LANES, dtype=jnp.int32)[None, :] == lax.axis_index("dp")
    ).astype(F32)
    keys = ("xn", "qkv", "lse", "o", "h", "gate")

    def expert_forward(values, layer):
        active = smooth_gate(dot(values, in_w[layer], 1, 0)).astype(BF16)
        return dot(active, expert_w[layer], 1, 0)

    def fold(own, peer):
        return (own + swap(peer.astype(BF16), "tensor").astype(F32)).astype(BF16)

    params0 = (gains[0], first_w, router_w[0], experts)
    *state0, outgoing0 = layer_start(
        {"a": x_own}, params0, segments, route_col[0], placing[0]
    )
    state0 = dict(zip(keys, state0))
    mine0 = all_to_all(outgoing0)
    side_xn0 = swap(state0["xn"], "tensor")
    side_o0 = swap(state0["o"][:, part:], "tensor")
    peer0 = swap(after(mine0, side_xn0, side_o0), "tensor")
    second_w = lax.all_gather(after(second_pack, mine0), "dp", axis=0, tiled=True)
    back0 = all_to_all(fold(expert_forward(mine0, 0), expert_forward(peer0, 0)))

    dz_out1 = dot(placing[1], dz_last, 1, 0).astype(BF16)
    mine_dz1 = all_to_all(after(dz_out1, back0))
    params1 = (gains[1], second_w, router_w[1], experts)
    *state1, outgoing1, out0 = layer_start(
        {"taking": taking[0], "back": back0, "h_before": state0["h"],
         "gate_before": state0["gate"]},
        params1, segments, route_col[1], placing[1],
    )
    state1 = dict(zip(keys, state1))
    side_xn1 = swap(state1["xn"], "tensor")
    side_o1 = swap(state1["o"][:, part:], "tensor")
    peer_dz1 = swap(after(mine_dz1, side_xn1, side_o1), "tensor")
    mine1 = all_to_all(after(outgoing1, mine_dz1))
    peer1 = swap(after(mine1, peer_dz1), "tensor")

    def both_back(layer, mine, peer, mine_dz, peer_dz):
        args = (in_w[layer], expert_w[layer], router_w[layer], hot_row, experts)
        return (
            expert_back(mine, mine_dz, *args, F32),
            expert_back(peer, peer_dz, *args, BF16),
        )

    own_b1, peer_b1 = both_back(1, mine1, peer1, mine_dz1, peer_dz1)
    peer_dx1 = swap(peer_b1[0], "tensor")
    dback1 = all_to_all((own_b1[0] + peer_dx1.astype(F32)).astype(BF16))
    late_mine1, late_peer1 = after((mine1, peer1), peer_b1[0])
    own_y1 = expert_forward(late_mine1, 1)
    peer_y1 = expert_forward(late_peer1, 1)
    total_y1 = fold(own_y1, after(peer_y1.astype(BF16), peer_dx1))
    grad1, dqkv1, dattn1, gains1, outgoing_dz0 = layer_end(
        dback1, taking[1], dz_last, out0, state1, params1, segments, placing[0]
    )

    mine_dz0 = all_to_all(outgoing_dz0)
    side_dqkv1 = swap(dqkv1[:, 3 * part:], "tensor")
    side_dattn1 = swap(dattn1, "tensor")
    peer_dz0 = swap(after(mine_dz0, side_dqkv1, side_dattn1), "tensor")

    def stack(first, second):
        return jnp.concatenate([first, second], axis=0)

    def attention_grad(xn, side_xn, dqkv, side_dqkv):
        return dot(stack(xn, side_xn), stack(dqkv[:, :3 * part], side_dqkv), 0, 0)

    def output_grad(dattn, side_dattn, mixed, side_mixed):
        return dot(stack(dattn, side_dattn), stack(mixed[:, :part], side_mixed), 0, 0)

    ready_xn1, ready_dattn1 = after((state1["xn"], dattn1), mine_dz0)
    full1 = jnp.concatenate(
        [
            attention_grad(ready_xn1, side_xn1, dqkv1, side_dqkv1),
            output_grad(ready_dattn1, side_dattn1, state1["o"], side_o1),
        ],
        axis=1,
    )
    peer_dz0 = after(peer_dz0, full1)
    own_b0, peer_b0 = both_back(0, mine0, peer0, mine_dz0, peer_dz0)
    half1 = exchange_across(full1, section)
    reduced1 = all_to_all(after(half1, peer_b0[0])).astype(F32).sum(axis=0)
    dback0 = all_to_all(fold(own_b0[0], peer_b0[0]))

    def pick(first, second):
        return jnp.where(section == 0, first, second)

    def gather_rows(number, index):
        return stack((own_b0, own_b1)[number][index], (peer_b0, peer_b1)[number][index])

    rows0, rows1 = (stack(mine0, peer0), stack(mine1, peer1))
    dy0, dy1 = (gather_rows(0, 3), gather_rows(1, 3))
    near_rows = pick(rows0, rows1)
    near_dy = pick(dy0, dy1)
    near_act = pick(gather_rows(0, 1), gather_rows(1, 1))
    near_dpre = pick(gather_rows(0, 2), gather_rows(1, 2))
    near_in = dot(near_rows, near_dpre, 0, 0)
    near_out = dot(near_act, near_dy, 0, 0)
    far_rows = pick(one_way(rows0, "section", 1, 0), one_way(rows1, "section", 0, 1))
    far_dy = pick(one_way(dy0, "section", 1, 0), one_way(dy1, "section", 0, 1))

    grad0, dqkv0, dattn0, gains0 = layer_end(
        after(dback0, near_in, near_out), taking[0], grad1, x_own, state0, params0, segments, None
    )

    side_dqkv0 = swap(dqkv0[:, 3 * part:], "tensor")
    side_dattn0 = swap(after(dattn0, side_dqkv0), "tensor")
    far_rows, far_dy = after((far_rows, far_dy), dqkv0)
    far_before = dot(far_rows, w_in[0, 0], 1, 0)
    far_act, far_dpre = gelu_pair(far_before, dot(far_dy, w_exp_out[0, 0], 1, 1))
    in_w_grad = near_in + dot(far_rows, far_dpre, 0, 0)
    expert_w_grad = near_out + dot(far_act, far_dy, 0, 0)
    qkv_half0 = exchange_across(
        attention_grad(state0["xn"], side_xn0, dqkv0, side_dqkv0), section
    )
    out_half0 = exchange_across(
        output_grad(dattn0, side_dattn0, state0["o"], side_o0), section
    )
    back1 = all_to_all(after(total_y1, dqkv0))
    out1 = (state1["h"] + state1["gate"] * dot(taking[1], back1, 1, 0)).astype(BF16)

    smalls = [
        jnp.concatenate([gain, (own[4] + peer[4])[:experts]], axis=0)
        for gain, own, peer in ((gains0, own_b0, peer_b0), (gains1, own_b1, peer_b1))
    ]
    own_small = pick(*smalls) + swap(pick(*reversed(smalls)), "section")
    own_small = own_small + swap(own_small, "tensor")
    copies = jnp.broadcast_to(own_small[None], (count,) + own_small.shape)
    own_small = jnp.sum(all_to_all(copies), axis=0)

    reduced0 = jnp.concatenate(
        [
            all_to_all(qkv_half0).astype(F32).sum(axis=0),
            all_to_all(out_half0).astype(F32).sum(axis=0),
        ],
        axis=1,
    )
    own_half = pick(reduced0, reduced1)
    other_half = swap(pick(reduced1, reduced0).astype(BF16), "section").astype(F32)
    joined = ordered(section, own_half, other_half)
    qkv_grad = jnp.stack([joined[:, part * kind:part * (kind + 1)] for kind in range(3)])
    out_grad = joined[:, 3 * part:].T
    section_out = by_section([pair_up(out0, tensor), pair_up(out1, tensor)], section)
    section_in_grad = by_section([pair_up(grad0, tensor), pair_up(grad1, tensor)], section)
    return (
        section_out[None],
        section_in_grad[None],
        own_small[0][None],
        qkv_grad[None],
        out_grad[None],
        own_small[1][None],
        own_small[2:].T[None],
        in_w_grad[None, None],
        expert_w_grad[None, None],
    )


def solution(mesh):
    in_specs = (
        P(None, ("dp", "tensor"), None),
        P(None, ("dp", "tensor"), None),
        P(None, "dp", None),
        P("section", None, "dp", None),
        P("section", None),
        P("section", None, "dp", "tensor"),
        P("section", "tensor", "dp"),
        P("section", None),
        P("section", None, None),
        P("section", "dp", None, "tensor"),
        P("section", "dp", "tensor", None),
    )
    out_specs = (
        P("section", None, ("dp", "tensor"), None),
        P("section", None, ("dp", "tensor"), None),
        P("section", None),
        P("section", None, "dp", "tensor"),
        P("section", "tensor", "dp"),
        P("section", None),
        P("section", None, None),
        P("section", "dp", None, "tensor"),
        P("section", "dp", "tensor", None),
    )
    return jax.shard_map(shards, mesh=mesh, in_specs=in_specs, out_specs=out_specs, check_vma=False)
```

time: 692 us -> 719 us (1.039)
  matrix products: 114 us -> 78.8 us
  Pallas kernels: 39.2 us -> 67.9 us
  local copies, waits for them, and re-layouts: 48.6 us -> 76.3 us
  starting transfers between devices: 119 us -> 107 us
  other arithmetic: 36.2 us -> 46.7 us
  waiting for transfers between devices: 310 us -> 320 us
    all_to_all x13 -> x12, waiting for transfers between devices: 110 us -> 46.6 us  [all_to_all(): return lax.all_to_all(values, 'dp', split_axis=0, concat_axis=0, tiled=True)]
    ppermute x37 -> x36, waiting for transfers between devices: 154 us -> 204 us  [swap(): return lax.ppermute(values, axis, [(0, 1), (1, 0)])]
    dot_general x23 -> x17, matrix products: 114 us -> 78.8 us  [dot(): lax.dot_general(left, right, (((left_dim,), (right_dim,)), ((), ())), pre...]
    pallas_call x4 -> x8, Pallas kernels: 39.2 us -> 67.9 us  [the longest x4 35.4 us: staged_call(): pl.pallas_call(body, out_shape=outs, in_specs=[pl.BlockSpec(memory_space=...]
    unnamed x188 -> x228, local copies, waits for them, and re-layouts: 33.4 us -> 59 us
    ppermute x4 -> x6, waiting for transfers between devices: 0.01 us -> 25.3 us  [one_way(): return lax.ppermute(values, axis, [(source, target)])]
    ppermute x37 -> x36, starting transfers between devices: 57.1 us -> 37.9 us  [swap(): return lax.ppermute(values, axis, [(0, 1), (1, 0)])]
    select_n x6 -> x10, other arithmetic: 0.18 us -> 12.9 us  [the longest x6 7.27 us: of_layer(): return jnp.where(section == layer, own, other)]
  transfers between devices with their start and end apart: 57 -> 56, of which waited for: 26 -> 28; matrix products, arithmetic and copies ran while one was open for 23% -> 20% of each run, Pallas kernels for 5% -> 8%
where the time goes in v3:
time: 719 us; the launch traced here: 712 us
  waiting for transfers between devices  320 us (45%)
  starting transfers between devices  107 us (15%)
  matrix products  78.8 us (11%)
  local copies, waits for them, and re-layouts  76.3 us (11%)
  Pallas kernels  67.9 us (9%)
  other arithmetic  46.7 us (6%)
  between operations  15.3 us (2%)
    ppermute x36, waiting for transfers between devices, swap(): return lax.ppermute(values, axis, [(0, 1), (1, 0)])  204 us
    dot_general x17, matrix products, dot(): lax.dot_general(left, right, (((left_dim,), (right_dim,)), ((), ())), pre...  78.8 us
    unnamed x228, local copies, waits for them, and re-layouts  59 us
    all_to_all x12, starting transfers between devices, all_to_all(): return lax.all_to_all(values, 'dp', split_axis=0, concat_axis=0, tiled=True)  50.5 us
    all_to_all x12, waiting for transfers between devices, all_to_all(): return lax.all_to_all(values, 'dp', split_axis=0, concat_axis=0, tiled=True)  46.6 us
    all_gather x1, waiting for transfers between devices, shards(): lax.all_gather(jnp.concatenate([first_pack, first_beside], axis=1), 'dp',...  43.9 us
    ppermute x36, starting transfers between devices, swap(): return lax.ppermute(values, axis, [(0, 1), (1, 0)])  37.9 us
    pallas_call x4, Pallas kernels, staged_call(): pl.pallas_call(body, out_shape=outs, in_specs=[pl.BlockSpec(memory_space=...  35.4 us
  transfers between devices with their start and end apart: 56, of which 28 were waited for; matrix products, arithmetic and copies ran while one was open for 20% of the time, Pallas kernels for 8%

profile of v3, /device:TPU:0, one launch (start us, length us, event | category | flops | bytes accessed | tf_op | source)
XLA Modules:
  0.0 711.8 jit_solution(7491158957947397666)
XLA Ops:
  8.4 4.9 collective-permute-start.3
  13.3 6.2 collective-permute-done.3
  21.1 6.4 collective-permute-done.4
  33.6 2.9 collective-permute-done.2
  38.6 43.9 %all-gather.3.cloned.1.call-done.refs_4_.refs_7_ = bf16[768,3072]{1,0:T(8,128)(2,1)} async-done(((bf16[96,3072]{1,0:T(8,128)(2,1)}), bf16[768,3072]{1,0:T(8,128)(2,1)}) %all-gather.3.cloned.1.call-update) | async-done | bytes 4718608 | tf_op jit(solution)/shard_map/all_gather | solution.py:471
  84.8 7.3 %shard_map.178 = (bf16[256,768]{1,0:T(8,128)(2,1)S(1)}, bf16[256,2304]{1,0:T(8,128)(2,1)S(1)}, f32[256,128]{1,0:T(8,128)S(1)}, bf16[256,768]{1,0:T(8,128)(2,1)S(...) custom-call(bf16[256,768]{1,0:T(8,128)(2,1)S(1)} %maximum_select_fusion.7.refs_0_.refs_10_, ...), custom_call_target="tpu_custom_call" | custom-call | flops 3000000000 | bytes 9250816 | tf_op jit(solution)/shard_map/pallas_call | solution.py:262
  94.1 3.5 all-to-all-start
  101.0 6.3 collective-permute-done.12
  108.2 10.4 %all-to-all-done = bf16[8,64,768]{2,1,0:T(8,128)(2,1)S(1)} async-done(((bf16[8,64,768]{2,1,0:T(8,128)(2,1)}), bf16[8,64,768]{2,1,0:T(8,128)(2,1)S(1)}, u32[]{:S(2)}, u32[]{:S(2)}) %all-to-all-start) | async-done | bytes 786464 | tf_op jit(solution)/shard_map/all_to_all | solution.py:30
  123.0 11.8 %collective-permute-done.8 = bf16[256,384]{1,0:T(8,128)(2,1)S(1)} collective-permute-done((bf16[256,384]{1,0:T(8,128)(2,1)S(1)}, bf16[256,384]{1,0:T(8,128)(2,1)S(1)}, u32[]{:S(2)}, u32[]{:S(2)}) %collective-permute-start.8) | collective-permute-done | bytes 196640 | tf_op jit(solution)/shard_map/ppermute | solution.py:22
  136.3 17.7 %collective-permute-done.6 = bf16[1536,768]{1,0:T(8,128)(2,1)} collective-permute-done((bf16[1536,768]{1,0:T(8,128)(2,1)}, bf16[1536,768]{1,0:T(8,128)(2,1)}, u32[]{:S(2)}, u32[]{:S(2)}) %collective-permute-start.6) | collective-permute-done | bytes 2359328 | tf_op jit(solution)/shard_map/ppermute | solution.py:22
  153.9 4.1 broadcast_select_fusion
  158.0 45.5 %collective-permute-done.5 = bf16[768,1536]{1,0:T(8,128)(2,1)S(1)} collective-permute-done((bf16[768,1536]{1,0:T(8,128)(2,1)}, bf16[768,1536]{1,0:T(8,128)(2,1)S(1)}, u32[]{:S(2)}, u32[]{:S(2)}) %collective-permute-start.5) | collective-permute-done | bytes 2359328 | tf_op jit(solution)/shard_map/ppermute | solution.py:22
  206.9 5.6 fusion.71
  213.0 18.4 %collective-permute-done.10 = bf16[512,768]{1,0:T(8,128)(2,1)} collective-permute-done((bf16[512,768]{1,0:T(8,128)(2,1)}, bf16[512,768]{1,0:T(8,128)(2,1)}, u32[]{:S(2)}, u32[]{:S(2)}) %collective-permute-start.10) | collective-permute-done | bytes 786464 | tf_op jit(solution)/shard_map/ppermute | solution.py:22
  231.5 5.5 add_convert_fusion.3
  237.0 4.5 all-to-all-start.1
  243.4 6.8 collective-permute-done.14
  251.5 11.0 %all-to-all-done.1 = bf16[8,64,768]{2,1,0:T(8,128)(2,1)S(1)} async-done(((bf16[8,64,768]{2,1,0:T(8,128)(2,1)}), bf16[8,64,768]{2,1,0:T(8,128)(2,1)S(1)}, u32[]{:S(2)}, u32[]{:S(2)}) %all-to-all-start.1) | async-done | bytes 786464 | tf_op jit(solution)/shard_map/all_to_all | solution.py:30
  262.5 3.8 all-to-all-start.2
  275.9 8.0 %shard_map.179 = (bf16[256,768]{1,0:T(8,128)(2,1)S(1)}, bf16[256,2304]{1,0:T(8,128)(2,1)S(1)}, f32[256,128]{1,0:T(8,128)S(1)}, bf16[256,768]{1,0:T(8,128)(2,1)S(...) custom-call(bf16[256,512]{1,0:T(8,128)(2,1)S(1)} %fusion.112.refs_0_, ...), custom_call_target="tpu_custom_call" | custom-call | flops 3000000000 | bytes 11086848 | tf_op jit(solution)/shard_map/pallas_call | solution.py:262
  288.7 5.1 all-to-all-start.3
  296.5 13.2 %collective-permute-done.16 = bf16[256,384]{1,0:T(8,128)(2,1)S(1)} collective-permute-done((bf16[256,384]{1,0:T(8,128)(2,1)S(1)}, bf16[256,384]{1,0:T(8,128)(2,1)S(1)}, u32[]{:S(2)}, u32[]{:S(2)}) %collective-permute-start.16) | collective-permute-done | bytes 196640 | tf_op jit(solution)/shard_map/ppermute | solution.py:22
  311.1 18.4 %collective-permute-done.17.dz_ref = bf16[512,768]{1,0:T(8,128)(2,1)S(1)} collective-permute-done((bf16[512,768]{1,0:T(8,128)(2,1)S(1)}, bf16[512,768]{1,0:T(8,128)(2,1)S(1)}, u32[]{:S(2)}, u32[]{:S(2)}) %collective-permute-start.17) | collective-permute-done | bytes 786464 | tf_op jit(solution)/shard_map/ppermute | solution.py:22
  331.0 17.7 %collective-permute-done.18.rows_ref = bf16[512,768]{1,0:T(8,128)(2,1)S(1)} collective-permute-done((bf16[512,768]{1,0:T(8,128)(2,1)S(1)}, bf16[512,768]{1,0:T(8,128)(2,1)S(1)}, u32[]{:S(2)}, u32[]{:S(2)}) %collective-permute-start.18) | collective-permute-done | bytes 786464 | tf_op jit(solution)/shard_map/ppermute | solution.py:22
  356.1 8.4 %shard_map.180 = (bf16[512,768]{1,0:T(8,128)(2,1)}, bf16[512,1536]{1,0:T(8,128)(2,1)S(1)}, bf16[512,1536]{1,0:T(8,128)(2,1)S(1)}, bf16[512,768]{1,0:T(8,128)(2,1)S(1)}, f32[128,768]{1,0:T(8,128)S(1)}) custom-call(bf16[512,768]{1,0:T(8,128)(2,1)S(1)} %copy-done.19, bf16[512,768]{1,0:T(8,128)(2,1)S(1)} %copy-done.52, bf16[768,1536]{1,0:T(8,128)(2,1)S(1)} %copy-done.7, ...), custom_call_target="tpu_custom_call" | custom-call | flops 3623878656 | bytes 12000000 | tf_op jit(solution)/shard_map/pallas_call | solution.py:376
  369.0 2.6 pad_maximum_fusion.1
  374.5 7.6 %shard_map.181 = (f32[512,768]{1,0:T(8,128)S(1)}, bf16[512,1536]{1,0:T(8,128)(2,1)S(1)}, bf16[512,1536]{1,0:T(8,128)(2,1)S(1)}, bf16[512,768]{1,0:T(8,128)(2,1)S(1)}, f32[128,768]{1,0:T(8,128)S(1)}) custom-call(bf16[512,768]{1,0:T(8,128)(2,1)S(1)} %bitcast.143, bf16[512,768]{1,0:T(8,128)(2,1)S(1)} %bitcast.148, bf16[768,1536]{1,0:T(8,128)(2,1)S(1)} %copy-done.8, ...), custom_call_target="tpu_custom_call" | custom-call | flops 3623878656 | bytes 12000000 | tf_op jit(solution)/shard_map/pallas_call | solution.py:376
  387.6 3.6 all-to-all-start.4
  400.1 6.8 collective-permute-start.39
  407.8 2.8 collective-permute-start.41
  412.0 6.3 fusion.74
  431.0 10.3 %shard_map.182 = (bf16[256,768]{1,0:T(8,128)(2,1)S(1)}, bf16[256,2304]{1,0:T(8,128)(2,1)S(1)}, bf16[256,768]{1,0:T(8,128)(2,1)S(1)}, f32[2,768]{1,0:T(2,128)S(1)}, bf16[512,768]{1,0:T(8,128)(2,1)S(1)}) custom-call(bf16[256,512]{1,0:T(8,128)(2,1)S(1)} %copy-done.29, bf16[512,768]{1,0:T(8,128)(2,1)S(1)} %bitcast.151, f32[2,768]{1,0:T(2,128)S(1)} %copy-done.44, ...), custom_call_target="tpu_custom_call" | custom-call | flops 5000000000 | bytes 11679744 | tf_op jit(solution)/shard_map/pallas_call | solution.py:262
  443.0 5.3 all-to-all-start.5
  450.9 6.3 add_convert_fusion.2
  457.8 2.8 broadcast_select_fusion.5
  462.9 6.4 all-to-all-done.5
  469.3 5.0 collective-permute-done.22
  484.3 8.7 %shard_map.183 = (f32[512,768]{1,0:T(8,128)S(1)}, bf16[512,1536]{1,0:T(8,128)(2,1)S(1)}, bf16[512,1536]{1,0:T(8,128)(2,1)S(1)}, bf16[512,768]{1,0:T(8,128)(2,1)S(1)}, f32[128,768]{1,0:T(8,128)S(1)}) custom-call(bf16[512,768]{1,0:T(8,128)(2,1)S(1)} %bitcast.140, bf16[512,768]{1,0:T(8,128)(2,1)} %bitcast.35.dz_ref, bf16[768,1536]{1,0:T(8,128)(2,1)S(1)} %copy-done.4, ...), custom_call_target="tpu_custom_call" | custom-call | flops 3623878656 | bytes 12000000 | tf_op jit(solution)/shard_map/pallas_call | solution.py:376
  494.9 7.8 %shard_map.184 = (bf16[512,768]{1,0:T(8,128)(2,1)S(1)}, bf16[512,1536]{1,0:T(8,128)(2,1)S(1)}, bf16[512,1536]{1,0:T(8,128)(2,1)S(1)}, bf16[512,768]{1,0:T(8,128)(2,1)S(1)}, f32[128,768]{1,0:T(8,128)S(1)}) custom-call(bf16[512,768]{1,0:T(8,128)(2,1)S(1)} %copy-done.17, bf16[512,768]{1,0:T(8,128)(2,1)S(1)} %collective-permute-done.23.dz_ref, ...), custom_call_target="tpu_custom_call" | custom-call | flops 3623878656 | bytes 12000000 | tf_op jit(solution)/shard_map/pallas_call | solution.py:376
  505.2 5.0 fusion.39
  510.2 11.9 %collective-permute-done.24 = bf16[512,768]{1,0:T(8,128)(2,1)S(1)} collective-permute-done((bf16[512,768]{1,0:T(8,128)(2,1)S(1)}, bf16[512,768]{1,0:T(8,128)(2,1)S(1)}, u32[]{:S(2)}, u32[]{:S(2)}) %collective-permute-start.24) | collective-permute-done | bytes 786464 | tf_op jit(solution)/shard_map/ppermute | solution.py:22
  524.4 4.3 all-to-all-start.6
  528.7 8.3 %fusion.45 = f32[1536,768]{1,0:T(8,128)} fusion(bf16[512,1536]{1,0:T(8,128)(2,1)} %copy-done.75, bf16[512,1536]{1,0:T(8,128)(2,1)} %copy-done.74, bf16[512,1536]{1,0:T(8,128)(2,1)} %copy-done.68, bf16[512,1536]{1,0:T(8,128)(2,1)} %copy-done.71, pred[]{:T(512)S(6)} %eq.54, bf16[1024,768]{1,0:T(8,128)(2,1)} %constant_dynamic-update-slice_fusion, ...), kind=kOutput, calls=%fused_computation.57 | convolution fusion | flops 2430861312 | bytes 14155777 | tf_op jit(solution)/shard_map/dot_general | solution.py:38
  537.0 3.4 fusion.57
  540.4 19.1 %collective-permute-done.40 = bf16[1024,768]{1,0:T(8,128)(2,1)} collective-permute-done((bf16[1024,768]{1,0:T(8,128)(2,1)}, bf16[1024,768]{1,0:T(8,128)(2,1)}, u32[]{:S(2)}, u32[]{:S(2)}) %collective-permute-start.40) | collective-permute-done | bytes 1572896 | tf_op jit(solution)/shard_map/ppermute | solution.py:26
  559.5 2.8 broadcast_select_fusion.4
  562.3 4.8 all-to-all-start.11
  571.9 9.7 %shard_map.185 = (bf16[256,768]{1,0:T(8,128)(2,1)S(1)}, bf16[256,2304]{1,0:T(8,128)(2,1)S(1)}, bf16[256,768]{1,0:T(8,128)(2,1)S(1)}, f32[2,768]{1,0:T(2,128)S(1)}) custom-call(bf16[256,512]{1,0:T(8,128)(2,1)S(1)} %copy-done.26, bf16[512,768]{1,0:T(8,128)(2,1)S(1)} %bitcast.150, f32[2,768]{1,0:T(2,128)S(1)} %copy-done.42, ...), custom_call_target="tpu_custom_call" | custom-call | flops 5000000000 | bytes 10631168 | tf_op jit(solution)/shard_map/pallas_call | solution.py:262
  583.4 4.6 fusion.142
  589.5 16.1 %add_bitcast_fusion.1 = f32[1,1,768,1536]{3,2,1,0:T(8,128)} fusion(f32[768,1536]{1,0:T(8,128)} %fusion.39, bf16[1024,768]{1,0:T(8,128)(2,1)} %broadcast_select_fusion.5, f32[1024,1536]{1,0:T(8,128)} %fusion.142, bf16[1024,768]{1,0:T(8,128)(2,1)} %broadcast_select_fusion.4, bf16[1,1,1536,768]{3,2,1,0:T(8,128)(2,1)} %param.21), kind=kOutput, calls=%fused_computation.16 | convolution fusion | flops 4864475136 | bytes 21233664 | tf_op jit(solution)/shard_map/dot_general | solution.py:38
  606.4 4.0 fusion.88
  611.1 5.1 all-to-all-start.8
  622.4 6.4 all-to-all-done.8
  628.8 3.5 all-to-all-start.7
  632.3 10.6 %add_bitcast_fusion = f32[1,1,1536,768]{3,2,1,0:T(8,128)} fusion(f32[1536,768]{1,0:T(8,128)} %fusion.45, bf16[1024,768]{1,0:T(8,128)(2,1)} %broadcast_select_fusion.4, f32[1024,1536]{1,0:T(8,128)} %fusion.142), kind=kOutput, calls=%fused_computation.15 | convolution fusion | flops 2431254528 | bytes 17301504 | tf_op jit(solution)/shard_map/dot_general | solution.py:38
  648.3 4.9 all-to-all-done.7
  653.2 3.4 all-to-all-start.10
  656.7 2.9 fusion.58
  659.5 7.5 %all-to-all-done.10 = bf16[8,48,384]{2,1,0:T(8,128)(2,1)S(1)} async-done(((bf16[8,48,384]{2,1,0:T(8,128)(2,1)}), bf16[8,48,384]{2,1,0:T(8,128)(2,1)S(1)}, u32[]{:S(2)}, u32[]{:S(2)}) %all-to-all-start.10) | async-done | bytes 294944 | tf_op jit(solution)/shard_map/all_to_all | solution.py:30
  667.0 3.6 all-to-all-start.9
  679.5 5.7 collective-permute-done.25
  689.5 7.3 %collective-permute-done.26 = bf16[2,128,768]{2,1,0:T(8,128)(2,1)S(1)} collective-permute-done((bf16[2,128,768]{2,1,0:T(8,128)(2,1)S(1)}, bf16[2,128,768]{2,1,0:T(8,128)(2,1)S(1)}, u32[]{:S(2)}, u32[]{:S(2)}) %collective-permute-start.26) | collective-permute-done | bytes 393248 | tf_op jit(solution)/shard_map/ppermute | solution.py:22
  698.7 4.5 collective-permute-done.37
  (384 shorter events, 157.7 us)
Async XLA Ops:
  7.2 75.2 %all-gather.3.cloned.1.call-start = ((), (), s32[]{:S(2)}) async-start(), calls=%async_computation.12 | async-start | bytes 5308416 | tf_op jit(solution)/shard_map/all_gather | solution.py:471
  8.4 11.1 %collective-permute-start.3 = (bf16[96,1536]{1,0:T(8,128)(2,1)S(1)}, bf16[96,1536]{1,0:T(8,128)(2,1)S(1)}, u32[]{:S(2)}, u32[]{:S(2)}) collective-permute-start(bf16[96,1536]{1,0:T(8,128)(2,1)S(1)} %bitcast.166), channel_id=1, source_target_pairs={{0,16},{1,17},{2,18},{3,19},{4,20},{5,21},{6,22},{7,23},{8,24},{9,... | collective-permute-start | bytes 884744 | tf_op jit(solution)/shard_map/ppermute | solution.py:26
  19.5 7.9 %collective-permute-start.4 = (bf16[96,1536]{1,0:T(8,128)(2,1)S(1)}, bf16[96,1536]{1,0:T(8,128)(2,1)S(1)}, u32[]{:S(2)}, u32[]{:S(2)}) collective-permute-start(bf16[96,1536]{1,0:T(8,128)(2,1)S(1)} %broadcast_select_fusion.9), channel_id=1, source_target_pairs={{0,1},{1,0},{2,3},{3,2},{4,5},{5,4},{6,7},{7,6},{8,9},{9,8},{10,11... | collective-permute-start | bytes 884744 | tf_op jit(solution)/shard_map/ppermute | solution.py:22
  28.4 4.7 collective-permute-start
  31.0 6.2 collective-permute-start.1
  32.6 3.9 collective-permute-start.2
  33.1 235.6 %copy-start.36 = (s32[256,1]{1,0:T(8,128)}, s32[256,1]{1,0:T(8,128)S(1)}, u32[]{:S(2)}) copy-start(s32[256,1]{1,0:T(8,128)S(1)} %copy.39.refs_2_.refs_5_) | copy-start | bytes 3076
  33.4 58.8 %copy-start.102 = (s32[256]{0:T(256)}, s32[256]{0:T(256)S(1)}, u32[]{:S(2)}) copy-start(s32[256]{0:T(256)S(1)} %convert_add_fusion.1) | copy-start | bytes 3076
  33.5 58.7 %copy-start.27 = (bf16[512,256]{1,0:T(8,128)(2,1)}, bf16[512,256]{1,0:T(8,128)(2,1)S(1)}, u32[]{:S(2)}) copy-start(bf16[512,256]{1,0:T(8,128)(2,1)S(1)} %fusion.113.refs_5_.refs_11_) | copy-start | bytes 786436
  37.2 55.0 %copy-start.31 = (bf16[128,768]{1,0:T(8,128)(2,1)}, bf16[128,768]{1,0:T(8,128)(2,1)S(1)}, u32[]{:S(2)}) copy-start(bf16[128,768]{1,0:T(8,128)(2,1)S(1)} %pad.7.refs_6_.router_ref) | copy-start | bytes 589828
  37.2 55.0 %copy-start.41 = (f32[2,768]{1,0:T(2,128)}, f32[2,768]{1,0:T(2,128)S(1)}, u32[]{:S(2)}) copy-start(f32[2,768]{1,0:T(2,128)S(1)} %slice_convert_fusion.1.refs_1_.refs_2_) | copy-start | bytes 18436
  37.3 60.6 %collective-permute-start.11 = (bf16[96,1536]{1,0:T(8,128)(2,1)S(1)}, bf16[96,1536]{1,0:T(8,128)(2,1)S(1)}, u32[]{:S(2)}, u32[]{:S(2)}) collective-permute-start(bf16[96,1536]{1,0:T(8,128)(2,1)S(1)} %bitcast.168), channel_id=1, source_target_pairs={{16,0},{17,1},{18,2},{19,3},{20,4},{21,5},{22,6},{23,7},{24,8},{25... | collective-permute-start | bytes 884744 | tf_op jit(solution)/shard_map/ppermute | solution.py:26
  94.1 24.5 %all-to-all-start = ((bf16[8,64,768]{2,1,0:T(8,128)(2,1)}), bf16[8,64,768]{2,1,0:T(8,128)(2,1)S(1)}, u32[]{:S(2)}, u32[]{:S(2)}) async-start(bf16[8,64,768]{2,1,0:T(8,128)(2,1)} %bitcast.16), calls=%async_computation | async-start | bytes 1572864 | tf_op jit(solution)/shard_map/all_to_all | solution.py:30
  97.7 171.0 %all-gather.5.cloned.1.call-start = ((), (), s32[]{:S(2)}) async-start(), calls=%async_computation.13 | async-start | bytes 5308416 | tf_op jit(solution)/shard_map/all_gather | solution.py:515
  98.0 9.3 %collective-permute-start.12 = (bf16[96,1536]{1,0:T(8,128)(2,1)S(1)}, bf16[96,1536]{1,0:T(8,128)(2,1)S(1)}, u32[]{:S(2)}, u32[]{:S(2)}) collective-permute-start(bf16[96,1536]{1,0:T(8,128)(2,1)S(1)} %broadcast_select_fusion.8), channel_id=1, source_target_pairs={{0,1},{1,0},{2,3},{3,2},{4,5},{5,4},{6,7},{7,6},{8,9},{9,8},{10,11... | collective-permute-start | bytes 884744 | tf_op jit(solution)/shard_map/ppermute | solution.py:22
  99.5 54.4 %collective-permute-start.6 = (bf16[1536,768]{1,0:T(8,128)(2,1)}, bf16[1536,768]{1,0:T(8,128)(2,1)}, u32[]{:S(2)}, u32[]{:S(2)}) collective-permute-start(bf16[1536,768]{1,0:T(8,128)(2,1)} %bitcast.172), channel_id=1, source_target_pairs={{0,16},{16,0},{1,17},{17,1},{2,18},{18,2},{3,19},{19,3},{4,20},{20... | collective-permute-start | bytes 7077896 | tf_op jit(solution)/shard_map/ppermute | solution.py:22
  118.6 84.9 %collective-permute-start.5 = (bf16[768,1536]{1,0:T(8,128)(2,1)}, bf16[768,1536]{1,0:T(8,128)(2,1)S(1)}, u32[]{:S(2)}, u32[]{:S(2)}) collective-permute-start(bf16[768,1536]{1,0:T(8,128)(2,1)} %bitcast.170), channel_id=1, source_target_pairs={{0,16},{16,0},{1,17},{17,1},{2,18},{18,2},{3,19},{19,3},{4,20},{20... | collective-permute-start | bytes 7077896 | tf_op jit(solution)/shard_map/ppermute | solution.py:22
  120.2 14.6 %collective-permute-start.7 = (bf16[256,768]{1,0:T(8,128)(2,1)S(1)}, bf16[256,768]{1,0:T(8,128)(2,1)S(1)}, u32[]{:S(2)}, u32[]{:S(2)}) collective-permute-start(bf16[256,768]{1,0:T(8,128)(2,1)S(1)} %get-tuple-element.79), channel_id=1, source_target_pairs={{0,1},{1,0},{2,3},{3,2},{4,5},{5,4},{6,7},{7,6},{8,9},{9,8},{10,11... | collective-permute-start | bytes 1179656 | tf_op jit(solution)/shard_map/ppermute | solution.py:22
  122.4 81.2 %copy-start.83 = (bf16[1,1,768,1536]{3,2,1,0:T(8,128)(2,1)S(1)}, bf16[1,1,768,1536]{3,2,1,0:T(8,128)(2,1)}, u32[]{:S(2)}) copy-start(bf16[1,1,768,1536]{3,2,1,0:T(8,128)(2,1)} %param.20) | copy-start | bytes 7077892
  122.4 12.4 %collective-permute-start.8 = (bf16[256,384]{1,0:T(8,128)(2,1)S(1)}, bf16[256,384]{1,0:T(8,128)(2,1)S(1)}, u32[]{:S(2)}, u32[]{:S(2)}) collective-permute-start(bf16[256,384]{1,0:T(8,128)(2,1)S(1)} %get-tuple-element.164), channel_id=1, source_target_pairs={{0,1},{1,0},{2,3},{3,2},{4,5},{5,4},{6,7},{7,6},{8,9},{9,8},{10,11... | collective-permute-start | bytes 589832 | tf_op jit(solution)/shard_map/ppermute | solution.py:22
  134.8 71.2 %copy-start.110 = (bf16[256,384]{1,0:T(8,128)(2,1)}, bf16[256,384]{1,0:T(8,128)(2,1)S(1)}, u32[]{:S(2)}) copy-start(bf16[256,384]{1,0:T(8,128)(2,1)S(1)} %collective-permute-done.8) | copy-start | bytes 589828
  134.8 71.2 %collective-permute-start.9 = (bf16[512,768]{1,0:T(8,128)(2,1)S(1)}, bf16[512,768]{1,0:T(8,128)(2,1)S(1)}, u32[]{:S(2)}, u32[]{:S(2)}) collective-permute-start(bf16[512,768]{1,0:T(8,128)(2,1)S(1)} %bitcast.137), channel_id=1, source_target_pairs={{0,1},{1,0},{2,3},{3,2},{4,5},{5,4},{6,7},{7,6},{8,9},{9,8},{10,11... | collective-permute-start | bytes 2359304 | tf_op jit(solution)/shard_map/ppermute | solution.py:22
  158.0 73.4 %copy-start.2 = (bf16[1536,768]{1,0:T(8,128)(2,1)}, bf16[1536,768]{1,0:T(8,128)(2,1)S(1)}, u32[]{:S(2)}) copy-start(bf16[1536,768]{1,0:T(8,128)(2,1)S(1)} %get-tuple-element.146.out_ref) | copy-start | bytes 7077892
  212.5 19.0 %collective-permute-start.10 = (bf16[512,768]{1,0:T(8,128)(2,1)}, bf16[512,768]{1,0:T(8,128)(2,1)}, u32[]{:S(2)}, u32[]{:S(2)}) collective-permute-start(bf16[512,768]{1,0:T(8,128)(2,1)} %fusion.71), channel_id=1, source_target_pairs={{0,1},{1,0},{2,3},{3,2},{4,5},{5,4},{6,7},{7,6},{8,9},{9,8},{10,11... | collective-permute-start | bytes 2359304 | tf_op jit(solution)/shard_map/ppermute | solution.py:22
  237.0 25.5 %all-to-all-start.1 = ((bf16[8,64,768]{2,1,0:T(8,128)(2,1)}), bf16[8,64,768]{2,1,0:T(8,128)(2,1)S(1)}, u32[]{:S(2)}, u32[]{:S(2)}) async-start(bf16[8,64,768]{2,1,0:T(8,128)(2,1)} %bitcast.177), calls=%async_computation.1 | async-start | bytes 1572864 | tf_op jit(solution)/shard_map/all_to_all | solution.py:30
  242.8 7.4 %collective-permute-start.14 = (bf16[128,768]{1,0:T(8,128)(2,1)S(1)}, bf16[128,768]{1,0:T(8,128)(2,1)S(1)}, u32[]{:S(2)}, u32[]{:S(2)}) collective-permute-start(bf16[128,768]{1,0:T(8,128)(2,1)S(1)} %get-tuple-element.156), channel_id=1, source_target_pairs={{0,1},{1,0},{2,3},{3,2},{4,5},{5,4},{6,7},{7,6},{8,9},{9,8},{10,11... | collective-permute-start | bytes 589832 | tf_op jit(solution)/shard_map/ppermute | solution.py:22
  262.5 26.1 %all-to-all-start.2 = ((bf16[8,64,768]{2,1,0:T(8,128)(2,1)}), bf16[8,64,768]{2,1,0:T(8,128)(2,1)S(1)}, u32[]{:S(2)}, u32[]{:S(2)}) async-start(bf16[8,64,768]{2,1,0:T(8,128)(2,1)} %bitcast.164), calls=%async_computation.2 | async-start | bytes 1572864 | tf_op jit(solution)/shard_map/all_to_all | solution.py:30
  288.7 41.8 %all-to-all-start.3 = ((bf16[8,64,768]{2,1,0:T(8,128)(2,1)}), bf16[8,64,768]{2,1,0:T(8,128)(2,1)S(1)}, u32[]{:S(2)}, u32[]{:S(2)}) async-start(bf16[8,64,768]{2,1,0:T(8,128)(2,1)} %bitcast.30), calls=%async_computation.3 | async-start | bytes 1572864 | tf_op jit(solution)/shard_map/all_to_all | solution.py:30
  293.7 16.6 %collective-permute-start.15 = (bf16[256,768]{1,0:T(8,128)(2,1)}, bf16[256,768]{1,0:T(8,128)(2,1)S(1)}, u32[]{:S(2)}, u32[]{:S(2)}) collective-permute-start(bf16[256,768]{1,0:T(8,128)(2,1)} %copy-done.55), channel_id=1, source_target_pairs={{0,1},{1,0},{2,3},{3,2},{4,5},{5,4},{6,7},{7,6},{8,9},{9,8},{10,11... | collective-permute-start | bytes 1179656 | tf_op jit(solution)/shard_map/ppermute | solution.py:22
  295.0 14.7 %collective-permute-start.16 = (bf16[256,384]{1,0:T(8,128)(2,1)S(1)}, bf16[256,384]{1,0:T(8,128)(2,1)S(1)}, u32[]{:S(2)}, u32[]{:S(2)}) collective-permute-start(bf16[256,384]{1,0:T(8,128)(2,1)S(1)} %get-tuple-element.174), channel_id=1, source_target_pairs={{0,1},{1,0},{2,3},{3,2},{4,5},{5,4},{6,7},{7,6},{8,9},{9,8},{10,11... | collective-permute-start | bytes 589832 | tf_op jit(solution)/shard_map/ppermute | solution.py:22
  310.4 19.2 %collective-permute-start.17 = (bf16[512,768]{1,0:T(8,128)(2,1)S(1)}, bf16[512,768]{1,0:T(8,128)(2,1)S(1)}, u32[]{:S(2)}, u32[]{:S(2)}) collective-permute-start(bf16[512,768]{1,0:T(8,128)(2,1)S(1)} %bitcast.147), channel_id=1, source_target_pairs={{0,1},{1,0},{2,3},{3,2},{4,5},{5,4},{6,7},{7,6},{8,9},{9,8},{10,11... | collective-permute-start | bytes 2359304 | tf_op jit(solution)/shard_map/ppermute | solution.py:22
  330.4 18.3 %collective-permute-start.18 = (bf16[512,768]{1,0:T(8,128)(2,1)S(1)}, bf16[512,768]{1,0:T(8,128)(2,1)S(1)}, u32[]{:S(2)}, u32[]{:S(2)}) collective-permute-start(bf16[512,768]{1,0:T(8,128)(2,1)S(1)} %bitcast.142), channel_id=1, source_target_pairs={{0,1},{1,0},{2,3},{3,2},{4,5},{5,4},{6,7},{7,6},{8,9},{9,8},{10,11... | collective-permute-start | bytes 2359304 | tf_op jit(solution)/shard_map/ppermute | solution.py:22
  367.6 17.7 %collective-permute-start.19 = (bf16[512,768]{1,0:T(8,128)(2,1)}, bf16[512,768]{1,0:T(8,128)(2,1)}, u32[]{:S(2)}, u32[]{:S(2)}) collective-permute-start(bf16[512,768]{1,0:T(8,128)(2,1)} %get-tuple-element.97), channel_id=1, source_target_pairs={{0,1},{1,0},{2,3},{3,2},{4,5},{5,4},{6,7},{7,6},{8,9},{9,8},{10,11... | collective-permute-start | bytes 2359304 | tf_op jit(solution)/shard_map/ppermute | solution.py:22
  371.5 85.6 %collective-permute-start.38 = (bf16[1024,768]{1,0:T(8,128)(2,1)}, bf16[1024,768]{1,0:T(8,128)(2,1)}, u32[]{:S(2)}, u32[]{:S(2)}) collective-permute-start(bf16[1024,768]{1,0:T(8,128)(2,1)} %pad_maximum_fusion.1), channel_id=1, source_target_pairs={{16,0},{17,1},{18,2},{19,3},{20,4},{21,5},{22,6},{23,7},{24,8},{25... | collective-permute-start | bytes 4718600 | tf_op jit(solution)/shard_map/ppermute | solution.py:26
  387.6 31.2 %all-to-all-start.4 = ((bf16[8,64,768]{2,1,0:T(8,128)(2,1)}), bf16[8,64,768]{2,1,0:T(8,128)(2,1)S(1)}, u32[]{:S(2)}, u32[]{:S(2)}) async-start(bf16[8,64,768]{2,1,0:T(8,128)(2,1)} %bitcast.165), calls=%async_computation.4 | async-start | bytes 1572864 | tf_op jit(solution)/shard_map/all_to_all | solution.py:30
  393.0 286.5 %collective-permute-start.13 = (bf16[128,768]{1,0:T(8,128)(2,1)}, bf16[128,768]{1,0:T(8,128)(2,1)}, u32[]{:S(2)}, u32[]{:S(2)}) collective-permute-start(bf16[128,768]{1,0:T(8,128)(2,1)} %get-tuple-element.169), channel_id=1, source_target_pairs={{0,1},{1,0},{2,3},{3,2},{4,5},{5,4},{6,7},{7,6},{8,9},{9,8},{10,11... | collective-permute-start | bytes 589832 | tf_op jit(solution)/shard_map/ppermute | solution.py:22
  400.1 57.7 %collective-permute-start.39 = (bf16[1024,768]{1,0:T(8,128)(2,1)}, bf16[1024,768]{1,0:T(8,128)(2,1)}, u32[]{:S(2)}, u32[]{:S(2)}) collective-permute-start(bf16[1024,768]{1,0:T(8,128)(2,1)} %pad_maximum_fusion.2), channel_id=1, source_target_pairs={{0,16},{1,17},{2,18},{3,19},{4,20},{5,21},{6,22},{7,23},{8,24},{9,... | collective-permute-start | bytes 4718600 | tf_op jit(solution)/shard_map/ppermute | solution.py:26
  407.8 132.6 %collective-permute-start.41 = (bf16[1024,768]{1,0:T(8,128)(2,1)}, bf16[1024,768]{1,0:T(8,128)(2,1)}, u32[]{:S(2)}, u32[]{:S(2)}) collective-permute-start(bf16[1024,768]{1,0:T(8,128)(2,1)} %constant_dynamic-update-slice_fusion.2), channel_id=1, source_target_pairs={{0,16},{1,17},{2,18},{3,19},{4,20},{5,21},{6,22},{7,23},{8,24},{9,... | collective-permute-start | bytes 4718600 | tf_op jit(solution)/shard_map/ppermute | solution.py:26
  418.3 31.2 %collective-permute-start.20 = (bf16[512,768]{1,0:T(8,128)(2,1)}, bf16[512,768]{1,0:T(8,128)(2,1)}, u32[]{:S(2)}, u32[]{:S(2)}) collective-permute-start(bf16[512,768]{1,0:T(8,128)(2,1)} %fusion.74), channel_id=1, source_target_pairs={{0,1},{1,0},{2,3},{3,2},{4,5},{5,4},{6,7},{7,6},{8,9},{9,8},{10,11... | collective-permute-start | bytes 2359304 | tf_op jit(solution)/shard_map/ppermute | solution.py:22
  443.0 26.4 %all-to-all-start.5 = ((bf16[8,64,768]{2,1,0:T(8,128)(2,1)}), bf16[8,64,768]{2,1,0:T(8,128)(2,1)}, u32[]{:S(2)}, u32[]{:S(2)}) async-start(bf16[8,64,768]{2,1,0:T(8,128)(2,1)} %bitcast.152), calls=%async_computation.5 | async-start | bytes 1572864 | tf_op jit(solution)/shard_map/all_to_all | solution.py:30
  449.4 24.9 %collective-permute-start.21 = (bf16[256,1152]{1,0:T(8,128)(2,1)}, bf16[256,1152]{1,0:T(8,128)(2,1)}, u32[]{:S(2)}, u32[]{:S(2)}) collective-permute-start(bf16[256,1152]{1,0:T(8,128)(2,1)} %get-tuple-element.150), channel_id=1, source_target_pairs={{0,1},{1,0},{2,3},{3,2},{4,5},{5,4},{6,7},{7,6},{8,9},{9,8},{10,11... | collective-permute-start | bytes 1769480 | tf_op jit(solution)/shard_map/ppermute | solution.py:22
  457.2 17.1 %collective-permute-start.22 = (bf16[256,768]{1,0:T(8,128)(2,1)S(1)}, bf16[256,768]{1,0:T(8,128)(2,1)}, u32[]{:S(2)}, u32[]{:S(2)}) collective-permute-start(bf16[256,768]{1,0:T(8,128)(2,1)S(1)} %copy-done.58), channel_id=1, source_target_pairs={{0,1},{1,0},{2,3},{3,2},{4,5},{5,4},{6,7},{7,6},{8,9},{9,8},{10,11... | collective-permute-start | bytes 1179656 | tf_op jit(solution)/shard_map/ppermute | solution.py:22
  461.4 209.2 %collective-permute-start.28 = (bf16[128,768]{1,0:T(8,128)(2,1)}, bf16[128,768]{1,0:T(8,128)(2,1)}, u32[]{:S(2)}, u32[]{:S(2)}) collective-permute-start(bf16[128,768]{1,0:T(8,128)(2,1)} %get-tuple-element.167), channel_id=1, source_target_pairs={{0,1},{1,0},{2,3},{3,2},{4,5},{5,4},{6,7},{7,6},{8,9},{9,8},{10,11... | collective-permute-start | bytes 589832 | tf_op jit(solution)/shard_map/ppermute | solution.py:22
  474.3 20.6 %collective-permute-start.23 = (bf16[512,768]{1,0:T(8,128)(2,1)}, bf16[512,768]{1,0:T(8,128)(2,1)S(1)}, u32[]{:S(2)}, u32[]{:S(2)}) collective-permute-start(bf16[512,768]{1,0:T(8,128)(2,1)} %bitcast.35.dz_ref), channel_id=1, source_target_pairs={{0,1},{1,0},{2,3},{3,2},{4,5},{5,4},{6,7},{7,6},{8,9},{9,8},{10,11... | collective-permute-start | bytes 2359304 | tf_op jit(solution)/shard_map/ppermute | solution.py:22
  483.3 53.7 %collective-permute-start.36 = (bf16[8,48,1536]{2,1,0:T(8,128)(2,1)}, bf16[8,48,1536]{2,1,0:T(8,128)(2,1)}, u32[]{:S(2)}, u32[]{:S(2)}) collective-permute-start(bf16[8,48,1536]{2,1,0:T(8,128)(2,1)} %fusion.83), channel_id=1, source_target_pairs={{0,16},{16,0},{1,17},{17,1},{2,18},{18,2},{3,19},{19,3},{4,20},{20... | collective-permute-start | bytes 3538952 | tf_op jit(solution)/shard_map/ppermute | solution.py:22
  502.7 19.3 %collective-permute-start.24 = (bf16[512,768]{1,0:T(8,128)(2,1)S(1)}, bf16[512,768]{1,0:T(8,128)(2,1)S(1)}, u32[]{:S(2)}, u32[]{:S(2)}) collective-permute-start(bf16[512,768]{1,0:T(8,128)(2,1)S(1)} %get-tuple-element.112), channel_id=1, source_target_pairs={{0,1},{1,0},{2,3},{3,2},{4,5},{5,4},{6,7},{7,6},{8,9},{9,8},{10,11... | collective-permute-start | bytes 2359304 | tf_op jit(solution)/shard_map/ppermute | solution.py:22
  522.0 37.5 %collective-permute-start.40 = (bf16[1024,768]{1,0:T(8,128)(2,1)}, bf16[1024,768]{1,0:T(8,128)(2,1)}, u32[]{:S(2)}, u32[]{:S(2)}) collective-permute-start(bf16[1024,768]{1,0:T(8,128)(2,1)} %constant_dynamic-update-slice_fusion), channel_id=1, source_target_pairs={{16,0},{17,1},{18,2},{19,3},{20,4},{21,5},{22,6},{23,7},{24,8},{25... | collective-permute-start | bytes 4718600 | tf_op jit(solution)/shard_map/ppermute | solution.py:26
  524.4 37.9 %all-to-all-start.6 = ((bf16[8,64,768]{2,1,0:T(8,128)(2,1)}), bf16[8,64,768]{2,1,0:T(8,128)(2,1)S(1)}, u32[]{:S(2)}, u32[]{:S(2)}) async-start(bf16[8,64,768]{2,1,0:T(8,128)(2,1)} %bitcast.36), calls=%async_computation.6 | async-start | bytes 1572864 | tf_op jit(solution)/shard_map/all_to_all | solution.py:30
  562.3 48.1 %all-to-all-start.11 = ((bf16[8,48,1536]{2,1,0:T(8,128)(2,1)}), bf16[8,48,1536]{2,1,0:T(8,128)(2,1)}, u32[]{:S(2)}, u32[]{:S(2)}) async-start(bf16[8,48,1536]{2,1,0:T(8,128)(2,1)} %fusion.57), calls=%async_computation.11 | async-start | bytes 2359296 | tf_op jit(solution)/shard_map/all_to_all | solution.py:30
  581.7 6.3 collective-permute-start.30
  581.9 23.8 %collective-permute-start.32 = (bf16[256,1152]{1,0:T(8,128)(2,1)S(1)}, bf16[256,1152]{1,0:T(8,128)(2,1)}, u32[]{:S(2)}, u32[]{:S(2)}) collective-permute-start(bf16[256,1152]{1,0:T(8,128)(2,1)S(1)} %get-tuple-element.148), channel_id=1, source_target_pairs={{0,1},{1,0},{2,3},{3,2},{4,5},{5,4},{6,7},{7,6},{8,9},{9,8},{10,11... | collective-permute-start | bytes 1769480 | tf_op jit(solution)/shard_map/ppermute | solution.py:22
  588.0 17.6 %collective-permute-start.31 = (f32[10,768]{1,0:T(8,128)S(1)}, f32[10,768]{1,0:T(8,128)S(1)}, u32[]{:S(2)}, u32[]{:S(2)}) collective-permute-start(f32[10,768]{1,0:T(8,128)S(1)} %fusion.126), channel_id=1, source_target_pairs={{0,1},{1,0},{2,3},{3,2},{4,5},{5,4},{6,7},{7,6},{8,9},{9,8},{10,11... | collective-permute-start | bytes 92168 | tf_op jit(solution)/shard_map/ppermute | solution.py:22
  605.6 15.1 %collective-permute-start.34 = (bf16[256,768]{1,0:T(8,128)(2,1)S(1)}, bf16[256,768]{1,0:T(8,128)(2,1)S(1)}, u32[]{:S(2)}, u32[]{:S(2)}) collective-permute-start(bf16[256,768]{1,0:T(8,128)(2,1)S(1)} %get-tuple-element.139), channel_id=1, source_target_pairs={{0,1},{1,0},{2,3},{3,2},{4,5},{5,4},{6,7},{7,6},{8,9},{9,8},{10,11... | collective-permute-start | bytes 1179656 | tf_op jit(solution)/shard_map/ppermute | solution.py:22
  611.1 17.6 %all-to-all-start.8 = ((f32[8,10,768]{2,1,0:T(8,128)}), f32[8,10,768]{2,1,0:T(8,128)S(1)}, u32[]{:S(2)}, u32[]{:S(2)}) async-start(f32[8,10,768]{2,1,0:T(8,128)} %broadcast_in_dim.27), calls=%async_computation.8 | async-start | bytes 786432 | tf_op jit(solution)/shard_map/all_to_all | solution.py:30
  618.7 37.9 %collective-permute-start.33 = (bf16[8,48,1152]{2,1,0:T(8,128)(2,1)}, bf16[8,48,1152]{2,1,0:T(8,128)(2,1)}, u32[]{:S(2)}, u32[]{:S(2)}) collective-permute-start(bf16[8,48,1152]{2,1,0:T(8,128)(2,1)} %fusion.94), channel_id=1, source_target_pairs={{0,16},{16,0},{1,17},{17,1},{2,18},{18,2},{3,19},{19,3},{4,20},{20... | collective-permute-start | bytes 2654216 | tf_op jit(solution)/shard_map/ppermute | solution.py:22
  622.3 25.2 %collective-permute-start.35 = (bf16[8,48,384]{2,1,0:T(8,128)(2,1)S(1)}, bf16[8,48,384]{2,1,0:T(8,128)(2,1)S(1)}, u32[]{:S(2)}, u32[]{:S(2)}) collective-permute-start(bf16[8,48,384]{2,1,0:T(8,128)(2,1)S(1)} %fusion.120), channel_id=1, source_target_pairs={{0,16},{16,0},{1,17},{17,1},{2,18},{18,2},{3,19},{19,3},{4,20},{20... | collective-permute-start | bytes 884744 | tf_op jit(solution)/shard_map/ppermute | solution.py:22
  628.8 24.5 %all-to-all-start.7 = ((bf16[8,64,768]{2,1,0:T(8,128)(2,1)}), bf16[8,64,768]{2,1,0:T(8,128)(2,1)S(1)}, u32[]{:S(2)}, u32[]{:S(2)}) async-start(bf16[8,64,768]{2,1,0:T(8,128)(2,1)} %bitcast.38), calls=%async_computation.7 | async-start | bytes 1572864 | tf_op jit(solution)/shard_map/all_to_all | solution.py:30
  643.6 26.9 %collective-permute-start.27 = (bf16[128,768]{1,0:T(8,128)(2,1)S(1)}, bf16[128,768]{1,0:T(8,128)(2,1)S(1)}, u32[]{:S(2)}, u32[]{:S(2)}) collective-permute-start(bf16[128,768]{1,0:T(8,128)(2,1)S(1)} %get-tuple-element.165), channel_id=1, source_target_pairs={{0,1},{1,0},{2,3},{3,2},{4,5},{5,4},{6,7},{7,6},{8,9},{9,8},{10,11... | collective-permute-start | bytes 589832 | tf_op jit(solution)/shard_map/ppermute | solution.py:22
  653.2 13.8 %all-to-all-start.10 = ((bf16[8,48,384]{2,1,0:T(8,128)(2,1)}), bf16[8,48,384]{2,1,0:T(8,128)(2,1)S(1)}, u32[]{:S(2)}, u32[]{:S(2)}) async-start(bf16[8,48,384]{2,1,0:T(8,128)(2,1)} %fusion.109), calls=%async_computation.10 | async-start | bytes 589824 | tf_op jit(solution)/shard_map/all_to_all | solution.py:30
  667.0 30.8 %all-to-all-start.9 = ((bf16[8,48,1152]{2,1,0:T(8,128)(2,1)}), bf16[8,48,1152]{2,1,0:T(8,128)(2,1)S(1)}, u32[]{:S(2)}, u32[]{:S(2)}) async-start(bf16[8,48,1152]{2,1,0:T(8,128)(2,1)} %fusion.58), calls=%async_computation.9 | async-start | bytes 1769472 | tf_op jit(solution)/shard_map/all_to_all | solution.py:30
  673.6 13.7 %collective-permute-start.29 = (bf16[2,128,768]{2,1,0:T(8,128)(2,1)}, bf16[2,128,768]{2,1,0:T(8,128)(2,1)}, u32[]{:S(2)}, u32[]{:S(2)}) collective-permute-start(bf16[2,128,768]{2,1,0:T(8,128)(2,1)} %get-tuple-element.152), channel_id=1, source_target_pairs={{0,16},{16,0},{1,17},{17,1},{2,18},{18,2},{3,19},{19,3},{4,20},{20... | collective-permute-start | bytes 1179656 | tf_op jit(solution)/shard_map/ppermute | solution.py:22
  678.2 7.0 collective-permute-start.25
  686.4 10.4 %collective-permute-start.26 = (bf16[2,128,768]{2,1,0:T(8,128)(2,1)S(1)}, bf16[2,128,768]{2,1,0:T(8,128)(2,1)S(1)}, u32[]{:S(2)}, u32[]{:S(2)}) collective-permute-start(bf16[2,128,768]{2,1,0:T(8,128)(2,1)S(1)} %get-tuple-element.154), channel_id=1, source_target_pairs={{0,16},{16,0},{1,17},{17,1},{2,18},{18,2},{3,19},{19,3},{4,20},{20... | collective-permute-start | bytes 1179656 | tf_op jit(solution)/shard_map/ppermute | solution.py:22
  698.0 5.2 collective-permute-start.37
  (105 other events, 773.9 us)
Sparse Core Ops, SparseCore 0:
  28.5 53.9 all-gather.2
  118.7 50.5 all-gather.4
